TPU v7x, 128 devices: a whole 4x4x4 slice. The times are simulated.
128 devices in a mesh: seq: 32 (over x, y, core), head: 4 (over z).
Axes of the slice: x: 4, y: 4, z: 4, core: 2. Of those that a mesh axis runs over, the one named last changes fastest.
Arguments:
- inputs: bfloat16 [65536, 2048], P('seq'), may hold values from -6 to 6
- w_qkv: bfloat16 [3, 2048, 2048], P(None, None, 'head'), may hold values from -0.125 to 0.125
- norm_gain: float32 [2048], P('head'), may hold values from 0.1 to 1.9
- w_out: bfloat16 [2048, 2048], P('head'), may hold values from -0.125 to 0.125
Outputs:
- mixed: bfloat16 [65536, 2048], P(('seq', 'head'))
All inputs are finite; a program needn't handle non-finite values.
Results may differ from a plain program's by a relative error of at most 0.0067.
Values may be sent and summed in bfloat16 or wider, within the bound.
No kernel may reach another device: no remote copies, remote signals or barrier semaphores. Data moves between devices by JAX's collectives and lax.ppermute only.
A program may use at most 128 MiB of HBM per device.

v0:
```python
import jax
import jax.numpy as jnp
from jax import lax
from jax.experimental import pallas as pl
from jax.experimental.pallas import tpu as pltpu
from jax.sharding import PartitionSpec as P


DH = 128
BLK = 256
F32 = jnp.float32
BF16 = jnp.bfloat16


def dot(a, b):
    return jnp.dot(a, b, preferred_element_type=F32)


def cost(flops, nbytes):
    return pl.CostEstimate(flops=int(flops), bytes_accessed=int(nbytes), transcendentals=0)


def hi_lo(state):
    high = state.astype(BF16)
    low = (state - high.astype(F32)).astype(BF16)
    return jnp.concatenate([high, low], axis=0)


def qkv_kernel(x_ref, wq_ref, wk_ref, wv_ref, q_ref, k_ref, v_ref, pre_ref, tot_ref, acc):
    step = pl.program_id(0)

    @pl.when(step == 0)
    def _():
        acc[...] = jnp.zeros_like(acc)

    x = x_ref[...]
    k_ref[...] = dot(x, wk_ref[0]).astype(BF16)
    v_ref[...] = dot(x, wv_ref[0]).astype(BF16)
    q_ref[...] = dot(x, wq_ref[0]).astype(BF16)
    heads = acc.shape[0]
    for b in range(x.shape[0] // BLK):
        rows = slice(b * BLK, (b + 1) * BLK)
        for h in range(heads):
            cols = slice(h * DH, (h + 1) * DH)
            before = acc[h]
            pre_ref[b, h] = hi_lo(before)
            acc[h] = before + lax.dot_general(
                k_ref[rows, cols], v_ref[rows, cols], (((0,), (0,)), ((), ())),
                preferred_element_type=F32,
            )

    @pl.when(step == pl.num_programs(0) - 1)
    def _():
        tot_ref[...] = acc[...]


def project(x, w_qkv, tile=512):
    tokens, width = x.shape
    feats = w_qkv.shape[2]
    heads = feats // DH
    blocks = tile // BLK
    weight = lambda which: pl.BlockSpec((1, width, feats), lambda i: (which, 0, 0))
    rows = pl.BlockSpec((tile, feats), lambda i: (i, 0))
    return pl.pallas_call(
        qkv_kernel,
        grid=(tokens // tile,),
        in_specs=[pl.BlockSpec((tile, width), lambda i: (i, 0)), weight(0), weight(1), weight(2)],
        out_specs=[
            rows,
            rows,
            rows,
            pl.BlockSpec((blocks, heads, 2 * DH, DH), lambda i: (i, 0, 0, 0)),
            pl.BlockSpec((heads, DH, DH), lambda i: (0, 0, 0)),
        ],
        out_shape=[jax.ShapeDtypeStruct((tokens, feats), BF16)] * 3
        + [
            jax.ShapeDtypeStruct((tokens // BLK, heads, 2 * DH, DH), BF16),
            jax.ShapeDtypeStruct((heads, DH, DH), F32),
        ],
        scratch_shapes=[pltpu.VMEM((heads, DH, DH), F32)],
        cost_estimate=cost(6 * tokens * width * feats, 2 * tokens * width + 6 * width * feats),
        name="project",
    )(x, w_qkv, w_qkv, w_qkv)


def local_kernel(q_ref, k_ref, v_ref, pre_ref, *rest):
    att_ref = rest[-1]
    heads = pre_ref.shape[1]
    lower = lax.broadcasted_iota(jnp.int32, (BLK, BLK), 0) >= lax.broadcasted_iota(
        jnp.int32, (BLK, BLK), 1
    )
    for b in range(q_ref.shape[0] // BLK):
        rows = slice(b * BLK, (b + 1) * BLK)
        for h in range(heads):
            cols = slice(h * DH, (h + 1) * DH)
            q = q_ref[rows, cols]
            scores = lax.dot_general(
                q, k_ref[rows, cols], (((1,), (1,)), ((), ())), preferred_element_type=F32
            )
            scores = jnp.where(lower, scores, 0.0).astype(BF16)
            att_ref[rows, cols] = dot(scores, v_ref[rows, cols]) + dot(
                jnp.concatenate([q, q], axis=1), pre_ref[b, h]
            )


def local_part(q, k, v, pre, att, piece, pieces, tile=256):
    tokens, feats = q.shape
    heads = feats // DH
    blocks = tile // BLK
    count = tokens // pieces
    start = piece * count // tile
    row = pl.BlockSpec((tile, feats), lambda i: (i + start, 0))
    return pl.pallas_call(
        local_kernel,
        grid=(count // tile,),
        in_specs=[
            row, row, row,
            pl.BlockSpec((blocks, heads, 2 * DH, DH), lambda i: (i + start, 0, 0, 0)),
        ]
        + [pl.BlockSpec(memory_space=pl.ANY)] * len(att),
        out_specs=row,
        out_shape=jax.ShapeDtypeStruct((tokens, feats), F32),
        input_output_aliases={4: 0} if att else {},
        cost_estimate=cost(8 * count * feats * BLK, 14 * count * feats),
        name="local_part",
    )(q, k, v, pre, *att)


def finish_kernel(place, q_ref, att_ref, carried_ref, gain_ref, n_ref):
    heads = carried_ref.shape[0]
    for h in range(heads):
        cols = slice(h * DH, (h + 1) * DH)
        q = q_ref[:, cols]
        att = att_ref[:, cols] + dot(jnp.concatenate([q, q], axis=1), hi_lo(carried_ref[h]))
        mean_sq = jnp.mean(att * att, axis=-1, keepdims=True)
        n_ref[:, cols] = (att / jnp.sqrt(mean_sq + 1e-06) * gain_ref[:, cols]).astype(BF16)


def finish(place, q, att, carried, gain, parts, tile=256):
    tokens, feats = q.shape
    count = tokens // parts
    per = count // tile
    heads = feats // DH
    row = lambda i, place: (place[0] * per + i, 0)
    return pl.pallas_call(
        finish_kernel,
        grid_spec=pltpu.PrefetchScalarGridSpec(
            num_scalar_prefetch=1,
            grid=(per,),
            in_specs=[
                pl.BlockSpec((tile, feats), row),
                pl.BlockSpec((tile, feats), row),
                pl.BlockSpec((heads, DH, DH), lambda i, place: (0, 0, 0)),
                pl.BlockSpec((1, feats), lambda i, place: (0, 0)),
            ],
            out_specs=pl.BlockSpec((tile, feats), lambda i, place: (i, 0)),
        ),
        out_shape=jax.ShapeDtypeStruct((count, feats), BF16),
        cost_estimate=cost(2 * count * feats * DH * 2, count * feats * 8),
        name="finish",
    )(place, q, att, carried, gain)


def near_kernel(n0, na, nb, w0, wa, wb, acc_ref):
    acc_ref[...] = dot(n0[...], w0[...]) + dot(na[...], wa[...]) + dot(nb[...], wb[...])


def far_kernel(core, acc_ref, nf, mine_ref, other_ref, out_ref):
    half = mine_ref.shape[0]
    mine = pl.multiple_of(core[0] * half, half)
    other = pl.multiple_of((1 - core[0]) * half, half)
    acc = acc_ref[...] + dot(nf[:, pl.ds(mine, half)], mine_ref[...])
    acc += dot(nf[:, pl.ds(other, half)], other_ref[...])
    out_ref[...] = acc.astype(BF16)


def mix_near(normed, weights, tile=512):
    rows, feats = normed[0].shape
    width = weights[0].shape[1]
    return pl.pallas_call(
        near_kernel,
        grid=(width // tile,),
        in_specs=[pl.BlockSpec(a.shape, lambda i: (0, 0)) for a in normed]
        + [pl.BlockSpec((a.shape[0], tile), lambda i: (0, i)) for a in weights],
        out_specs=pl.BlockSpec((rows, tile), lambda i: (0, i)),
        out_shape=jax.ShapeDtypeStruct((rows, width), F32),
        cost_estimate=cost(6 * rows * feats * width, 10 * rows * width),
        compiler_params=pltpu.CompilerParams(vmem_limit_bytes=24 << 20),
        name="mix_near",
    )(*normed, *weights)


def mix_far(core, acc, normed, weights, tile=512):
    rows, feats = normed.shape
    width = acc.shape[1]
    column = lambda a: pl.BlockSpec((a.shape[0], tile), lambda i, core: (0, i))
    return pl.pallas_call(
        far_kernel,
        grid_spec=pltpu.PrefetchScalarGridSpec(
            num_scalar_prefetch=1,
            grid=(width // tile,),
            in_specs=[column(acc), pl.BlockSpec(normed.shape, lambda i, core: (0, 0))]
            + [column(a) for a in weights],
            out_specs=pl.BlockSpec((rows, tile), lambda i, core: (0, i)),
        ),
        out_shape=jax.ShapeDtypeStruct((rows, width), BF16),
        cost_estimate=cost(2 * rows * feats * width, 8 * rows * width),
        compiler_params=pltpu.CompilerParams(vmem_limit_bytes=24 << 20),
        name="mix_far",
    )(core, acc, normed, *weights)


def pair_up(size, stride, total, first):
    pairs = []
    for i in range(total):
        at = (i // stride) % size
        to = at ^ 1 if first else (at + (1 if at % 2 else -1)) % size
        pairs.append((i, i + (to - at) * stride))
    return pairs


def exclusive_prefix(value, position, stride, total):
    other = lax.ppermute(value.astype(BF16), "seq", pair_up(4, stride, total, True))
    other = other.astype(F32)
    value = value.astype(BF16).astype(F32)
    pair = value + other
    odd = lax.rem(position, 2) == 1
    before = jnp.where(odd, other, 0.0)
    far = lax.ppermute(pair.astype(BF16), "seq", pair_up(4, stride, total, False))
    far = far.astype(F32)
    return before + jnp.where(position >= 2, far, 0.0), pair + far


def layer(inputs, w_qkv, norm_gain, w_out):
    parts = lax.axis_size("head")
    total = lax.axis_size("seq")
    seq = lax.axis_index("seq")
    core = lax.rem(seq, 2)
    y = lax.rem(seq // 2, 4)
    x = seq // 8
    head = lax.axis_index("head")
    core_id = core.astype(jnp.int32).reshape(1)
    step = 1 - 2 * core

    def place(shift):
        return lax.rem(head + shift + parts, parts).astype(jnp.int32).reshape(1)

    def along(direction):
        pairs = []
        for i in range(total):
            shift = direction * (1 - 2 * (i % 2))
            for h in range(parts):
                pairs.append((i * parts + h, i * parts + (h + shift) % parts))
        return pairs

    partner = [(i, i ^ 1) for i in range(total)]
    across = [(i, (i + 2) % parts) for i in range(parts)]

    def swap(a):
        return lax.ppermute(a, "seq", partner)

    def send(a, direction):
        return lax.ppermute(a, ("seq", "head"), along(direction))

    near = send(w_out, 1)
    rows = w_out.shape[0] // 2
    far = send(lax.dynamic_slice_in_dim(near, core * rows, rows, 0), 1)
    near_other = swap(near)
    far_other = swap(far)

    q, k, v, pre, tot = project(inputs, w_qkv)
    other = swap(tot)
    att = []
    for piece in range(4):
        att = [local_part(q, k, v, pre, att, piece, 4)]
    att = att[0]
    before, row = exclusive_prefix(tot + other, y, 2, total)
    carried = jnp.where(core == 1, other, 0.0) + before
    before, _ = exclusive_prefix(row, x, 8, total)
    carried = carried + before

    gain = norm_gain.reshape(1, -1)
    na = send(finish(place(step), q, att, carried, gain, parts), 1)
    nb = send(finish(place(-step), q, att, carried, gain, parts), -1)
    nf = finish(place(2), q, att, carried, gain, parts)
    nf = lax.ppermute(nf, "head", across)
    n0 = finish(place(0), q, att, carried, gain, parts)
    acc = mix_near([n0, na, nb], [w_out, near, near_other])
    return mix_far(core_id, acc, nf, [far, far_other])


def solution(mesh):
    return jax.shard_map(
        layer,
        mesh=mesh,
        in_specs=(P("seq", None), P(None, None, "head"), P("head"), P("head", None)),
        out_specs=P(("seq", "head"), None),
        check_vma=False,
    )
```

profile of v0, /device:TPU:0, one launch (start us, length us, event | category | flops | bytes accessed | tf_op | source)
XLA Modules:
  0.0 104.4 jit_solution(12786328617031239488)
XLA Ops:
  0.0 2.0 %collective-permute-start.7 = (bf16[512,2048]{1,0:T(8,128)(2,1)}, bf16[512,2048]{1,0:T(8,128)(2,1)S(1)}, u32[]{:S(2)}, u32[]{:S(2)}) collective-permute-start(bf16[512,2048]{1,0:T(8,128)(2,1)} %w0.1), channel_id=1, source_target_pairs={{0,1},{1,2},{2,3},{3,0},{4,7},{5,4},{6,5},{7,6},{8,9},{9,10},{10,1... | collective-permute-start | bytes 6291464 | tf_op jit(solution)/shard_map/ppermute | solution.py:263
  2.0 19.4 %project.1 = (bf16[2048,512]{1,0:T(8,128)(2,1)}, bf16[2048,512]{1,0:T(8,128)(2,1)}, bf16[2048,512]{1,0:T(8,128)(2,1)}, bf16[8,4,256,128]{3,2,1,0:T(8,128)(2,1)}, f32[4,128,128]{2,1,0:T(8,128)}) custom-call(bf16[2048,2048]{1,0:T(8,128)(2,1)} %x_ref.1, bf16[3,2048,512]{2,1,0:T(8,128)(2,1)} %wv_ref.1, bf16[3,2048,512]{2,1,0:T(8,128)(2,1)} %wv_ref.1, ...), custom_call_target="tpu_custom_call" | custom-call | flops 12884901888 | bytes 14680064 | tf_op jit(solution)/shard_map/project/pallas_call | solution.py:64
  21.4 1.8 %collective-permute-start = (f32[4,128,128]{2,1,0:T(8,128)}, f32[4,128,128]{2,1,0:T(8,128)S(1)}, u32[]{:S(2)}, u32[]{:S(2)}) collective-permute-start(f32[4,128,128]{2,1,0:T(8,128)} %get-tuple-element.14), channel_id=1, source_target_pairs={{0,4},{4,0},{8,12},{12,8},{16,20},{20,16},{24,28},{28,24},{32,36},... | collective-permute-start | bytes 786440 | tf_op jit(solution)/shard_map/ppermute | solution.py:260
  25.5 1.7 %collective-permute-start.1 = (bf16[4,128,128]{2,1,0:T(8,128)(2,1)S(1)}, bf16[4,128,128]{2,1,0:T(8,128)(2,1)S(1)}, u32[]{:S(2)}, u32[]{:S(2)}) collective-permute-start(bf16[4,128,128]{2,1,0:T(8,128)(2,1)S(1)} %add_convert_fusion), channel_id=1, source_target_pairs={{0,8},{4,12},{8,0},{12,4},{16,24},{20,28},{24,16},{28,20},{32,40},... | collective-permute-start | bytes 393224 | tf_op jit(solution)/shard_map/ppermute | solution.py:223
  29.5 1.8 %collective-permute-done.1 = bf16[4,128,128]{2,1,0:T(8,128)(2,1)S(1)} collective-permute-done((bf16[4,128,128]{2,1,0:T(8,128)(2,1)S(1)}, bf16[4,128,128]{2,1,0:T(8,128)(2,1)S(1)}, u32[]{:S(2)}, u32[]{:S(2)}) %collective-permute-start.1) | collective-permute-done | bytes 131104 | tf_op jit(solution)/shard_map/ppermute | solution.py:223
  31.4 3.1 %collective-permute-start.2 = (bf16[4,128,128]{2,1,0:T(8,128)(2,1)S(1)}, bf16[4,128,128]{2,1,0:T(8,128)(2,1)S(1)}, u32[]{:S(2)}, u32[]{:S(2)}) collective-permute-start(bf16[4,128,128]{2,1,0:T(8,128)(2,1)S(1)} %fusion.6), channel_id=1, source_target_pairs={{0,24},{4,28},{8,16},{12,20},{16,8},{20,12},{24,0},{28,4},{32,56},... | collective-permute-start | bytes 393224 | tf_op jit(solution)/shard_map/ppermute | solution.py:229
  34.5 4.1 %collective-permute-done.2 = bf16[4,128,128]{2,1,0:T(8,128)(2,1)S(1)} collective-permute-done((bf16[4,128,128]{2,1,0:T(8,128)(2,1)S(1)}, bf16[4,128,128]{2,1,0:T(8,128)(2,1)S(1)}, u32[]{:S(2)}, u32[]{:S(2)}) %collective-permute-start.2) | collective-permute-done | bytes 131104 | tf_op jit(solution)/shard_map/ppermute | solution.py:229
  39.3 1.5 %collective-permute-start.3 = (bf16[4,128,128]{2,1,0:T(8,128)(2,1)}, bf16[4,128,128]{2,1,0:T(8,128)(2,1)}, u32[]{:S(2)}, u32[]{:S(2)}) collective-permute-start(bf16[4,128,128]{2,1,0:T(8,128)(2,1)} %fusion.3), channel_id=1, source_target_pairs={{0,32},{4,36},{8,40},{12,44},{16,48},{20,52},{24,56},{28,60},{32,0... | collective-permute-start | bytes 393224 | tf_op jit(solution)/shard_map/ppermute | solution.py:223
  40.8 3.4 %local_part.4.rest_0_ = f32[2048,512]{1,0:T(8,128)} custom-call(bf16[2048,512]{1,0:T(8,128)(2,1)} %get-tuple-element.10.q_ref, bf16[2048,512]{1,0:T(8,128)(2,1)} %get-tuple-element.11.k_ref, bf16[2048,512]{1,0:T(8,128)(2,1)} %get-tuple-element.12.v_ref, bf16[8,4,256,128]{3,2,1,0:T(8,128)(2,1)} %get-tuple-element.13.pre_ref), custom_call_target="tpu_custom_call" | custom-call | flops 536870912 | bytes 3670016 | tf_op jit(solution)/shard_map/local_part/pallas_call | solution.py:113
  44.6 1.7 %fusion.5 = bf16[4,128,128]{2,1,0:T(8,128)(2,1)} fusion(bf16[4,128,128]{2,1,0:T(8,128)(2,1)} %collective-permute-done.3, bf16[4,128,128]{2,1,0:T(8,128)(2,1)} %fusion.3), kind=kLoop, calls=%fused_computation.11 | loop fusion | flops 262144 | bytes 393216 | tf_op jit(solution)/shard_map/convert_element_type | solution.py:229
  46.3 2.8 %collective-permute-start.4 = (bf16[4,128,128]{2,1,0:T(8,128)(2,1)}, bf16[4,128,128]{2,1,0:T(8,128)(2,1)}, u32[]{:S(2)}, u32[]{:S(2)}) collective-permute-start(bf16[4,128,128]{2,1,0:T(8,128)(2,1)} %fusion.5), channel_id=1, source_target_pairs={{0,96},{4,100},{8,104},{12,108},{16,112},{20,116},{24,120},{28,124... | collective-permute-start | bytes 393224 | tf_op jit(solution)/shard_map/ppermute | solution.py:229
  49.0 3.4 %local_part.5.rest_0_ = f32[2048,512]{1,0:T(8,128)} custom-call(bf16[2048,512]{1,0:T(8,128)(2,1)} %get-tuple-element.10.q_ref, bf16[2048,512]{1,0:T(8,128)(2,1)} %get-tuple-element.11.k_ref, bf16[2048,512]{1,0:T(8,128)(2,1)} %get-tuple-element.12.v_ref, bf16[8,4,256,128]{3,2,1,0:T(8,128)(2,1)} %get-tuple-element.13.pre_ref, ...), custom_call_target="tpu_custom_call", output_to_operand_aliasing={{}: (4, {})} | custom-call | flops 536870912 | bytes 3670016 | tf_op jit(solution)/shard_map/local_part/pallas_call | solution.py:113
  52.4 3.4 %local_part.6.rest_0_ = f32[2048,512]{1,0:T(8,128)} custom-call(bf16[2048,512]{1,0:T(8,128)(2,1)} %get-tuple-element.10.q_ref, bf16[2048,512]{1,0:T(8,128)(2,1)} %get-tuple-element.11.k_ref, bf16[2048,512]{1,0:T(8,128)(2,1)} %get-tuple-element.12.v_ref, bf16[8,4,256,128]{3,2,1,0:T(8,128)(2,1)} %get-tuple-element.13.pre_ref, ...), custom_call_target="tpu_custom_call", output_to_operand_aliasing={{}: (4, {})} | custom-call | flops 536870912 | bytes 3670016 | tf_op jit(solution)/shard_map/local_part/pallas_call | solution.py:113
  55.9 3.4 %local_part.7.att_ref = f32[2048,512]{1,0:T(8,128)} custom-call(bf16[2048,512]{1,0:T(8,128)(2,1)} %get-tuple-element.10.q_ref, bf16[2048,512]{1,0:T(8,128)(2,1)} %get-tuple-element.11.k_ref, bf16[2048,512]{1,0:T(8,128)(2,1)} %get-tuple-element.12.v_ref, bf16[8,4,256,128]{3,2,1,0:T(8,128)(2,1)} %get-tuple-element.13.pre_ref, ...), custom_call_target="tpu_custom_call", output_to_operand_aliasing={{}: (4, {})} | custom-call | flops 536870912 | bytes 3670016 | tf_op jit(solution)/shard_map/local_part/pallas_call | solution.py:113
  59.3 1.8 %fusion.2.carried_ref = f32[4,128,128]{2,1,0:T(8,128)} fusion(bf16[4,128,128]{2,1,0:T(8,128)(2,1)S(1)} %collective-permute-done.1, bf16[4,128,128]{2,1,0:T(8,128)(2,1)} %copy-done.2, bf16[4,128,128]{2,1,0:T(8,128)(2,1)} %collective-permute-done.3, bf16[4,128,128]{2,1,0:T(8,128)(2,1)} %collective-permute-done.4, f32[4,128,128]{2,1,0:T(8,128)S(1)} %collective-permute-done, ...), kind=kLoop, calls=%fused_computation.8 | loop fusion | flops 851968 | bytes 1048581 | tf_op jit(solution)/shard_map/add | solution.py:280
  61.1 2.9 %finish.6 = bf16[512,512]{1,0:T(8,128)(2,1)} custom-call(s32[1]{0:T(128)} %bitcast.4.place, bf16[2048,512]{1,0:T(8,128)(2,1)} %get-tuple-element.10.q_ref, f32[2048,512]{1,0:T(8,128)} %local_part.7.att_ref, f32[4,128,128]{2,1,0:T(8,128)} %fusion.2.carried_ref, f32[1,512]{1,0:T(1,128)} %bitcast.6), custom_call_target="tpu_custom_call" | custom-call | flops 134217728 | bytes 2097152 | tf_op jit(solution)/shard_map/finish/pallas_call | solution.py:145
  64.5 2.9 %finish.5 = bf16[512,512]{1,0:T(8,128)(2,1)} custom-call(s32[1]{0:T(128)} %bitcast.3.place, bf16[2048,512]{1,0:T(8,128)(2,1)} %get-tuple-element.10.q_ref, f32[2048,512]{1,0:T(8,128)} %local_part.7.att_ref, f32[4,128,128]{2,1,0:T(8,128)} %fusion.2.carried_ref, f32[1,512]{1,0:T(1,128)} %bitcast.7), custom_call_target="tpu_custom_call" | custom-call | flops 134217728 | bytes 2097152 | tf_op jit(solution)/shard_map/finish/pallas_call | solution.py:145
  67.4 1.6 %collective-permute-start.5 = (bf16[512,512]{1,0:T(8,128)(2,1)}, bf16[512,512]{1,0:T(8,128)(2,1)}, u32[]{:S(2)}, u32[]{:S(2)}) collective-permute-start(bf16[512,512]{1,0:T(8,128)(2,1)} %finish.5), channel_id=1, source_target_pairs={{0,1},{1,2},{2,3},{3,0},{4,7},{5,4},{6,5},{7,6},{8,9},{9,10},{10,1... | collective-permute-start | bytes 1572872 | tf_op jit(solution)/shard_map/ppermute | solution.py:263
  69.0 2.9 %finish.7 = bf16[512,512]{1,0:T(8,128)(2,1)} custom-call(s32[1]{0:T(128)} %bitcast.5.place, bf16[2048,512]{1,0:T(8,128)(2,1)} %get-tuple-element.10.q_ref, f32[2048,512]{1,0:T(8,128)} %local_part.7.att_ref, f32[4,128,128]{2,1,0:T(8,128)} %fusion.2.carried_ref, f32[1,512]{1,0:T(1,128)} %bitcast.8), custom_call_target="tpu_custom_call" | custom-call | flops 134217728 | bytes 2097152 | tf_op jit(solution)/shard_map/finish/pallas_call | solution.py:145
  73.0 2.9 %finish.4.n0 = bf16[512,512]{1,0:T(8,128)(2,1)} custom-call(s32[1]{0:T(128)} %bitcast.1.place, bf16[2048,512]{1,0:T(8,128)(2,1)} %get-tuple-element.10.q_ref, f32[2048,512]{1,0:T(8,128)} %local_part.7.att_ref, f32[4,128,128]{2,1,0:T(8,128)} %fusion.2.carried_ref, f32[1,512]{1,0:T(1,128)} %bitcast.9), custom_call_target="tpu_custom_call" | custom-call | flops 134217728 | bytes 2097152 | tf_op jit(solution)/shard_map/finish/pallas_call | solution.py:145
  76.7 14.4 %collective-permute-done.5.na = bf16[512,512]{1,0:T(8,128)(2,1)} collective-permute-done((bf16[512,512]{1,0:T(8,128)(2,1)}, bf16[512,512]{1,0:T(8,128)(2,1)}, u32[]{:S(2)}, u32[]{:S(2)}) %collective-permute-start.5) | collective-permute-done | bytes 524320 | tf_op jit(solution)/shard_map/ppermute | solution.py:263
  91.1 1.6 %copy-done = bf16[512,2048]{1,0:T(8,128)(2,1)S(1)} copy-done((bf16[512,2048]{1,0:T(8,128)(2,1)S(1)}, bf16[512,2048]{1,0:T(8,128)(2,1)}, u32[]{:S(2)}) %copy-start) | copy-done | bytes 2097176
  93.8 5.8 %mix_near.1.acc_ref = f32[512,2048]{1,0:T(8,128)S(1)} custom-call(bf16[512,512]{1,0:T(8,128)(2,1)S(1)} %copy-done.1, bf16[512,512]{1,0:T(8,128)(2,1)} %collective-permute-done.5.na, bf16[512,512]{1,0:T(8,128)(2,1)} %collective-permute-done.6.nb, bf16[512,2048]{1,0:T(8,128)(2,1)S(1)} %copy-done, bf16[512,2048]{1,0:T(8,128)(2,1)S(1)} %collective-permute-done.7.wa, ...), custom_call_target="tpu_custom_call" | custom-call | flops 3221225472 | bytes 10485760 | tf_op jit(solution)/shard_map/mix_near/pallas_call | solution.py:180
  99.6 4.8 %mix_far.1 = bf16[512,2048]{1,0:T(8,128)(2,1)} custom-call(s32[1]{0:T(128)} %bitcast.core, f32[512,2048]{1,0:T(8,128)S(1)} %mix_near.1.acc_ref, bf16[512,512]{1,0:T(8,128)(2,1)} %collective-permute-done.9.nf, bf16[256,2048]{1,0:T(8,128)(2,1)S(1)} %collective-permute-done.10.mine_ref, bf16[256,2048]{1,0:T(8,128)(2,1)} %collective-permute-done.11.other_ref), custom_call_target="tpu_custom_call" | custom-call | flops 1073741824 | bytes 8388608 | tf_op jit(solution)/shard_map/mix_far/pallas_call | solution.py:197
  (23 shorter events, 9.3 us)
Async XLA Ops:
  0.0 28.4 %collective-permute-start.7 = (bf16[512,2048]{1,0:T(8,128)(2,1)}, bf16[512,2048]{1,0:T(8,128)(2,1)S(1)}, u32[]{:S(2)}, u32[]{:S(2)}) collective-permute-start(bf16[512,2048]{1,0:T(8,128)(2,1)} %w0.1), channel_id=1, source_target_pairs={{0,1},{1,2},{2,3},{3,0},{4,7},{5,4},{6,5},{7,6},{8,9},{9,10},{10,1... | collective-permute-start | bytes 6291464 | tf_op jit(solution)/shard_map/ppermute | solution.py:263
  21.4 3.1 %collective-permute-start = (f32[4,128,128]{2,1,0:T(8,128)}, f32[4,128,128]{2,1,0:T(8,128)S(1)}, u32[]{:S(2)}, u32[]{:S(2)}) collective-permute-start(f32[4,128,128]{2,1,0:T(8,128)} %get-tuple-element.14), channel_id=1, source_target_pairs={{0,4},{4,0},{8,12},{12,8},{16,20},{20,16},{24,28},{28,24},{32,36},... | collective-permute-start | bytes 786440 | tf_op jit(solution)/shard_map/ppermute | solution.py:260
  25.5 5.9 %collective-permute-start.1 = (bf16[4,128,128]{2,1,0:T(8,128)(2,1)S(1)}, bf16[4,128,128]{2,1,0:T(8,128)(2,1)S(1)}, u32[]{:S(2)}, u32[]{:S(2)}) collective-permute-start(bf16[4,128,128]{2,1,0:T(8,128)(2,1)S(1)} %add_convert_fusion), channel_id=1, source_target_pairs={{0,8},{4,12},{8,0},{12,4},{16,24},{20,28},{24,16},{28,20},{32,40},... | collective-permute-start | bytes 393224 | tf_op jit(solution)/shard_map/ppermute | solution.py:223
  28.4 62.8 %collective-permute-start.8 = (bf16[512,2048]{1,0:T(8,128)(2,1)S(1)}, bf16[512,2048]{1,0:T(8,128)(2,1)}, u32[]{:S(2)}, u32[]{:S(2)}) collective-permute-start(bf16[512,2048]{1,0:T(8,128)(2,1)S(1)} %collective-permute-done.7.wa), channel_id=1, source_target_pairs={{0,4},{4,0},{8,12},{12,8},{16,20},{20,16},{24,28},{28,24},{32,36},... | collective-permute-start | bytes 6291464 | tf_op jit(solution)/shard_map/ppermute | solution.py:260
  29.5 29.7 %collective-permute-start.10 = (bf16[256,2048]{1,0:T(8,128)(2,1)}, bf16[256,2048]{1,0:T(8,128)(2,1)S(1)}, u32[]{:S(2)}, u32[]{:S(2)}) collective-permute-start(bf16[256,2048]{1,0:T(8,128)(2,1)} %constant_dynamic-slice_fusion), channel_id=1, source_target_pairs={{0,1},{1,2},{2,3},{3,0},{4,7},{5,4},{6,5},{7,6},{8,9},{9,10},{10,1... | collective-permute-start | bytes 3145736 | tf_op jit(solution)/shard_map/ppermute | solution.py:263
  31.4 7.2 %collective-permute-start.2 = (bf16[4,128,128]{2,1,0:T(8,128)(2,1)S(1)}, bf16[4,128,128]{2,1,0:T(8,128)(2,1)S(1)}, u32[]{:S(2)}, u32[]{:S(2)}) collective-permute-start(bf16[4,128,128]{2,1,0:T(8,128)(2,1)S(1)} %fusion.6), channel_id=1, source_target_pairs={{0,24},{4,28},{8,16},{12,20},{16,8},{20,12},{24,0},{28,4},{32,56},... | collective-permute-start | bytes 393224 | tf_op jit(solution)/shard_map/ppermute | solution.py:229
  38.6 0.7 copy-start.2
  39.3 5.3 %collective-permute-start.3 = (bf16[4,128,128]{2,1,0:T(8,128)(2,1)}, bf16[4,128,128]{2,1,0:T(8,128)(2,1)}, u32[]{:S(2)}, u32[]{:S(2)}) collective-permute-start(bf16[4,128,128]{2,1,0:T(8,128)(2,1)} %fusion.3), channel_id=1, source_target_pairs={{0,32},{4,36},{8,40},{12,44},{16,48},{20,52},{24,56},{28,60},{32,0... | collective-permute-start | bytes 393224 | tf_op jit(solution)/shard_map/ppermute | solution.py:223
  46.3 13.0 %collective-permute-start.4 = (bf16[4,128,128]{2,1,0:T(8,128)(2,1)}, bf16[4,128,128]{2,1,0:T(8,128)(2,1)}, u32[]{:S(2)}, u32[]{:S(2)}) collective-permute-start(bf16[4,128,128]{2,1,0:T(8,128)(2,1)} %fusion.5), channel_id=1, source_target_pairs={{0,96},{4,100},{8,104},{12,108},{16,112},{20,116},{24,120},{28,124... | collective-permute-start | bytes 393224 | tf_op jit(solution)/shard_map/ppermute | solution.py:229
  59.3 40.3 %collective-permute-start.11 = (bf16[256,2048]{1,0:T(8,128)(2,1)S(1)}, bf16[256,2048]{1,0:T(8,128)(2,1)}, u32[]{:S(2)}, u32[]{:S(2)}) collective-permute-start(bf16[256,2048]{1,0:T(8,128)(2,1)S(1)} %collective-permute-done.10.mine_ref), channel_id=1, source_target_pairs={{0,4},{4,0},{8,12},{12,8},{16,20},{20,16},{24,28},{28,24},{32,36},... | collective-permute-start | bytes 3145736 | tf_op jit(solution)/shard_map/ppermute | solution.py:260
  64.0 12.7 %collective-permute-start.6 = (bf16[512,512]{1,0:T(8,128)(2,1)}, bf16[512,512]{1,0:T(8,128)(2,1)}, u32[]{:S(2)}, u32[]{:S(2)}) collective-permute-start(bf16[512,512]{1,0:T(8,128)(2,1)} %finish.6), channel_id=1, source_target_pairs={{0,3},{1,0},{2,1},{3,2},{4,5},{5,6},{6,7},{7,4},{8,11},{9,8},{10,9... | collective-permute-start | bytes 1572872 | tf_op jit(solution)/shard_map/ppermute | solution.py:263
  67.4 23.7 %collective-permute-start.5 = (bf16[512,512]{1,0:T(8,128)(2,1)}, bf16[512,512]{1,0:T(8,128)(2,1)}, u32[]{:S(2)}, u32[]{:S(2)}) collective-permute-start(bf16[512,512]{1,0:T(8,128)(2,1)} %finish.5), channel_id=1, source_target_pairs={{0,1},{1,2},{2,3},{3,0},{4,7},{5,4},{6,5},{7,6},{8,9},{9,10},{10,1... | collective-permute-start | bytes 1572872 | tf_op jit(solution)/shard_map/ppermute | solution.py:263
  71.9 27.7 %collective-permute-start.9 = (bf16[512,512]{1,0:T(8,128)(2,1)}, bf16[512,512]{1,0:T(8,128)(2,1)}, u32[]{:S(2)}, u32[]{:S(2)}) collective-permute-start(bf16[512,512]{1,0:T(8,128)(2,1)} %finish.7), channel_id=1, source_target_pairs={{0,2},{1,3},{2,0},{3,1},{4,6},{5,7},{6,4},{7,5},{8,10},{9,11},{10,... | collective-permute-start | bytes 1572872 | tf_op jit(solution)/shard_map/ppermute | solution.py:286
  91.1 1.6 %copy-start = (bf16[512,2048]{1,0:T(8,128)(2,1)S(1)}, bf16[512,2048]{1,0:T(8,128)(2,1)}, u32[]{:S(2)}) copy-start(bf16[512,2048]{1,0:T(8,128)(2,1)} %w0.1) | copy-start | bytes 6291460
  92.7 1.0 copy-start.1
where the time goes:
time: 105 us; the launch traced here: 104 us
  Pallas kernels  55.2 us (53%)
  waiting for transfers between devices  24.2 us (23%)
  starting transfers between devices  15.9 us (15%)
  other arithmetic  5.22 us (5%)
  local copies, waits for them, and re-layouts  3.79 us (4%)
    pallas_call x1, Pallas kernels, project(): pl.pallas_call(qkv_kernel, grid=(tokens // tile,), in_specs=[pl.BlockSpec...  19.4 us
    ppermute x4, waiting for transfers between devices, send(): return lax.ppermute(a, ('seq', 'head'), along(direction))  16.4 us
    pallas_call x4, Pallas kernels, local_part(): pl.pallas_call(local_kernel, grid=(count // tile,), in_specs=[row, row, r...  13.6 us
    pallas_call x4, Pallas kernels, finish(): pl.pallas_call(finish_kernel, grid_spec=pltpu.PrefetchScalarGridSpec(num_...  11.7 us
    ppermute x2, starting transfers between devices, exclusive_prefix(): lax.ppermute(pair.astype(BF16), 'seq', pair_up(4, stride, total, False))  5.85 us
    pallas_call x1, Pallas kernels, mix_near(): pl.pallas_call(near_kernel, grid=(width // tile,), in_specs=[pl.BlockSpec...  5.8 us
    pallas_call x1, Pallas kernels, mix_far(): pl.pallas_call(far_kernel, grid_spec=pltpu.PrefetchScalarGridSpec(num_sca...  4.76 us
    ppermute x2, waiting for transfers between devices, exclusive_prefix(): lax.ppermute(pair.astype(BF16), 'seq', pair_up(4, stride, total, False))  4.08 us
  transfers between devices with their start and end apart: 12, of which 7 were waited for; matrix products, arithmetic and copies ran while one was open for 6% of the time, Pallas kernels for 48%

commit v1 on v0

--- a/solution.py
+++ b/solution.py
@@ -185,7 +185,7 @@
         out_specs=pl.BlockSpec((rows, tile), lambda i: (0, i)),
         out_shape=jax.ShapeDtypeStruct((rows, width), F32),
         cost_estimate=cost(6 * rows * feats * width, 10 * rows * width),
-        compiler_params=pltpu.CompilerParams(vmem_limit_bytes=24 << 20),
+        compiler_params=pltpu.CompilerParams(vmem_limit_bytes=59 << 20),
         name="mix_near",
     )(*normed, *weights)
 
@@ -205,7 +205,7 @@
         ),
         out_shape=jax.ShapeDtypeStruct((rows, width), BF16),
         cost_estimate=cost(2 * rows * feats * width, 8 * rows * width),
-        compiler_params=pltpu.CompilerParams(vmem_limit_bytes=24 << 20),
+        compiler_params=pltpu.CompilerParams(vmem_limit_bytes=59 << 20),
         name="mix_far",
     )(core, acc, normed, *weights)
 
@@ -254,7 +254,6 @@
         return pairs
 
     partner = [(i, i ^ 1) for i in range(total)]
-    across = [(i, (i + 2) % parts) for i in range(parts)]
 
     def swap(a):
         return lax.ppermute(a, "seq", partner)
@@ -280,10 +279,10 @@
     carried = carried + before
 
     gain = norm_gain.reshape(1, -1)
+    nf = send(finish(place(2), q, att, carried, gain, parts), 1)
     na = send(finish(place(step), q, att, carried, gain, parts), 1)
     nb = send(finish(place(-step), q, att, carried, gain, parts), -1)
-    nf = finish(place(2), q, att, carried, gain, parts)
-    nf = lax.ppermute(nf, "head", across)
+    nf = send(nf, 1)
     n0 = finish(place(0), q, att, carried, gain, parts)
     acc = mix_near([n0, na, nb], [w_out, near, near_other])
     return mix_far(core_id, acc, nf, [far, far_other])

time: 105 us -> 97.8 us (0.931)
  waiting for transfers between devices: 24.2 us -> 16.9 us
  Pallas kernels: 55.2 us -> 58.5 us
  local copies, waits for them, and re-layouts: 3.79 us -> 1.71 us
  other arithmetic: 5.22 us -> 3.72 us
    ppermute x4 -> x6, waiting for transfers between devices: 16.4 us -> 10.7 us  [send(): return lax.ppermute(a, ('seq', 'head'), along(direction))]
    ppermute x2, waiting for transfers between devices: 4.08 us -> 1.71 us  [exclusive_prefix(): lax.ppermute(pair.astype(BF16), 'seq', pair_up(4, stride, total, False))]
    pallas_call x1, Pallas kernels: 5.8 us -> 7.86 us  [mix_near(): pl.pallas_call(near_kernel, grid=(width // tile,), in_specs=[pl.BlockSpec...]
    unnamed x6 -> x12, local copies, waits for them, and re-layouts: 2.64 us -> 0.61 us
    ppermute x4 -> x6, starting transfers between devices: 4.06 us -> 5.65 us  [send(): return lax.ppermute(a, ('seq', 'head'), along(direction))]
    ppermute x1 -> x0, starting transfers between devices: 1.07 us -> none  [layer(): nf = lax.ppermute(nf, 'head', across)]
  transfers between devices with their start and end apart: 12 -> 13, of which waited for: 7 -> 8; matrix products, arithmetic and copies ran while one was open for 6% -> 5% of each run, Pallas kernels for 48% -> 54%
where the time goes in v1:
time: 97.8 us; the launch traced here: 97.3 us
  Pallas kernels  58.5 us (60%)
  waiting for transfers between devices  16.9 us (17%)
  starting transfers between devices  16.4 us (17%)
  other arithmetic  3.72 us (4%)
  local copies, waits for them, and re-layouts  1.71 us (2%)
    pallas_call x1, Pallas kernels, project(): pl.pallas_call(qkv_kernel, grid=(tokens // tile,), in_specs=[pl.BlockSpec...  19.4 us
    pallas_call x4, Pallas kernels, local_part(): pl.pallas_call(local_kernel, grid=(count // tile,), in_specs=[row, row, r...  13.6 us
    pallas_call x4, Pallas kernels, finish(): pl.pallas_call(finish_kernel, grid_spec=pltpu.PrefetchScalarGridSpec(num_...  12 us
    ppermute x6, waiting for transfers between devices, send(): return lax.ppermute(a, ('seq', 'head'), along(direction))  10.7 us
    pallas_call x1, Pallas kernels, mix_near(): pl.pallas_call(near_kernel, grid=(width // tile,), in_specs=[pl.BlockSpec...  7.86 us
    ppermute x2, starting transfers between devices, exclusive_prefix(): lax.ppermute(pair.astype(BF16), 'seq', pair_up(4, stride, total, False))  5.85 us
    ppermute x6, starting transfers between devices, send(): return lax.ppermute(a, ('seq', 'head'), along(direction))  5.65 us
    pallas_call x1, Pallas kernels, mix_far(): pl.pallas_call(far_kernel, grid_spec=pltpu.PrefetchScalarGridSpec(num_sca...  5.62 us
  transfers between devices with their start and end apart: 13, of which 8 were waited for; matrix products, arithmetic and copies ran while one was open for 5% of the time, Pallas kernels for 54%

profile of v1, /device:TPU:0, one launch (start us, length us, event | category | flops | bytes accessed | tf_op | source)
XLA Modules:
  0.0 97.3 jit_solution(16882835826688522591)
XLA Ops:
  0.0 2.0 %collective-permute-start.7 = (bf16[512,2048]{1,0:T(8,128)(2,1)}, bf16[512,2048]{1,0:T(8,128)(2,1)S(1)}, u32[]{:S(2)}, u32[]{:S(2)}) collective-permute-start(bf16[512,2048]{1,0:T(8,128)(2,1)} %w0.1), channel_id=1, source_target_pairs={{0,1},{1,2},{2,3},{3,0},{4,7},{5,4},{6,5},{7,6},{8,9},{9,10},{10,1... | collective-permute-start | bytes 6291464 | tf_op jit(solution)/shard_map/ppermute | solution.py:262
  2.0 19.4 %project.1 = (bf16[2048,512]{1,0:T(8,128)(2,1)}, bf16[2048,512]{1,0:T(8,128)(2,1)}, bf16[2048,512]{1,0:T(8,128)(2,1)}, bf16[8,4,256,128]{3,2,1,0:T(8,128)(2,1)}, f32[4,128,128]{2,1,0:T(8,128)}) custom-call(bf16[2048,2048]{1,0:T(8,128)(2,1)} %x_ref.1, bf16[3,2048,512]{2,1,0:T(8,128)(2,1)} %wv_ref.1, bf16[3,2048,512]{2,1,0:T(8,128)(2,1)} %wv_ref.1, ...), custom_call_target="tpu_custom_call" | custom-call | flops 12884901888 | bytes 14680064 | tf_op jit(solution)/shard_map/project/pallas_call | solution.py:64
  21.4 1.8 %collective-permute-start = (f32[4,128,128]{2,1,0:T(8,128)}, f32[4,128,128]{2,1,0:T(8,128)S(1)}, u32[]{:S(2)}, u32[]{:S(2)}) collective-permute-start(f32[4,128,128]{2,1,0:T(8,128)} %get-tuple-element.14), channel_id=1, source_target_pairs={{0,4},{4,0},{8,12},{12,8},{16,20},{20,16},{24,28},{28,24},{32,36},... | collective-permute-start | bytes 786440 | tf_op jit(solution)/shard_map/ppermute | solution.py:259
  23.2 1.4 %collective-permute-done = f32[4,128,128]{2,1,0:T(8,128)S(1)} collective-permute-done((f32[4,128,128]{2,1,0:T(8,128)}, f32[4,128,128]{2,1,0:T(8,128)S(1)}, u32[]{:S(2)}, u32[]{:S(2)}) %collective-permute-start) | collective-permute-done | bytes 262176 | tf_op jit(solution)/shard_map/ppermute | solution.py:259
  25.6 1.7 %collective-permute-start.1 = (bf16[4,128,128]{2,1,0:T(8,128)(2,1)S(1)}, bf16[4,128,128]{2,1,0:T(8,128)(2,1)S(1)}, u32[]{:S(2)}, u32[]{:S(2)}) collective-permute-start(bf16[4,128,128]{2,1,0:T(8,128)(2,1)S(1)} %add_convert_fusion), channel_id=1, source_target_pairs={{0,8},{4,12},{8,0},{12,4},{16,24},{20,28},{24,16},{28,20},{32,40},... | collective-permute-start | bytes 393224 | tf_op jit(solution)/shard_map/ppermute | solution.py:223
  28.4 3.1 %collective-permute-done.1 = bf16[4,128,128]{2,1,0:T(8,128)(2,1)S(1)} collective-permute-done((bf16[4,128,128]{2,1,0:T(8,128)(2,1)S(1)}, bf16[4,128,128]{2,1,0:T(8,128)(2,1)S(1)}, u32[]{:S(2)}, u32[]{:S(2)}) %collective-permute-start.1) | collective-permute-done | bytes 131104 | tf_op jit(solution)/shard_map/ppermute | solution.py:223
  31.5 3.1 %collective-permute-start.2 = (bf16[4,128,128]{2,1,0:T(8,128)(2,1)S(1)}, bf16[4,128,128]{2,1,0:T(8,128)(2,1)S(1)}, u32[]{:S(2)}, u32[]{:S(2)}) collective-permute-start(bf16[4,128,128]{2,1,0:T(8,128)(2,1)S(1)} %fusion.6), channel_id=1, source_target_pairs={{0,24},{4,28},{8,16},{12,20},{16,8},{20,12},{24,0},{28,4},{32,56},... | collective-permute-start | bytes 393224 | tf_op jit(solution)/shard_map/ppermute | solution.py:229
  36.1 1.7 %collective-permute-done.2 = bf16[4,128,128]{2,1,0:T(8,128)(2,1)S(1)} collective-permute-done((bf16[4,128,128]{2,1,0:T(8,128)(2,1)S(1)}, bf16[4,128,128]{2,1,0:T(8,128)(2,1)S(1)}, u32[]{:S(2)}, u32[]{:S(2)}) %collective-permute-start.2) | collective-permute-done | bytes 131104 | tf_op jit(solution)/shard_map/ppermute | solution.py:229
  38.4 1.5 %collective-permute-start.3 = (bf16[4,128,128]{2,1,0:T(8,128)(2,1)S(1)}, bf16[4,128,128]{2,1,0:T(8,128)(2,1)S(1)}, u32[]{:S(2)}, u32[]{:S(2)}) collective-permute-start(bf16[4,128,128]{2,1,0:T(8,128)(2,1)S(1)} %fusion.3), channel_id=1, source_target_pairs={{0,32},{4,36},{8,40},{12,44},{16,48},{20,52},{24,56},{28,60},{32,0... | collective-permute-start | bytes 393224 | tf_op jit(solution)/shard_map/ppermute | solution.py:223
  39.9 3.4 %local_part.4.rest_0_ = f32[2048,512]{1,0:T(8,128)} custom-call(bf16[2048,512]{1,0:T(8,128)(2,1)} %get-tuple-element.10.q_ref, bf16[2048,512]{1,0:T(8,128)(2,1)} %get-tuple-element.11.k_ref, bf16[2048,512]{1,0:T(8,128)(2,1)} %get-tuple-element.12.v_ref, bf16[8,4,256,128]{3,2,1,0:T(8,128)(2,1)} %get-tuple-element.13.pre_ref), custom_call_target="tpu_custom_call" | custom-call | flops 536870912 | bytes 3670016 | tf_op jit(solution)/shard_map/local_part/pallas_call | solution.py:113
  44.1 2.8 %collective-permute-start.4 = (bf16[4,128,128]{2,1,0:T(8,128)(2,1)}, bf16[4,128,128]{2,1,0:T(8,128)(2,1)}, u32[]{:S(2)}, u32[]{:S(2)}) collective-permute-start(bf16[4,128,128]{2,1,0:T(8,128)(2,1)} %fusion.5), channel_id=1, source_target_pairs={{0,96},{4,100},{8,104},{12,108},{16,112},{20,116},{24,120},{28,124... | collective-permute-start | bytes 393224 | tf_op jit(solution)/shard_map/ppermute | solution.py:229
  46.9 3.4 %local_part.5.rest_0_ = f32[2048,512]{1,0:T(8,128)} custom-call(bf16[2048,512]{1,0:T(8,128)(2,1)} %get-tuple-element.10.q_ref, bf16[2048,512]{1,0:T(8,128)(2,1)} %get-tuple-element.11.k_ref, bf16[2048,512]{1,0:T(8,128)(2,1)} %get-tuple-element.12.v_ref, bf16[8,4,256,128]{3,2,1,0:T(8,128)(2,1)} %get-tuple-element.13.pre_ref, ...), custom_call_target="tpu_custom_call", output_to_operand_aliasing={{}: (4, {})} | custom-call | flops 536870912 | bytes 3670016 | tf_op jit(solution)/shard_map/local_part/pallas_call | solution.py:113
  50.3 3.4 %local_part.6.rest_0_ = f32[2048,512]{1,0:T(8,128)} custom-call(bf16[2048,512]{1,0:T(8,128)(2,1)} %get-tuple-element.10.q_ref, bf16[2048,512]{1,0:T(8,128)(2,1)} %get-tuple-element.11.k_ref, bf16[2048,512]{1,0:T(8,128)(2,1)} %get-tuple-element.12.v_ref, bf16[8,4,256,128]{3,2,1,0:T(8,128)(2,1)} %get-tuple-element.13.pre_ref, ...), custom_call_target="tpu_custom_call", output_to_operand_aliasing={{}: (4, {})} | custom-call | flops 536870912 | bytes 3670016 | tf_op jit(solution)/shard_map/local_part/pallas_call | solution.py:113
  53.7 3.4 %local_part.7.att_ref = f32[2048,512]{1,0:T(8,128)} custom-call(bf16[2048,512]{1,0:T(8,128)(2,1)} %get-tuple-element.10.q_ref, bf16[2048,512]{1,0:T(8,128)(2,1)} %get-tuple-element.11.k_ref, bf16[2048,512]{1,0:T(8,128)(2,1)} %get-tuple-element.12.v_ref, bf16[8,4,256,128]{3,2,1,0:T(8,128)(2,1)} %get-tuple-element.13.pre_ref, ...), custom_call_target="tpu_custom_call", output_to_operand_aliasing={{}: (4, {})} | custom-call | flops 536870912 | bytes 3670016 | tf_op jit(solution)/shard_map/local_part/pallas_call | solution.py:113
  57.2 1.8 %fusion.2.carried_ref = f32[4,128,128]{2,1,0:T(8,128)} fusion(bf16[4,128,128]{2,1,0:T(8,128)(2,1)S(1)} %collective-permute-done.1, bf16[4,128,128]{2,1,0:T(8,128)(2,1)} %copy-done.5, bf16[4,128,128]{2,1,0:T(8,128)(2,1)} %copy-done.4, bf16[4,128,128]{2,1,0:T(8,128)(2,1)} %collective-permute-done.4, f32[4,128,128]{2,1,0:T(8,128)S(1)} %copy-done.3, pred[]{:T(512)S(6)} %ge.7, ...), kind=kLoop, calls=%fused_computation.8 | loop fusion | flops 851968 | bytes 1048581 | tf_op jit(solution)/shard_map/add | solution.py:279
  59.0 2.9 %finish.7 = bf16[512,512]{1,0:T(8,128)(2,1)} custom-call(s32[1]{0:T(128)} %bitcast.5.place, bf16[2048,512]{1,0:T(8,128)(2,1)} %get-tuple-element.10.q_ref, f32[2048,512]{1,0:T(8,128)} %local_part.7.att_ref, f32[4,128,128]{2,1,0:T(8,128)} %fusion.2.carried_ref, f32[1,512]{1,0:T(1,128)} %bitcast.6), custom_call_target="tpu_custom_call" | custom-call | flops 134217728 | bytes 2097152 | tf_op jit(solution)/shard_map/finish/pallas_call | solution.py:145
  62.3 3.3 %finish.6 = bf16[512,512]{1,0:T(8,128)(2,1)} custom-call(s32[1]{0:T(128)} %bitcast.4.place, bf16[2048,512]{1,0:T(8,128)(2,1)} %get-tuple-element.10.q_ref, f32[2048,512]{1,0:T(8,128)} %local_part.7.att_ref, f32[4,128,128]{2,1,0:T(8,128)} %fusion.2.carried_ref, f32[1,512]{1,0:T(1,128)} %bitcast.7), custom_call_target="tpu_custom_call" | custom-call | flops 134217728 | bytes 2097152 | tf_op jit(solution)/shard_map/finish/pallas_call | solution.py:145
  65.6 2.9 %collective-permute-start.6 = (bf16[512,512]{1,0:T(8,128)(2,1)}, bf16[512,512]{1,0:T(8,128)(2,1)}, u32[]{:S(2)}, u32[]{:S(2)}) collective-permute-start(bf16[512,512]{1,0:T(8,128)(2,1)} %finish.6), channel_id=1, source_target_pairs={{0,3},{1,0},{2,1},{3,2},{4,5},{5,6},{6,7},{7,4},{8,11},{9,8},{10,9... | collective-permute-start | bytes 1572872 | tf_op jit(solution)/shard_map/ppermute | solution.py:262
  68.4 2.9 %finish.5 = bf16[512,512]{1,0:T(8,128)(2,1)} custom-call(s32[1]{0:T(128)} %bitcast.3.place, bf16[2048,512]{1,0:T(8,128)(2,1)} %get-tuple-element.10.q_ref, f32[2048,512]{1,0:T(8,128)} %local_part.7.att_ref, f32[4,128,128]{2,1,0:T(8,128)} %fusion.2.carried_ref, f32[1,512]{1,0:T(1,128)} %bitcast.8), custom_call_target="tpu_custom_call" | custom-call | flops 134217728 | bytes 2097152 | tf_op jit(solution)/shard_map/finish/pallas_call | solution.py:145
  71.3 4.0 %collective-permute-done.9 = bf16[512,512]{1,0:T(8,128)(2,1)} collective-permute-done((bf16[512,512]{1,0:T(8,128)(2,1)}, bf16[512,512]{1,0:T(8,128)(2,1)}, u32[]{:S(2)}, u32[]{:S(2)}) %collective-permute-start.9) | collective-permute-done | bytes 524320 | tf_op jit(solution)/shard_map/ppermute | solution.py:262
  75.4 2.9 %finish.4.n0 = bf16[512,512]{1,0:T(8,128)(2,1)} custom-call(s32[1]{0:T(128)} %bitcast.1.place, bf16[2048,512]{1,0:T(8,128)(2,1)} %get-tuple-element.10.q_ref, f32[2048,512]{1,0:T(8,128)} %local_part.7.att_ref, f32[4,128,128]{2,1,0:T(8,128)} %fusion.2.carried_ref, f32[1,512]{1,0:T(1,128)} %bitcast.9), custom_call_target="tpu_custom_call" | custom-call | flops 134217728 | bytes 2097152 | tf_op jit(solution)/shard_map/finish/pallas_call | solution.py:145
  79.0 4.9 %collective-permute-done.5.na = bf16[512,512]{1,0:T(8,128)(2,1)} collective-permute-done((bf16[512,512]{1,0:T(8,128)(2,1)}, bf16[512,512]{1,0:T(8,128)(2,1)}, u32[]{:S(2)}, u32[]{:S(2)}) %collective-permute-start.5) | collective-permute-done | bytes 524320 | tf_op jit(solution)/shard_map/ppermute | solution.py:262
  83.8 7.9 %mix_near.1.acc_ref = f32[512,2048]{1,0:T(8,128)} custom-call(bf16[512,512]{1,0:T(8,128)(2,1)} %finish.4.n0, bf16[512,512]{1,0:T(8,128)(2,1)} %collective-permute-done.5.na, bf16[512,512]{1,0:T(8,128)(2,1)} %collective-permute-done.6.nb, bf16[512,2048]{1,0:T(8,128)(2,1)} %w0.1, bf16[512,2048]{1,0:T(8,128)(2,1)} %copy-done, ...), custom_call_target="tpu_custom_call" | custom-call | flops 3221225472 | bytes 10485760 | tf_op jit(solution)/shard_map/mix_near/pallas_call | solution.py:180
  91.7 5.6 %mix_far.1 = bf16[512,2048]{1,0:T(8,128)(2,1)} custom-call(s32[1]{0:T(128)} %bitcast.core, f32[512,2048]{1,0:T(8,128)} %mix_near.1.acc_ref, bf16[512,512]{1,0:T(8,128)(2,1)} %collective-permute-done.10.nf, bf16[256,2048]{1,0:T(8,128)(2,1)} %copy-done.1, bf16[256,2048]{1,0:T(8,128)(2,1)} %collective-permute-done.12.other_ref), custom_call_target="tpu_custom_call" | custom-call | flops 1073741824 | bytes 8388608 | tf_op jit(solution)/shard_map/mix_far/pallas_call | solution.py:197
  (31 shorter events, 6.2 us)
Async XLA Ops:
  0.0 28.4 %collective-permute-start.7 = (bf16[512,2048]{1,0:T(8,128)(2,1)}, bf16[512,2048]{1,0:T(8,128)(2,1)S(1)}, u32[]{:S(2)}, u32[]{:S(2)}) collective-permute-start(bf16[512,2048]{1,0:T(8,128)(2,1)} %w0.1), channel_id=1, source_target_pairs={{0,1},{1,2},{2,3},{3,0},{4,7},{5,4},{6,5},{7,6},{8,9},{9,10},{10,1... | collective-permute-start | bytes 6291464 | tf_op jit(solution)/shard_map/ppermute | solution.py:262
  21.4 3.1 %collective-permute-start = (f32[4,128,128]{2,1,0:T(8,128)}, f32[4,128,128]{2,1,0:T(8,128)S(1)}, u32[]{:S(2)}, u32[]{:S(2)}) collective-permute-start(f32[4,128,128]{2,1,0:T(8,128)} %get-tuple-element.14), channel_id=1, source_target_pairs={{0,4},{4,0},{8,12},{12,8},{16,20},{20,16},{24,28},{28,24},{32,36},... | collective-permute-start | bytes 786440 | tf_op jit(solution)/shard_map/ppermute | solution.py:259
  24.5 10.1 %copy-start.2 = (f32[4,128,128]{2,1,0:T(8,128)}, f32[4,128,128]{2,1,0:T(8,128)S(1)}, u32[]{:S(2)}) copy-start(f32[4,128,128]{2,1,0:T(8,128)S(1)} %collective-permute-done) | copy-start | bytes 786436
  25.6 5.9 %collective-permute-start.1 = (bf16[4,128,128]{2,1,0:T(8,128)(2,1)S(1)}, bf16[4,128,128]{2,1,0:T(8,128)(2,1)S(1)}, u32[]{:S(2)}, u32[]{:S(2)}) collective-permute-start(bf16[4,128,128]{2,1,0:T(8,128)(2,1)S(1)} %add_convert_fusion), channel_id=1, source_target_pairs={{0,8},{4,12},{8,0},{12,4},{16,24},{20,28},{24,16},{28,20},{32,40},... | collective-permute-start | bytes 393224 | tf_op jit(solution)/shard_map/ppermute | solution.py:223
  28.4 15.0 %copy-start = (bf16[512,2048]{1,0:T(8,128)(2,1)}, bf16[512,2048]{1,0:T(8,128)(2,1)S(1)}, u32[]{:S(2)}) copy-start(bf16[512,2048]{1,0:T(8,128)(2,1)S(1)} %collective-permute-done.7.wa) | copy-start | bytes 6291460
  28.4 55.5 %collective-permute-start.8 = (bf16[512,2048]{1,0:T(8,128)(2,1)S(1)}, bf16[512,2048]{1,0:T(8,128)(2,1)}, u32[]{:S(2)}, u32[]{:S(2)}) collective-permute-start(bf16[512,2048]{1,0:T(8,128)(2,1)S(1)} %collective-permute-done.7.wa), channel_id=1, source_target_pairs={{0,4},{4,0},{8,12},{12,8},{16,20},{20,16},{24,28},{28,24},{32,36},... | collective-permute-start | bytes 6291464 | tf_op jit(solution)/shard_map/ppermute | solution.py:259
  31.5 6.3 %collective-permute-start.2 = (bf16[4,128,128]{2,1,0:T(8,128)(2,1)S(1)}, bf16[4,128,128]{2,1,0:T(8,128)(2,1)S(1)}, u32[]{:S(2)}, u32[]{:S(2)}) collective-permute-start(bf16[4,128,128]{2,1,0:T(8,128)(2,1)S(1)} %fusion.6), channel_id=1, source_target_pairs={{0,24},{4,28},{8,16},{12,20},{16,8},{20,12},{24,0},{28,4},{32,56},... | collective-permute-start | bytes 393224 | tf_op jit(solution)/shard_map/ppermute | solution.py:229
  35.7 26.5 %collective-permute-start.11 = (bf16[256,2048]{1,0:T(8,128)(2,1)}, bf16[256,2048]{1,0:T(8,128)(2,1)S(1)}, u32[]{:S(2)}, u32[]{:S(2)}) collective-permute-start(bf16[256,2048]{1,0:T(8,128)(2,1)} %constant_dynamic-slice_fusion), channel_id=1, source_target_pairs={{0,1},{1,2},{2,3},{3,0},{4,7},{5,4},{6,5},{7,6},{8,9},{9,10},{10,1... | collective-permute-start | bytes 3145736 | tf_op jit(solution)/shard_map/ppermute | solution.py:262
  37.8 0.7 copy-start.5
  38.4 5.0 %collective-permute-start.3 = (bf16[4,128,128]{2,1,0:T(8,128)(2,1)S(1)}, bf16[4,128,128]{2,1,0:T(8,128)(2,1)S(1)}, u32[]{:S(2)}, u32[]{:S(2)}) collective-permute-start(bf16[4,128,128]{2,1,0:T(8,128)(2,1)S(1)} %fusion.3), channel_id=1, source_target_pairs={{0,32},{4,36},{8,40},{12,44},{16,48},{20,52},{24,56},{28,60},{32,0... | collective-permute-start | bytes 393224 | tf_op jit(solution)/shard_map/ppermute | solution.py:223
  43.4 6.9 %copy-start.4 = (bf16[4,128,128]{2,1,0:T(8,128)(2,1)}, bf16[4,128,128]{2,1,0:T(8,128)(2,1)S(1)}, u32[]{:S(2)}) copy-start(bf16[4,128,128]{2,1,0:T(8,128)(2,1)S(1)} %collective-permute-done.3) | copy-start | bytes 393220
  44.1 13.0 %collective-permute-start.4 = (bf16[4,128,128]{2,1,0:T(8,128)(2,1)}, bf16[4,128,128]{2,1,0:T(8,128)(2,1)}, u32[]{:S(2)}, u32[]{:S(2)}) collective-permute-start(bf16[4,128,128]{2,1,0:T(8,128)(2,1)} %fusion.5), channel_id=1, source_target_pairs={{0,96},{4,100},{8,104},{12,108},{16,112},{20,116},{24,120},{28,124... | collective-permute-start | bytes 393224 | tf_op jit(solution)/shard_map/ppermute | solution.py:229
  53.7 3.4 %copy-start.3 = (f32[4,128,128]{2,1,0:T(8,128)S(1)}, f32[4,128,128]{2,1,0:T(8,128)}, u32[]{:S(2)}) copy-start(f32[4,128,128]{2,1,0:T(8,128)} %copy-done.2) | copy-start | bytes 786436
  61.9 13.5 %collective-permute-start.9 = (bf16[512,512]{1,0:T(8,128)(2,1)}, bf16[512,512]{1,0:T(8,128)(2,1)}, u32[]{:S(2)}, u32[]{:S(2)}) collective-permute-start(bf16[512,512]{1,0:T(8,128)(2,1)} %finish.7), channel_id=1, source_target_pairs={{0,1},{1,2},{2,3},{3,0},{4,7},{5,4},{6,5},{7,6},{8,9},{9,10},{10,1... | collective-permute-start | bytes 1572872 | tf_op jit(solution)/shard_map/ppermute | solution.py:262
  62.2 3.3 %copy-start.1 = (bf16[256,2048]{1,0:T(8,128)(2,1)}, bf16[256,2048]{1,0:T(8,128)(2,1)S(1)}, u32[]{:S(2)}) copy-start(bf16[256,2048]{1,0:T(8,128)(2,1)S(1)} %collective-permute-done.11.mine_ref) | copy-start | bytes 3145732
  62.2 29.5 %collective-permute-start.12 = (bf16[256,2048]{1,0:T(8,128)(2,1)S(1)}, bf16[256,2048]{1,0:T(8,128)(2,1)}, u32[]{:S(2)}, u32[]{:S(2)}) collective-permute-start(bf16[256,2048]{1,0:T(8,128)(2,1)S(1)} %collective-permute-done.11.mine_ref), channel_id=1, source_target_pairs={{0,4},{4,0},{8,12},{12,8},{16,20},{20,16},{24,28},{28,24},{32,36},... | collective-permute-start | bytes 3145736 | tf_op jit(solution)/shard_map/ppermute | solution.py:259
  65.6 13.4 %collective-permute-start.6 = (bf16[512,512]{1,0:T(8,128)(2,1)}, bf16[512,512]{1,0:T(8,128)(2,1)}, u32[]{:S(2)}, u32[]{:S(2)}) collective-permute-start(bf16[512,512]{1,0:T(8,128)(2,1)} %finish.6), channel_id=1, source_target_pairs={{0,3},{1,0},{2,1},{3,2},{4,5},{5,6},{6,7},{7,4},{8,11},{9,8},{10,9... | collective-permute-start | bytes 1572872 | tf_op jit(solution)/shard_map/ppermute | solution.py:262
  71.3 12.5 %collective-permute-start.5 = (bf16[512,512]{1,0:T(8,128)(2,1)}, bf16[512,512]{1,0:T(8,128)(2,1)}, u32[]{:S(2)}, u32[]{:S(2)}) collective-permute-start(bf16[512,512]{1,0:T(8,128)(2,1)} %finish.5), channel_id=1, source_target_pairs={{0,1},{1,2},{2,3},{3,0},{4,7},{5,4},{6,5},{7,6},{8,9},{9,10},{10,1... | collective-permute-start | bytes 1572872 | tf_op jit(solution)/shard_map/ppermute | solution.py:262
  75.4 16.3 %collective-permute-start.10 = (bf16[512,512]{1,0:T(8,128)(2,1)}, bf16[512,512]{1,0:T(8,128)(2,1)}, u32[]{:S(2)}, u32[]{:S(2)}) collective-permute-start(bf16[512,512]{1,0:T(8,128)(2,1)} %collective-permute-done.9), channel_id=1, source_target_pairs={{0,1},{1,2},{2,3},{3,0},{4,7},{5,4},{6,5},{7,6},{8,9},{9,10},{10,1... | collective-permute-start | bytes 1572872 | tf_op jit(solution)/shard_map/ppermute | solution.py:262

commit v2 on v0

v2 whole, which is shorter than its diff:
```python
import jax
import jax.numpy as jnp
from jax import lax
from jax.experimental import pallas as pl
from jax.experimental.pallas import tpu as pltpu
from jax.sharding import PartitionSpec as P


DH = 128
BLK = 256
F32 = jnp.float32
BF16 = jnp.bfloat16


def dot(a, b):
    return jnp.dot(a, b, preferred_element_type=F32)


def cost(flops, nbytes):
    return pl.CostEstimate(flops=int(flops), bytes_accessed=int(nbytes), transcendentals=0)


def hi_lo(state):
    high = state.astype(BF16)
    low = (state - high.astype(F32)).astype(BF16)
    return jnp.concatenate([high, low], axis=0)


def qkv_kernel(x_hbm, w_hbm, q_ref, k_ref, v_ref, pre_ref, tot_ref, acc, x_buf, w_buf, x_sem, w_sem):
    step = pl.program_id(0)
    steps = pl.num_programs(0)
    tile = x_buf.shape[1]

    def tokens(i):
        slot = lax.rem(i, 2)
        rows = pl.ds(pl.multiple_of(i * tile, tile), tile)
        return pltpu.make_async_copy(x_hbm.at[rows], x_buf.at[slot], x_sem.at[slot])

    def weight(which):
        return pltpu.make_async_copy(w_hbm.at[which], w_buf.at[which], w_sem.at[which])

    @pl.when(step == 0)
    def _():
        tokens(0).start()
        weight(1).start()
        weight(2).start()
        weight(0).start()
        acc[...] = jnp.zeros_like(acc)

    @pl.when(step + 1 < steps)
    def _():
        tokens(step + 1).start()

    tokens(step).wait()
    slot = lax.rem(step, 2)

    for which, out in ((1, k_ref), (2, v_ref), (0, q_ref)):

        @pl.when(step == 0)
        def _():
            weight(which).wait()

        out[...] = dot(x_buf[slot], w_buf[which]).astype(BF16)

    heads = acc.shape[0]
    for b in range(tile // BLK):
        rows = slice(b * BLK, (b + 1) * BLK)
        for h in range(heads):
            cols = slice(h * DH, (h + 1) * DH)
            before = acc[h]
            pre_ref[b, h] = hi_lo(before)
            acc[h] = before + lax.dot_general(
                k_ref[rows, cols], v_ref[rows, cols], (((0,), (0,)), ((), ())),
                preferred_element_type=F32,
            )

    @pl.when(step == steps - 1)
    def _():
        tot_ref[...] = acc[...]


def project(x, w_qkv, tile=512):
    tokens, width = x.shape
    feats = w_qkv.shape[2]
    heads = feats // DH
    blocks = tile // BLK
    rows = pl.BlockSpec((tile, feats), lambda i: (i, 0))
    return pl.pallas_call(
        qkv_kernel,
        grid=(tokens // tile,),
        in_specs=[pl.BlockSpec(memory_space=pl.ANY)] * 2,
        out_specs=[
            rows,
            rows,
            rows,
            pl.BlockSpec((blocks, heads, 2 * DH, DH), lambda i: (i, 0, 0, 0)),
            pl.BlockSpec((heads, DH, DH), lambda i: (0, 0, 0)),
        ],
        out_shape=[jax.ShapeDtypeStruct((tokens, feats), BF16)] * 3
        + [
            jax.ShapeDtypeStruct((tokens // BLK, heads, 2 * DH, DH), BF16),
            jax.ShapeDtypeStruct((heads, DH, DH), F32),
        ],
        scratch_shapes=[
            pltpu.VMEM((heads, DH, DH), F32),
            pltpu.VMEM((2, tile, width), BF16),
            pltpu.VMEM((3, width, feats), BF16),
            pltpu.SemaphoreType.DMA((2,)),
            pltpu.SemaphoreType.DMA((3,)),
        ],
        cost_estimate=cost(6 * tokens * width * feats, 2 * tokens * width + 6 * width * feats),
        name="project",
    )(x, w_qkv)


def local_kernel(q_ref, k_ref, v_ref, pre_ref, *rest):
    att_ref = rest[-1]
    heads = pre_ref.shape[1]
    lower = lax.broadcasted_iota(jnp.int32, (BLK, BLK), 0) >= lax.broadcasted_iota(
        jnp.int32, (BLK, BLK), 1
    )
    for b in range(q_ref.shape[0] // BLK):
        rows = slice(b * BLK, (b + 1) * BLK)
        for h in range(heads):
            cols = slice(h * DH, (h + 1) * DH)
            q = q_ref[rows, cols]
            scores = lax.dot_general(
                q, k_ref[rows, cols], (((1,), (1,)), ((), ())), preferred_element_type=F32
            )
            scores = jnp.where(lower, scores, 0.0).astype(BF16)
            att_ref[rows, cols] = dot(scores, v_ref[rows, cols]) + dot(
                jnp.concatenate([q, q], axis=1), pre_ref[b, h]
            )


def local_part(q, k, v, pre, att, piece, pieces, tile=256):
    tokens, feats = q.shape
    heads = feats // DH
    blocks = tile // BLK
    count = tokens // pieces
    start = piece * count // tile
    row = pl.BlockSpec((tile, feats), lambda i: (i + start, 0))
    return pl.pallas_call(
        local_kernel,
        grid=(count // tile,),
        in_specs=[
            row, row, row,
            pl.BlockSpec((blocks, heads, 2 * DH, DH), lambda i: (i + start, 0, 0, 0)),
        ]
        + [pl.BlockSpec(memory_space=pl.ANY)] * len(att),
        out_specs=row,
        out_shape=jax.ShapeDtypeStruct((tokens, feats), F32),
        input_output_aliases={4: 0} if att else {},
        cost_estimate=cost(8 * count * feats * BLK, 14 * count * feats),
        name="local_part",
    )(q, k, v, pre, *att)


def finish_kernel(place, q_ref, att_ref, core_ref, y1_ref, y2_ref, x1_ref, x2_ref, gain_ref, n_ref):
    heads = core_ref.shape[0]
    core, y, x = place[1], place[2], place[3]
    takes = (
        (core == 1, core_ref),
        (lax.rem(y, 2) == 1, y1_ref),
        (y >= 2, y2_ref),
        (lax.rem(x, 2) == 1, x1_ref),
        (x >= 2, x2_ref),
    )
    for h in range(heads):
        cols = slice(h * DH, (h + 1) * DH)
        carried = jnp.zeros((DH, DH), F32)
        for take, ref in takes:
            carried = carried + jnp.where(take, ref[h].astype(F32), 0.0)
        q = q_ref[:, cols]
        att = att_ref[:, cols] + dot(jnp.concatenate([q, q], axis=1), hi_lo(carried))
        mean_sq = jnp.mean(att * att, axis=-1, keepdims=True)
        n_ref[:, cols] = (att / jnp.sqrt(mean_sq + 1e-06) * gain_ref[:, cols]).astype(BF16)


def finish(place, direction, shift, q, att, received, gain, parts, tile=256):
    tokens, feats = q.shape
    count = tokens // parts
    per = count // tile
    heads = feats // DH

    def row(i, place):
        to = place[0] + direction * (1 - 2 * place[1]) + shift + parts
        return (lax.rem(to, parts) * per + i, 0)

    return pl.pallas_call(
        finish_kernel,
        grid_spec=pltpu.PrefetchScalarGridSpec(
            num_scalar_prefetch=1,
            grid=(per,),
            in_specs=[pl.BlockSpec((tile, feats), row), pl.BlockSpec((tile, feats), row)]
            + [pl.BlockSpec((heads, DH, DH), lambda i, place: (0, 0, 0))] * len(received)
            + [pl.BlockSpec((1, feats), lambda i, place: (0, 0))],
            out_specs=pl.BlockSpec((tile, feats), lambda i, place: (i, 0)),
        ),
        out_shape=jax.ShapeDtypeStruct((count, feats), BF16),
        cost_estimate=cost(2 * count * feats * DH * 2, count * feats * 8),
        name="finish",
    )(place, q, att, *received, gain)


def first_kernel(n0, na, w0, wa, acc_ref):
    acc_ref[...] = dot(n0[...], w0[...]) + dot(na[...], wa[...])


def last_kernel(core, acc_ref, nb, nf, wb, mine_ref, other_ref, out_ref):
    half = mine_ref.shape[0]
    mine = pl.multiple_of(core[0] * half, half)
    other = pl.multiple_of((1 - core[0]) * half, half)
    acc = acc_ref[...] + dot(nb[...], wb[...])
    acc += dot(nf[:, pl.ds(mine, half)], mine_ref[...])
    acc += dot(nf[:, pl.ds(other, half)], other_ref[...])
    out_ref[...] = acc.astype(BF16)


def mix_first(normed, weights, tile=512):
    rows, feats = normed[0].shape
    width = weights[0].shape[1]
    return pl.pallas_call(
        first_kernel,
        grid=(width // tile,),
        in_specs=[pl.BlockSpec(a.shape, lambda i: (0, 0)) for a in normed]
        + [pl.BlockSpec((a.shape[0], tile), lambda i: (0, i)) for a in weights],
        out_specs=pl.BlockSpec((rows, tile), lambda i: (0, i)),
        out_shape=jax.ShapeDtypeStruct((rows, width), F32),
        cost_estimate=cost(4 * rows * feats * width, 8 * rows * width),
        compiler_params=pltpu.CompilerParams(vmem_limit_bytes=24 << 20),
        name="mix_first",
    )(*normed, *weights)


def mix_last(core, acc, normed, weights, tile=512):
    rows, feats = normed[0].shape
    width = acc.shape[1]
    column = lambda a: pl.BlockSpec((a.shape[0], tile), lambda i, core: (0, i))
    return pl.pallas_call(
        last_kernel,
        grid_spec=pltpu.PrefetchScalarGridSpec(
            num_scalar_prefetch=1,
            grid=(width // tile,),
            in_specs=[column(acc)]
            + [pl.BlockSpec(a.shape, lambda i, core: (0, 0)) for a in normed]
            + [column(a) for a in weights],
            out_specs=pl.BlockSpec((rows, tile), lambda i, core: (0, i)),
        ),
        out_shape=jax.ShapeDtypeStruct((rows, width), BF16),
        cost_estimate=cost(4 * rows * feats * width, 8 * rows * width),
        compiler_params=pltpu.CompilerParams(vmem_limit_bytes=24 << 20),
        name="mix_last",
    )(core, acc, *normed, *weights)


def pair_up(size, stride, total, first):
    pairs = []
    for i in range(total):
        at = (i // stride) % size
        to = at ^ 1 if first else (at + (1 if at % 2 else -1)) % size
        pairs.append((i, i + (to - at) * stride))
    return pairs


def pair_rounds(value, stride, total):
    value = value.astype(BF16)
    other = lax.ppermute(value, "seq", pair_up(4, stride, total, True))
    pair = (value.astype(F32) + other.astype(F32)).astype(BF16)
    far = lax.ppermute(pair, "seq", pair_up(4, stride, total, False))
    return other, far, pair.astype(F32) + far.astype(F32)


def layer(inputs, w_qkv, norm_gain, w_out):
    parts = lax.axis_size("head")
    total = lax.axis_size("seq")
    seq = lax.axis_index("seq")
    core = lax.rem(seq, 2)
    y = lax.rem(seq // 2, 4)
    x = seq // 8
    head = lax.axis_index("head")
    core_id = core.astype(jnp.int32).reshape(1)
    place = jnp.stack([head, core, y, x]).astype(jnp.int32)

    def along(direction):
        pairs = []
        for i in range(total):
            shift = direction * (1 - 2 * (i % 2))
            for h in range(parts):
                pairs.append((i * parts + h, i * parts + (h + shift) % parts))
        return pairs

    partner = [(i, i ^ 1) for i in range(total)]

    def swap(a):
        return lax.ppermute(a, "seq", partner)

    def send(a, direction):
        return lax.ppermute(a, ("seq", "head"), along(direction))

    near = send(w_out, 1)
    rows = w_out.shape[0] // 2
    far = send(lax.dynamic_slice_in_dim(near, core * rows, rows, 0), 1)
    near_other = swap(near)
    far_other = swap(far)

    q, k, v, pre, tot = project(inputs, w_qkv)
    other = swap(tot)
    att = []
    for piece in range(4):
        att = [local_part(q, k, v, pre, att, piece, 4)]
    att = att[0]
    y1, y2, row = pair_rounds(tot + other, 2, total)
    x1, x2, _ = pair_rounds(row, 8, total)
    received = (other, y1, y2, x1, x2)

    gain = norm_gain.reshape(1, -1)
    nf = send(finish(place, 0, 2, q, att, received, gain, parts), 1)
    na = send(finish(place, 1, 0, q, att, received, gain, parts), 1)
    nb = send(finish(place, -1, 0, q, att, received, gain, parts), -1)
    nf = send(nf, 1)
    n0 = finish(place, 0, 0, q, att, received, gain, parts)
    acc = mix_first([n0, na], [w_out, near])
    return mix_last(core_id, acc, [nb, nf], [near_other, far, far_other])


def solution(mesh):
    return jax.shard_map(
        layer,
        mesh=mesh,
        in_specs=(P("seq", None), P(None, None, "head"), P("head"), P("head", None)),
        out_specs=P(("seq", "head"), None),
        check_vma=False,
    )
```

time: 105 us -> 97.5 us (0.929)
  the two profiles are of different devices: /device:TPU:0 before, /device:TPU:1 now
where the time goes in v2:
time: 97.5 us; the launch traced here: 96.9 us
  Pallas kernels  59.6 us (61%)
  starting transfers between devices  21.9 us (22%)
  waiting for transfers between devices  6.83 us (7%)
  local copies, waits for them, and re-layouts  5.08 us (5%)
  other arithmetic  3.42 us (4%)
    pallas_call x1, Pallas kernels, project(): pl.pallas_call(qkv_kernel, grid=(tokens // tile,), in_specs=[pl.BlockSpec...  20.1 us
    pallas_call x4, Pallas kernels, finish(): pl.pallas_call(finish_kernel, grid_spec=pltpu.PrefetchScalarGridSpec(num_...  15.5 us
    ppermute x6, starting transfers between devices, send(): return lax.ppermute(a, ('seq', 'head'), along(direction))  14 us
    pallas_call x4, Pallas kernels, local_part(): pl.pallas_call(local_kernel, grid=(count // tile,), in_specs=[row, row, r...  13.6 us
    pallas_call x1, Pallas kernels, mix_last(): pl.pallas_call(last_kernel, grid_spec=pltpu.PrefetchScalarGridSpec(num_sc...  5.95 us
    ppermute x2, starting transfers between devices, pair_rounds(): far = lax.ppermute(pair, 'seq', pair_up(4, stride, total, False))  4.72 us
    pallas_call x1, Pallas kernels, mix_first(): pl.pallas_call(first_kernel, grid=(width // tile,), in_specs=[pl.BlockSpe...  4.39 us
    unnamed x12, local copies, waits for them, and re-layouts  3.94 us
  transfers between devices with their start and end apart: 13, of which 4 were waited for; matrix products, arithmetic and copies ran while one was open for 5% of the time, Pallas kernels for 55%

profile of v2, /device:TPU:1, one launch (start us, length us, event | category | flops | bytes accessed | tf_op | source)
XLA Modules:
  0.0 96.9 jit_solution(15063234168772907743)
XLA Ops:
  0.0 4.6 %collective-permute-start.6 = (bf16[512,2048]{1,0:T(8,128)(2,1)}, bf16[512,2048]{1,0:T(8,128)(2,1)S(1)}, u32[]{:S(2)}, u32[]{:S(2)}) collective-permute-start(bf16[512,2048]{1,0:T(8,128)(2,1)} %w0.1), channel_id=1, source_target_pairs={{0,1},{1,2},{2,3},{3,0},{4,7},{5,4},{6,5},{7,6},{8,9},{9,10},{10,1... | collective-permute-start | bytes 6291464 | tf_op jit(solution)/shard_map/ppermute | solution.py:299
  4.6 20.1 %project.1 = (bf16[2048,512]{1,0:T(8,128)(2,1)}, bf16[2048,512]{1,0:T(8,128)(2,1)}, bf16[2048,512]{1,0:T(8,128)(2,1)}, bf16[8,4,256,128]{3,2,1,0:T(8,128)(2,1)}, f32[4,128,128]{2,1,0:T(8,128)}) custom-call(bf16[2048,2048]{1,0:T(8,128)(2,1)} %x_hbm.1, bf16[3,2048,512]{2,1,0:T(8,128)(2,1)} %w_hbm.1), custom_call_target="tpu_custom_call" | custom-call | flops 12884901888 | bytes 14680064 | tf_op jit(solution)/shard_map/project/pallas_call | solution.py:88
  24.8 1.7 %collective-permute-done.core_ref = f32[4,128,128]{2,1,0:T(8,128)S(1)} collective-permute-done((f32[4,128,128]{2,1,0:T(8,128)}, f32[4,128,128]{2,1,0:T(8,128)S(1)}, u32[]{:S(2)}, u32[]{:S(2)}) %collective-permute-start) | collective-permute-done | bytes 262176 | tf_op jit(solution)/shard_map/ppermute | solution.py:296
  27.6 1.4 %collective-permute-start.1 = (bf16[4,128,128]{2,1,0:T(8,128)(2,1)S(1)}, bf16[4,128,128]{2,1,0:T(8,128)(2,1)S(1)}, u32[]{:S(2)}, u32[]{:S(2)}) collective-permute-start(bf16[4,128,128]{2,1,0:T(8,128)(2,1)S(1)} %add_convert_fusion.3), channel_id=1, source_target_pairs={{0,8},{4,12},{8,0},{12,4},{16,24},{20,28},{24,16},{28,20},{32,40},... | collective-permute-start | bytes 393224 | tf_op jit(solution)/shard_map/ppermute | solution.py:268
  30.1 1.9 %collective-permute-start.11 = (bf16[256,2048]{1,0:T(8,128)(2,1)}, bf16[256,2048]{1,0:T(8,128)(2,1)S(1)}, u32[]{:S(2)}, u32[]{:S(2)}) collective-permute-start(bf16[256,2048]{1,0:T(8,128)(2,1)} %constant_dynamic-slice_fusion), channel_id=1, source_target_pairs={{0,1},{1,2},{2,3},{3,0},{4,7},{5,4},{6,5},{7,6},{8,9},{9,10},{10,1... | collective-permute-start | bytes 3145736 | tf_op jit(solution)/shard_map/ppermute | solution.py:299
  32.6 2.8 %collective-permute-start.2 = (bf16[4,128,128]{2,1,0:T(8,128)(2,1)S(1)}, bf16[4,128,128]{2,1,0:T(8,128)(2,1)S(1)}, u32[]{:S(2)}, u32[]{:S(2)}) collective-permute-start(bf16[4,128,128]{2,1,0:T(8,128)(2,1)S(1)} %add_convert_fusion.2), channel_id=1, source_target_pairs={{0,24},{4,28},{8,16},{12,20},{16,8},{20,12},{24,0},{28,4},{32,56},... | collective-permute-start | bytes 393224 | tf_op jit(solution)/shard_map/ppermute | solution.py:270
  35.4 2.7 %collective-permute-done.2.y2_ref = bf16[4,128,128]{2,1,0:T(8,128)(2,1)S(1)} collective-permute-done((bf16[4,128,128]{2,1,0:T(8,128)(2,1)S(1)}, bf16[4,128,128]{2,1,0:T(8,128)(2,1)S(1)}, u32[]{:S(2)}, u32[]{:S(2)}) %collective-permute-start.2) | collective-permute-done | bytes 131104 | tf_op jit(solution)/shard_map/ppermute | solution.py:270
  39.4 1.2 %collective-permute-start.3 = (bf16[4,128,128]{2,1,0:T(8,128)(2,1)}, bf16[4,128,128]{2,1,0:T(8,128)(2,1)}, u32[]{:S(2)}, u32[]{:S(2)}) collective-permute-start(bf16[4,128,128]{2,1,0:T(8,128)(2,1)} %add_convert_fusion.1), channel_id=1, source_target_pairs={{0,32},{4,36},{8,40},{12,44},{16,48},{20,52},{24,56},{28,60},{32,0... | collective-permute-start | bytes 393224 | tf_op jit(solution)/shard_map/ppermute | solution.py:268
  40.6 3.4 %local_part.4.rest_0_ = f32[2048,512]{1,0:T(8,128)} custom-call(bf16[2048,512]{1,0:T(8,128)(2,1)} %get-tuple-element.10.q_ref, bf16[2048,512]{1,0:T(8,128)(2,1)} %get-tuple-element.11.k_ref, bf16[2048,512]{1,0:T(8,128)(2,1)} %get-tuple-element.12.v_ref, bf16[8,4,256,128]{3,2,1,0:T(8,128)(2,1)} %get-tuple-element.13.pre_ref), custom_call_target="tpu_custom_call" | custom-call | flops 536870912 | bytes 3670016 | tf_op jit(solution)/shard_map/local_part/pallas_call | solution.py:143
  44.0 3.4 %local_part.5.rest_0_ = f32[2048,512]{1,0:T(8,128)} custom-call(bf16[2048,512]{1,0:T(8,128)(2,1)} %get-tuple-element.10.q_ref, bf16[2048,512]{1,0:T(8,128)(2,1)} %get-tuple-element.11.k_ref, bf16[2048,512]{1,0:T(8,128)(2,1)} %get-tuple-element.12.v_ref, bf16[8,4,256,128]{3,2,1,0:T(8,128)(2,1)} %get-tuple-element.13.pre_ref, ...), custom_call_target="tpu_custom_call", output_to_operand_aliasing={{}: (4, {})} | custom-call | flops 536870912 | bytes 3670016 | tf_op jit(solution)/shard_map/local_part/pallas_call | solution.py:143
  47.5 3.4 %local_part.6.rest_0_ = f32[2048,512]{1,0:T(8,128)} custom-call(bf16[2048,512]{1,0:T(8,128)(2,1)} %get-tuple-element.10.q_ref, bf16[2048,512]{1,0:T(8,128)(2,1)} %get-tuple-element.11.k_ref, bf16[2048,512]{1,0:T(8,128)(2,1)} %get-tuple-element.12.v_ref, bf16[8,4,256,128]{3,2,1,0:T(8,128)(2,1)} %get-tuple-element.13.pre_ref, ...), custom_call_target="tpu_custom_call", output_to_operand_aliasing={{}: (4, {})} | custom-call | flops 536870912 | bytes 3670016 | tf_op jit(solution)/shard_map/local_part/pallas_call | solution.py:143
  51.9 1.9 %collective-permute-start.4 = (bf16[4,128,128]{2,1,0:T(8,128)(2,1)S(1)}, bf16[4,128,128]{2,1,0:T(8,128)(2,1)S(1)}, u32[]{:S(2)}, u32[]{:S(2)}) collective-permute-start(bf16[4,128,128]{2,1,0:T(8,128)(2,1)S(1)} %add_convert_fusion), channel_id=1, source_target_pairs={{0,96},{4,100},{8,104},{12,108},{16,112},{20,116},{24,120},{28,124... | collective-permute-start | bytes 393224 | tf_op jit(solution)/shard_map/ppermute | solution.py:270
  53.8 3.4 %local_part.7.att_ref = f32[2048,512]{1,0:T(8,128)} custom-call(bf16[2048,512]{1,0:T(8,128)(2,1)} %get-tuple-element.10.q_ref, bf16[2048,512]{1,0:T(8,128)(2,1)} %get-tuple-element.11.k_ref, bf16[2048,512]{1,0:T(8,128)(2,1)} %get-tuple-element.12.v_ref, bf16[8,4,256,128]{3,2,1,0:T(8,128)(2,1)} %get-tuple-element.13.pre_ref, ...), custom_call_target="tpu_custom_call", output_to_operand_aliasing={{}: (4, {})} | custom-call | flops 536870912 | bytes 3670016 | tf_op jit(solution)/shard_map/local_part/pallas_call | solution.py:143
  58.4 3.9 %finish.7 = bf16[512,512]{1,0:T(8,128)(2,1)} custom-call(s32[4]{0:T(128)} %pad_add_fusion.place, bf16[2048,512]{1,0:T(8,128)(2,1)} %get-tuple-element.10.q_ref, f32[2048,512]{1,0:T(8,128)} %local_part.7.att_ref, f32[4,128,128]{2,1,0:T(8,128)} %copy-done.2, bf16[4,128,128]{2,1,0:T(8,128)(2,1)} %copy-done.3, bf16[4,128,128]{2,1,0:T(8,128)(2,1)} %copy-done.4, ...), custom_call_target="tpu_custom_call" | custom-call | flops 134217728 | bytes 2097152 | tf_op jit(solution)/shard_map/finish/pallas_call | solution.py:190
  62.3 2.3 %collective-permute-start.8 = (bf16[512,512]{1,0:T(8,128)(2,1)}, bf16[512,512]{1,0:T(8,128)(2,1)}, u32[]{:S(2)}, u32[]{:S(2)}) collective-permute-start(bf16[512,512]{1,0:T(8,128)(2,1)} %finish.7), channel_id=1, source_target_pairs={{0,1},{1,2},{2,3},{3,0},{4,7},{5,4},{6,5},{7,6},{8,9},{9,10},{10,1... | collective-permute-start | bytes 1572872 | tf_op jit(solution)/shard_map/ppermute | solution.py:299
  65.1 3.9 %finish.5 = bf16[512,512]{1,0:T(8,128)(2,1)} custom-call(s32[4]{0:T(128)} %pad_add_fusion.place, bf16[2048,512]{1,0:T(8,128)(2,1)} %get-tuple-element.10.q_ref, f32[2048,512]{1,0:T(8,128)} %local_part.7.att_ref, f32[4,128,128]{2,1,0:T(8,128)} %copy-done.2, bf16[4,128,128]{2,1,0:T(8,128)(2,1)} %copy-done.3, bf16[4,128,128]{2,1,0:T(8,128)(2,1)} %copy-done.4, ...), custom_call_target="tpu_custom_call" | custom-call | flops 134217728 | bytes 2097152 | tf_op jit(solution)/shard_map/finish/pallas_call | solution.py:190
  69.0 2.6 %collective-permute-start.5 = (bf16[512,512]{1,0:T(8,128)(2,1)}, bf16[512,512]{1,0:T(8,128)(2,1)}, u32[]{:S(2)}, u32[]{:S(2)}) collective-permute-start(bf16[512,512]{1,0:T(8,128)(2,1)} %finish.5), channel_id=1, source_target_pairs={{0,1},{1,2},{2,3},{3,0},{4,7},{5,4},{6,5},{7,6},{8,9},{9,10},{10,1... | collective-permute-start | bytes 1572872 | tf_op jit(solution)/shard_map/ppermute | solution.py:299
  71.6 3.9 %finish.6 = bf16[512,512]{1,0:T(8,128)(2,1)} custom-call(s32[4]{0:T(128)} %pad_add_fusion.place, bf16[2048,512]{1,0:T(8,128)(2,1)} %get-tuple-element.10.q_ref, f32[2048,512]{1,0:T(8,128)} %local_part.7.att_ref, f32[4,128,128]{2,1,0:T(8,128)} %copy-done.2, bf16[4,128,128]{2,1,0:T(8,128)(2,1)} %copy-done.3, bf16[4,128,128]{2,1,0:T(8,128)(2,1)} %copy-done.4, ...), custom_call_target="tpu_custom_call" | custom-call | flops 134217728 | bytes 2097152 | tf_op jit(solution)/shard_map/finish/pallas_call | solution.py:190
  75.5 2.7 %collective-permute-start.9 = (bf16[512,512]{1,0:T(8,128)(2,1)}, bf16[512,512]{1,0:T(8,128)(2,1)}, u32[]{:S(2)}, u32[]{:S(2)}) collective-permute-start(bf16[512,512]{1,0:T(8,128)(2,1)} %collective-permute-done.8), channel_id=1, source_target_pairs={{0,1},{1,2},{2,3},{3,0},{4,7},{5,4},{6,5},{7,6},{8,9},{9,10},{10,1... | collective-permute-start | bytes 1572872 | tf_op jit(solution)/shard_map/ppermute | solution.py:299
  78.2 3.9 %finish.4.n0 = bf16[512,512]{1,0:T(8,128)(2,1)} custom-call(s32[4]{0:T(128)} %pad_add_fusion.place, bf16[2048,512]{1,0:T(8,128)(2,1)} %get-tuple-element.10.q_ref, f32[2048,512]{1,0:T(8,128)} %local_part.7.att_ref, f32[4,128,128]{2,1,0:T(8,128)} %copy-done.2, bf16[4,128,128]{2,1,0:T(8,128)(2,1)} %copy-done.3, bf16[4,128,128]{2,1,0:T(8,128)(2,1)} %copy-done.4, ...), custom_call_target="tpu_custom_call" | custom-call | flops 134217728 | bytes 2097152 | tf_op jit(solution)/shard_map/finish/pallas_call | solution.py:190
  83.1 1.6 %copy-done.1 = bf16[512,2048]{1,0:T(8,128)(2,1)S(1)} copy-done((bf16[512,2048]{1,0:T(8,128)(2,1)S(1)}, bf16[512,2048]{1,0:T(8,128)(2,1)}, u32[]{:S(2)}) %copy-start.1) | copy-done | bytes 2097176
  84.7 4.4 %mix_first.1.acc_ref = f32[512,2048]{1,0:T(8,128)S(1)} custom-call(bf16[512,512]{1,0:T(8,128)(2,1)S(1)} %copy-done, bf16[512,512]{1,0:T(8,128)(2,1)} %collective-permute-done.5.na, bf16[512,2048]{1,0:T(8,128)(2,1)S(1)} %copy-done.1, bf16[512,2048]{1,0:T(8,128)(2,1)S(1)} %collective-permute-done.6.wa), custom_call_target="tpu_custom_call" | custom-call | flops 2147483648 | bytes 8388608 | tf_op jit(solution)/shard_map/mix_first/pallas_call | solution.py:223
  89.1 1.9 %collective-permute-done.7.nb = bf16[512,512]{1,0:T(8,128)(2,1)} collective-permute-done((bf16[512,512]{1,0:T(8,128)(2,1)}, bf16[512,512]{1,0:T(8,128)(2,1)}, u32[]{:S(2)}, u32[]{:S(2)}) %collective-permute-start.7) | collective-permute-done | bytes 524320 | tf_op jit(solution)/shard_map/ppermute | solution.py:299
  91.0 6.0 %mix_last.1 = bf16[512,2048]{1,0:T(8,128)(2,1)} custom-call(s32[1]{0:T(128)} %bitcast.core, f32[512,2048]{1,0:T(8,128)S(1)} %mix_first.1.acc_ref, bf16[512,512]{1,0:T(8,128)(2,1)} %collective-permute-done.7.nb, bf16[512,512]{1,0:T(8,128)(2,1)} %collective-permute-done.9.nf, bf16[512,2048]{1,0:T(8,128)(2,1)} %collective-permute-done.10.wb, ...), custom_call_target="tpu_custom_call" | custom-call | flops 2147483648 | bytes 8388608 | tf_op jit(solution)/shard_map/mix_last/pallas_call | solution.py:240
  (31 shorter events, 8.1 us)
Async XLA Ops:
  0.0 28.9 %collective-permute-start.6 = (bf16[512,2048]{1,0:T(8,128)(2,1)}, bf16[512,2048]{1,0:T(8,128)(2,1)S(1)}, u32[]{:S(2)}, u32[]{:S(2)}) collective-permute-start(bf16[512,2048]{1,0:T(8,128)(2,1)} %w0.1), channel_id=1, source_target_pairs={{0,1},{1,2},{2,3},{3,0},{4,7},{5,4},{6,5},{7,6},{8,9},{9,10},{10,1... | collective-permute-start | bytes 6291464 | tf_op jit(solution)/shard_map/ppermute | solution.py:299
  24.7 1.8 %collective-permute-start = (f32[4,128,128]{2,1,0:T(8,128)}, f32[4,128,128]{2,1,0:T(8,128)S(1)}, u32[]{:S(2)}, u32[]{:S(2)}) collective-permute-start(f32[4,128,128]{2,1,0:T(8,128)} %get-tuple-element.14), channel_id=1, source_target_pairs={{0,4},{4,0},{8,12},{12,8},{16,20},{20,16},{24,28},{28,24},{32,36},... | collective-permute-start | bytes 786440 | tf_op jit(solution)/shard_map/ppermute | solution.py:296
  26.5 17.5 %copy-start.2 = (f32[4,128,128]{2,1,0:T(8,128)}, f32[4,128,128]{2,1,0:T(8,128)S(1)}, u32[]{:S(2)}) copy-start(f32[4,128,128]{2,1,0:T(8,128)S(1)} %collective-permute-done.core_ref) | copy-start | bytes 786436
  27.6 5.0 %collective-permute-start.1 = (bf16[4,128,128]{2,1,0:T(8,128)(2,1)S(1)}, bf16[4,128,128]{2,1,0:T(8,128)(2,1)S(1)}, u32[]{:S(2)}, u32[]{:S(2)}) collective-permute-start(bf16[4,128,128]{2,1,0:T(8,128)(2,1)S(1)} %add_convert_fusion.3), channel_id=1, source_target_pairs={{0,8},{4,12},{8,0},{12,4},{16,24},{20,28},{24,16},{28,20},{32,40},... | collective-permute-start | bytes 393224 | tf_op jit(solution)/shard_map/ppermute | solution.py:268
  30.1 34.5 %collective-permute-start.11 = (bf16[256,2048]{1,0:T(8,128)(2,1)}, bf16[256,2048]{1,0:T(8,128)(2,1)S(1)}, u32[]{:S(2)}, u32[]{:S(2)}) collective-permute-start(bf16[256,2048]{1,0:T(8,128)(2,1)} %constant_dynamic-slice_fusion), channel_id=1, source_target_pairs={{0,1},{1,2},{2,3},{3,0},{4,7},{5,4},{6,5},{7,6},{8,9},{9,10},{10,1... | collective-permute-start | bytes 3145736 | tf_op jit(solution)/shard_map/ppermute | solution.py:299
  32.0 58.9 %collective-permute-start.10 = (bf16[512,2048]{1,0:T(8,128)(2,1)S(1)}, bf16[512,2048]{1,0:T(8,128)(2,1)}, u32[]{:S(2)}, u32[]{:S(2)}) collective-permute-start(bf16[512,2048]{1,0:T(8,128)(2,1)S(1)} %collective-permute-done.6.wa), channel_id=1, source_target_pairs={{0,4},{4,0},{8,12},{12,8},{16,20},{20,16},{24,28},{28,24},{32,36},... | collective-permute-start | bytes 6291464 | tf_op jit(solution)/shard_map/ppermute | solution.py:296
  32.6 11.5 %copy-start.3 = (bf16[4,128,128]{2,1,0:T(8,128)(2,1)}, bf16[4,128,128]{2,1,0:T(8,128)(2,1)S(1)}, u32[]{:S(2)}) copy-start(bf16[4,128,128]{2,1,0:T(8,128)(2,1)S(1)} %collective-permute-done.1.y1_ref) | copy-start | bytes 393220
  32.6 5.5 %collective-permute-start.2 = (bf16[4,128,128]{2,1,0:T(8,128)(2,1)S(1)}, bf16[4,128,128]{2,1,0:T(8,128)(2,1)S(1)}, u32[]{:S(2)}, u32[]{:S(2)}) collective-permute-start(bf16[4,128,128]{2,1,0:T(8,128)(2,1)S(1)} %add_convert_fusion.2), channel_id=1, source_target_pairs={{0,24},{4,28},{8,16},{12,20},{16,8},{20,12},{24,0},{28,4},{32,56},... | collective-permute-start | bytes 393224 | tf_op jit(solution)/shard_map/ppermute | solution.py:270
  38.1 0.7 copy-start.4
  39.4 11.4 %collective-permute-start.3 = (bf16[4,128,128]{2,1,0:T(8,128)(2,1)}, bf16[4,128,128]{2,1,0:T(8,128)(2,1)}, u32[]{:S(2)}, u32[]{:S(2)}) collective-permute-start(bf16[4,128,128]{2,1,0:T(8,128)(2,1)} %add_convert_fusion.1), channel_id=1, source_target_pairs={{0,32},{4,36},{8,40},{12,44},{16,48},{20,52},{24,56},{28,60},{32,0... | collective-permute-start | bytes 393224 | tf_op jit(solution)/shard_map/ppermute | solution.py:268
  51.9 5.9 %collective-permute-start.4 = (bf16[4,128,128]{2,1,0:T(8,128)(2,1)S(1)}, bf16[4,128,128]{2,1,0:T(8,128)(2,1)S(1)}, u32[]{:S(2)}, u32[]{:S(2)}) collective-permute-start(bf16[4,128,128]{2,1,0:T(8,128)(2,1)S(1)} %add_convert_fusion), channel_id=1, source_target_pairs={{0,96},{4,100},{8,104},{12,108},{16,112},{20,116},{24,120},{28,124... | collective-permute-start | bytes 393224 | tf_op jit(solution)/shard_map/ppermute | solution.py:270
  57.8 0.6 copy-start.5
  62.3 13.1 %collective-permute-start.8 = (bf16[512,512]{1,0:T(8,128)(2,1)}, bf16[512,512]{1,0:T(8,128)(2,1)}, u32[]{:S(2)}, u32[]{:S(2)}) collective-permute-start(bf16[512,512]{1,0:T(8,128)(2,1)} %finish.7), channel_id=1, source_target_pairs={{0,1},{1,2},{2,3},{3,0},{4,7},{5,4},{6,5},{7,6},{8,9},{9,10},{10,1... | collective-permute-start | bytes 1572872 | tf_op jit(solution)/shard_map/ppermute | solution.py:299
  64.6 26.4 %collective-permute-start.12 = (bf16[256,2048]{1,0:T(8,128)(2,1)S(1)}, bf16[256,2048]{1,0:T(8,128)(2,1)}, u32[]{:S(2)}, u32[]{:S(2)}) collective-permute-start(bf16[256,2048]{1,0:T(8,128)(2,1)S(1)} %collective-permute-done.11.mine_ref), channel_id=1, source_target_pairs={{0,4},{4,0},{8,12},{12,8},{16,20},{20,16},{24,28},{28,24},{32,36},... | collective-permute-start | bytes 3145736 | tf_op jit(solution)/shard_map/ppermute | solution.py:296
  69.0 13.0 %collective-permute-start.5 = (bf16[512,512]{1,0:T(8,128)(2,1)}, bf16[512,512]{1,0:T(8,128)(2,1)}, u32[]{:S(2)}, u32[]{:S(2)}) collective-permute-start(bf16[512,512]{1,0:T(8,128)(2,1)} %finish.5), channel_id=1, source_target_pairs={{0,1},{1,2},{2,3},{3,0},{4,7},{5,4},{6,5},{7,6},{8,9},{9,10},{10,1... | collective-permute-start | bytes 1572872 | tf_op jit(solution)/shard_map/ppermute | solution.py:299
  75.5 15.5 %collective-permute-start.7 = (bf16[512,512]{1,0:T(8,128)(2,1)}, bf16[512,512]{1,0:T(8,128)(2,1)}, u32[]{:S(2)}, u32[]{:S(2)}) collective-permute-start(bf16[512,512]{1,0:T(8,128)(2,1)} %finish.6), channel_id=1, source_target_pairs={{0,3},{1,0},{2,1},{3,2},{4,5},{5,6},{6,7},{7,4},{8,11},{9,8},{10,9... | collective-permute-start | bytes 1572872 | tf_op jit(solution)/shard_map/ppermute | solution.py:299
  75.5 15.5 %collective-permute-start.9 = (bf16[512,512]{1,0:T(8,128)(2,1)}, bf16[512,512]{1,0:T(8,128)(2,1)}, u32[]{:S(2)}, u32[]{:S(2)}) collective-permute-start(bf16[512,512]{1,0:T(8,128)(2,1)} %collective-permute-done.8), channel_id=1, source_target_pairs={{0,1},{1,2},{2,3},{3,0},{4,7},{5,4},{6,5},{7,6},{8,9},{9,10},{10,1... | collective-permute-start | bytes 1572872 | tf_op jit(solution)/shard_map/ppermute | solution.py:299
  82.0 1.0 %copy-start = (bf16[512,512]{1,0:T(8,128)(2,1)S(1)}, bf16[512,512]{1,0:T(8,128)(2,1)}, u32[]{:S(2)}) copy-start(bf16[512,512]{1,0:T(8,128)(2,1)} %finish.4.n0) | copy-start | bytes 1572868
  83.1 1.6 %copy-start.1 = (bf16[512,2048]{1,0:T(8,128)(2,1)S(1)}, bf16[512,2048]{1,0:T(8,128)(2,1)}, u32[]{:S(2)}) copy-start(bf16[512,2048]{1,0:T(8,128)(2,1)} %w0.1) | copy-start | bytes 6291460

commit v3 on v2

v3 whole, which is shorter than its diff:
```python
import jax
import jax.numpy as jnp
from jax import lax
from jax.experimental import pallas as pl
from jax.experimental.pallas import tpu as pltpu
from jax.sharding import PartitionSpec as P


DH = 128
BLK = 256
F32 = jnp.float32
BF16 = jnp.bfloat16


def dot(a, b):
    return jnp.dot(a, b, preferred_element_type=F32)


def cost(flops, nbytes):
    return pl.CostEstimate(flops=int(flops), bytes_accessed=int(nbytes), transcendentals=0)


def hi_lo(state):
    high = state.astype(BF16)
    low = (state - high.astype(F32)).astype(BF16)
    return jnp.concatenate([high, low], axis=0)


def local_block(att_ref, rows, q_ref, k_ref, v_ref, pre, at):
    lower = lax.broadcasted_iota(jnp.int32, (BLK, BLK), 0) >= lax.broadcasted_iota(
        jnp.int32, (BLK, BLK), 1
    )
    for h in range(q_ref.shape[1] // DH):
        cols = slice(h * DH, (h + 1) * DH)
        q = q_ref[rows, cols]
        scores = lax.dot_general(
            q, k_ref[rows, cols], (((1,), (1,)), ((), ())), preferred_element_type=F32
        )
        scores = jnp.where(lower, scores, 0.0).astype(BF16)
        left = jnp.concatenate([scores, q, q], axis=1)
        right = jnp.concatenate([v_ref[rows, cols], pre[at, h]], axis=0)
        att_ref[rows, cols] = dot(left, right)


def qkv_kernel(
    x_hbm, w_hbm, q_hbm, k_hbm, v_hbm, pre_hbm, tot_ref, att_hbm,
    x, w, q, k, v, pre, att, x_sem, w_sem, out_sem,
):
    steps = x_sem.shape[0] // 2
    tile = x.shape[0] // steps
    width = x.shape[1]
    half = width // 2
    heads = tot_ref.shape[0]
    blocks = tile // BLK
    inside = att.shape[0] // tile

    def tokens(i, part):
        at = (pl.ds(i * tile, tile), pl.ds(part * half, half))
        return pltpu.make_async_copy(x_hbm.at[at], x.at[at], x_sem.at[2 * i + part])

    def weight(which, part):
        at = pl.ds(part * half, half)
        return pltpu.make_async_copy(
            w_hbm.at[which, at], w.at[which, at], w_sem.at[2 * which + part]
        )

    for part in range(2):
        tokens(0, part).start()
        weight(1, part).start()
    for which in (2, 0):
        for part in range(2):
            weight(which, part).start()
    for i in range(1, steps):
        for part in range(2):
            tokens(i, part).start()

    pending = []

    def put(i, source, target, which):
        copy = pltpu.make_async_copy(source, target, out_sem.at[i, which])
        copy.start()
        pending.append(copy)

    state = [jnp.zeros((DH, DH), F32)] * heads
    for i in range(steps):
        rows = pl.ds(i * tile, tile)
        if i == 0:
            total = None
            for part in range(2):
                tokens(0, part).wait()
                weight(1, part).wait()
                cut = pl.ds(part * half, half)
                product = dot(x[rows, cut], w[1, cut])
                total = product if total is None else total + product
            k[rows] = total.astype(BF16)
        else:
            for part in range(2):
                tokens(i, part).wait()
            k[rows] = dot(x[rows], w[1]).astype(BF16)
        for which, out in ((2, v), (0, q)):
            if i == 0:
                for part in range(2):
                    weight(which, part).wait()
            out[rows] = dot(x[rows], w[which]).astype(BF16)
        for b in range(i * blocks, (i + 1) * blocks):
            block = slice(b * BLK, (b + 1) * BLK)
            for h in range(heads):
                cols = slice(h * DH, (h + 1) * DH)
                pre[b, h] = hi_lo(state[h])
                state[h] = state[h] + lax.dot_general(
                    k[block, cols], v[block, cols], (((0,), (0,)), ((), ())),
                    preferred_element_type=F32,
                )
            if i < inside:
                local_block(att, block, q, k, v, pre, b)
        put(i, q.at[rows], q_hbm.at[rows], 0)
        put(i, k.at[rows], k_hbm.at[rows], 1)
        put(i, v.at[rows], v_hbm.at[rows], 2)
        at = pl.ds(i * blocks, blocks)
        put(i, pre.at[at], pre_hbm.at[at], 3)
        if i < inside:
            put(i, att.at[rows], att_hbm.at[rows], 4)
    for h in range(heads):
        tot_ref[h] = state[h]
    for copy in pending:
        copy.wait()


def project(x, w_qkv, inside, tile=512):
    tokens, width = x.shape
    feats = w_qkv.shape[2]
    heads = feats // DH
    steps = tokens // tile
    wide = (tokens, feats)
    states = (tokens // BLK, heads, 2 * DH, DH)
    anywhere = pl.BlockSpec(memory_space=pl.ANY)
    return pl.pallas_call(
        qkv_kernel,
        in_specs=[anywhere] * 2,
        out_specs=[anywhere] * 4 + [pl.BlockSpec(memory_space=pltpu.VMEM), anywhere],
        out_shape=[jax.ShapeDtypeStruct(wide, BF16)] * 3
        + [
            jax.ShapeDtypeStruct(states, BF16),
            jax.ShapeDtypeStruct((heads, DH, DH), F32),
            jax.ShapeDtypeStruct(wide, F32),
        ],
        scratch_shapes=[
            pltpu.VMEM((tokens, width), BF16),
            pltpu.VMEM((3, width, feats), BF16),
            pltpu.VMEM(wide, BF16),
            pltpu.VMEM(wide, BF16),
            pltpu.VMEM(wide, BF16),
            pltpu.VMEM(states, BF16),
            pltpu.VMEM((inside * tile, feats), F32),
            pltpu.SemaphoreType.DMA((2 * steps,)),
            pltpu.SemaphoreType.DMA((6,)),
            pltpu.SemaphoreType.DMA((steps, 5)),
        ],
        cost_estimate=cost(6 * tokens * width * feats, 2 * tokens * width + 6 * width * feats),
        name="project",
    )(x, w_qkv)


def local_kernel(q_ref, k_ref, v_ref, pre_ref, att_in, att_ref):
    for b in range(q_ref.shape[0] // BLK):
        local_block(att_ref, slice(b * BLK, (b + 1) * BLK), q_ref, k_ref, v_ref, pre_ref, b)


def local_part(q, k, v, pre, att, piece, pieces, tile=256):
    tokens, feats = q.shape
    heads = feats // DH
    blocks = tile // BLK
    count = tokens // pieces
    start = piece * count // tile
    row = pl.BlockSpec((tile, feats), lambda i: (i + start, 0))
    return pl.pallas_call(
        local_kernel,
        grid=(count // tile,),
        in_specs=[
            row, row, row,
            pl.BlockSpec((blocks, heads, 2 * DH, DH), lambda i: (i + start, 0, 0, 0)),
            pl.BlockSpec(memory_space=pl.ANY),
        ],
        out_specs=row,
        out_shape=jax.ShapeDtypeStruct((tokens, feats), F32),
        input_output_aliases={4: 0},
        cost_estimate=cost(8 * count * feats * BLK, 14 * count * feats),
        name="local_part",
    )(q, k, v, pre, att)


def norm_rows(q_ref, att_ref, pair, gain_ref, n_ref, h):
    cols = slice(h * DH, (h + 1) * DH)
    q = q_ref[:, cols]
    att = att_ref[:, cols] + dot(jnp.concatenate([q, q], axis=1), pair)
    mean_sq = jnp.mean(att * att, axis=-1, keepdims=True)
    n_ref[:, cols] = (att * lax.rsqrt(mean_sq + 1e-06) * gain_ref[:, cols]).astype(BF16)


def start_kernel(
    head, core, y, x, q_ref, att_ref, core_ref, y1_ref, y2_ref, x1_ref, x2_ref, gain_ref,
    n_ref, pair_ref,
):
    takes = (
        (core[0] == 1, core_ref),
        (lax.rem(y[0], 2) == 1, y1_ref),
        (y[0] >= 2, y2_ref),
        (lax.rem(x[0], 2) == 1, x1_ref),
        (x[0] >= 2, x2_ref),
    )
    for h in range(core_ref.shape[0]):

        @pl.when(pl.program_id(0) == 0)
        def _():
            carried = jnp.zeros((DH, DH), F32)
            for take, ref in takes:
                carried = carried + jnp.where(take, ref[h].astype(F32), 0.0)
            pair_ref[h] = hi_lo(carried)

    for h in range(core_ref.shape[0]):
        norm_rows(q_ref, att_ref, pair_ref[h], gain_ref, n_ref, h)


def finish_kernel(head, core, y, x, q_ref, att_ref, pair_ref, gain_ref, n_ref):
    for h in range(pair_ref.shape[0]):
        norm_rows(q_ref, att_ref, pair_ref[h], gain_ref, n_ref, h)


def finish(place, direction, shift, q, att, received, gain, parts, tile=256):
    tokens, feats = q.shape
    count = tokens // parts
    per = count // tile
    heads = feats // DH

    def row(i, head, core, y, x):
        to = head[0] + direction * (1 - 2 * core[0]) + shift + parts
        return (lax.rem(to, parts) * per + i, 0)

    first = len(received) > 1
    normed = jax.ShapeDtypeStruct((count, feats), BF16)
    rows = pl.BlockSpec((tile, feats), lambda i, *place: (i, 0))
    whole = lambda a: pl.BlockSpec(a.shape, lambda i, *place: (0,) * len(a.shape))
    pair = jax.ShapeDtypeStruct((heads, 2 * DH, DH), BF16)
    return pl.pallas_call(
        start_kernel if first else finish_kernel,
        grid_spec=pltpu.PrefetchScalarGridSpec(
            num_scalar_prefetch=4,
            grid=(per,),
            in_specs=[pl.BlockSpec((tile, feats), row), pl.BlockSpec((tile, feats), row)]
            + [whole(a) for a in received]
            + [whole(gain)],
            out_specs=[rows, whole(pair)] if first else rows,
        ),
        out_shape=[normed, pair] if first else normed,
        cost_estimate=cost(2 * count * feats * DH * 2, count * feats * 8),
        name="finish",
    )(*place, q, att, *received, gain)


def first_kernel(n0, na, w0, wa, *rest):
    acc_ref = rest[-1]
    acc_ref[...] = dot(n0[...], w0[...]) + dot(na[...], wa[...])


def last_kernel(
    core, acc_hbm, nb_hbm, nf_hbm, wb_hbm, mine_hbm, other_hbm, out_hbm,
    acc, nb, nf, wb, mine, other, out, n_sem, w_sem, out_sem,
):
    tiles = w_sem.shape[0]
    tile = out.shape[1] // tiles
    half = mine.shape[0]
    rows = [pltpu.make_async_copy(nb_hbm, nb, n_sem.at[0]), pltpu.make_async_copy(nf_hbm, nf, n_sem.at[1])]
    columns = [slice(j * tile, (j + 1) * tile) for j in range(tiles)]
    weights = [
        [
            pltpu.make_async_copy(source.at[:, cut], target.at[:, cut], w_sem.at[j, which])
            for which, (source, target) in enumerate(
                ((wb_hbm, wb), (mine_hbm, mine), (other_hbm, other), (acc_hbm, acc))
            )
        ]
        for j, cut in enumerate(columns)
    ]
    for which in range(2):
        rows[which].start()
        for copy in weights[0][which :: 2]:
            copy.start()
    for copies in weights[1:]:
        for copy in copies:
            copy.start()
    own = pl.multiple_of(core[0] * half, half)
    partner = pl.multiple_of((1 - core[0]) * half, half)
    pending = []
    for j, cut in enumerate(columns):
        if j == 0:
            rows[0].wait()
        weights[j][0].wait()
        total = dot(nb[...], wb[:, cut])
        if j == 0:
            rows[1].wait()
        weights[j][1].wait()
        total += dot(nf[:, pl.ds(own, half)], mine[:, cut])
        weights[j][2].wait()
        total += dot(nf[:, pl.ds(partner, half)], other[:, cut])
        weights[j][3].wait()
        out[:, cut] = (total + acc[:, cut]).astype(BF16)
        copy = pltpu.make_async_copy(out.at[:, cut], out_hbm.at[:, cut], out_sem.at[j])
        copy.start()
        pending.append(copy)
    for copy in pending:
        copy.wait()


def mix_first(normed, weights, later, tile=512):
    rows, feats = normed[0].shape
    width = weights[0].shape[1]
    return pl.pallas_call(
        first_kernel,
        grid=(width // tile,),
        in_specs=[pl.BlockSpec(a.shape, lambda i: (0, 0)) for a in normed]
        + [pl.BlockSpec((a.shape[0], tile), lambda i: (0, i)) for a in weights]
        + [pl.BlockSpec(memory_space=pl.ANY)] * len(later),
        out_specs=pl.BlockSpec((rows, tile), lambda i: (0, i)),
        out_shape=jax.ShapeDtypeStruct((rows, width), F32),
        cost_estimate=cost(4 * rows * feats * width, 8 * rows * width),
        compiler_params=pltpu.CompilerParams(vmem_limit_bytes=24 << 20),
        name="mix_first",
    )(*normed, *weights, *later)


def mix_last(core, acc, normed, weights, tiles=2):
    rows, feats = normed[0].shape
    width = acc.shape[1]
    anywhere = pl.BlockSpec(memory_space=pl.ANY)
    operands = [acc, *normed, *weights]
    return pl.pallas_call(
        last_kernel,
        grid_spec=pltpu.PrefetchScalarGridSpec(
            num_scalar_prefetch=1,
            grid=(1,),
            in_specs=[anywhere] * len(operands),
            out_specs=anywhere,
            scratch_shapes=[pltpu.VMEM(a.shape, a.dtype) for a in operands]
            + [
                pltpu.VMEM((rows, width), BF16),
                pltpu.SemaphoreType.DMA((2,)),
                pltpu.SemaphoreType.DMA((tiles, 4)),
                pltpu.SemaphoreType.DMA((tiles,)),
            ],
        ),
        out_shape=jax.ShapeDtypeStruct((rows, width), BF16),
        cost_estimate=cost(4 * rows * feats * width, 8 * rows * width),
        compiler_params=pltpu.CompilerParams(vmem_limit_bytes=24 << 20),
        name="mix_last",
    )(core, *operands)


def pair_up(size, stride, total, first):
    pairs = []
    for i in range(total):
        at = (i // stride) % size
        to = at ^ 1 if first else (at + (1 if at % 2 else -1)) % size
        pairs.append((i, i + (to - at) * stride))
    return pairs


def pair_rounds(value, stride, total):
    value = value.astype(BF16)
    other = lax.ppermute(value, "seq", pair_up(4, stride, total, True))
    pair = (value.astype(F32) + other.astype(F32)).astype(BF16)
    far = lax.ppermute(pair, "seq", pair_up(4, stride, total, False))
    return other, far, pair.astype(F32) + far.astype(F32)


def layer(inputs, w_qkv, norm_gain, w_out):
    parts = lax.axis_size("head")
    total = lax.axis_size("seq")
    seq = lax.axis_index("seq")
    core = lax.rem(seq, 2)
    y = lax.rem(seq // 2, 4)
    x = seq // 8
    head = lax.axis_index("head")
    core_id = core.astype(jnp.int32).reshape(1)
    place = [a.astype(jnp.int32).reshape(1) for a in (head, core, y, x)]

    def along(direction):
        pairs = []
        for i in range(total):
            shift = direction * (1 - 2 * (i % 2))
            for h in range(parts):
                pairs.append((i * parts + h, i * parts + (h + shift) % parts))
        return pairs

    partner = [(i, i ^ 1) for i in range(total)]

    def swap(a):
        return lax.ppermute(a, "seq", partner)

    def send(a, direction):
        return lax.ppermute(a, ("seq", "head"), along(direction))

    near = send(w_out, 1)
    rows = w_out.shape[0] // 2
    far = lax.dynamic_slice_in_dim(near, core * rows, rows, 0)
    far = send(far, 1)
    near_other = swap(near)
    far_other = swap(far)

    q, k, v, pre, tot, att = project(inputs, w_qkv, 1)
    other = swap(tot)
    for piece in range(1, 4):
        att = local_part(q, k, v, pre, att, piece, 4)
    y1, y2, row = pair_rounds(tot + other, 2, total)
    x1, x2, _ = pair_rounds(row, 8, total)
    received = (other, y1, y2, x1, x2)

    gain = norm_gain.reshape(1, -1)
    nf, pair = finish(place, 0, 2, q, att, received, gain, parts)
    nf = send(nf, 1)
    na = send(finish(place, 1, 0, q, att, (pair,), gain, parts), 1)
    nb = send(finish(place, -1, 0, q, att, (pair,), gain, parts), -1)
    nf = send(nf, 1)
    n0 = finish(place, 0, 0, q, att, (pair,), gain, parts)
    later = [near_other, far, far_other]
    acc = mix_first([n0, na], [w_out, near], later)
    return mix_last(core_id, acc, [nb, nf], later)


def solution(mesh):
    return jax.shard_map(
        layer,
        mesh=mesh,
        in_specs=(P("seq", None), P(None, None, "head"), P("head"), P("head", None)),
        out_specs=P(("seq", "head"), None),
        check_vma=False,
    )
```

time: 97.5 us -> 106 us (1.087)
  the two profiles are of different devices: /device:TPU:1 before, /device:TPU:0 now
where the time goes in v3:
time: 106 us
  Pallas kernels  53.5 us (50%)
  waiting for transfers between devices  25.7 us (24%)
  starting transfers between devices  17.1 us (16%)
  local copies, waits for them, and re-layouts  6.54 us (6%)
  other arithmetic  2.43 us (2%)
    pallas_call x1, Pallas kernels, project(): pl.pallas_call(qkv_kernel, in_specs=[anywhere] * 2, out_specs=[anywhere]...  20.8 us
    ppermute x6, waiting for transfers between devices, send(): return lax.ppermute(a, ('seq', 'head'), along(direction))  14.3 us
    pallas_call x3, Pallas kernels, local_part(): pl.pallas_call(local_kernel, grid=(count // tile,), in_specs=[row, row, r...  11.2 us
    pallas_call x4, Pallas kernels, finish(): pl.pallas_call(start_kernel if first else finish_kernel, grid_spec=pltpu....  11.2 us
    ppermute x2, waiting for transfers between devices, pair_rounds(): other = lax.ppermute(value, 'seq', pair_up(4, stride, total, True))  7.33 us
    ppermute x2, starting transfers between devices, pair_rounds(): far = lax.ppermute(pair, 'seq', pair_up(4, stride, total, False))  6.03 us
    pallas_call x1, Pallas kernels, mix_last(): pl.pallas_call(last_kernel, grid_spec=pltpu.PrefetchScalarGridSpec(num_sc...  5.86 us
    unnamed x16, local copies, waits for them, and re-layouts  5.31 us
  transfers between devices with their start and end apart: 13, of which 6 were waited for; matrix products, arithmetic and copies ran while one was open for 3% of the time, Pallas kernels for 45%

profile of v3, /device:TPU:0, one launch (start us, length us, event | category | flops | bytes accessed | tf_op | source)
XLA Modules:
  0.0 105.6 jit_solution(18134070269015945083)
XLA Ops:
  0.0 2.0 %collective-permute-start.6 = (bf16[512,2048]{1,0:T(8,128)(2,1)}, bf16[512,2048]{1,0:T(8,128)(2,1)S(1)}, u32[]{:S(2)}, u32[]{:S(2)}) collective-permute-start(bf16[512,2048]{1,0:T(8,128)(2,1)} %w0.1), channel_id=1, source_target_pairs={{0,1},{1,2},{2,3},{3,0},{4,7},{5,4},{6,5},{7,6},{8,9},{9,10},{10,1... | collective-permute-start | bytes 6291464 | tf_op jit(solution)/shard_map/ppermute | solution.py:399
  2.0 20.8 %project.1 = (bf16[2048,512]{1,0:T(8,128)(2,1)}, bf16[2048,512]{1,0:T(8,128)(2,1)}, bf16[2048,512]{1,0:T(8,128)(2,1)}, bf16[8,4,256,128]{3,2,1,0:T(8,128)(2,1)},...) custom-call(bf16[2048,2048]{1,0:T(8,128)(2,1)} %x_hbm.1, bf16[3,2048,512]{2,1,0:T(8,128)(2,1)} %w_hbm.1), custom_call_target="tpu_custom_call" | custom-call | flops 12884901888 | bytes 14680064 | tf_op jit(solution)/shard_map/project/pallas_call | solution.py:137
  22.9 1.8 %collective-permute-start = (f32[4,128,128]{2,1,0:T(8,128)}, f32[4,128,128]{2,1,0:T(8,128)S(1)}, u32[]{:S(2)}, u32[]{:S(2)}) collective-permute-start(f32[4,128,128]{2,1,0:T(8,128)} %get-tuple-element.18), channel_id=1, source_target_pairs={{0,4},{4,0},{8,12},{12,8},{16,20},{20,16},{24,28},{28,24},{32,36},... | collective-permute-start | bytes 786440 | tf_op jit(solution)/shard_map/ppermute | solution.py:396
  24.6 3.7 %collective-permute-done.6.wa = bf16[512,2048]{1,0:T(8,128)(2,1)S(1)} collective-permute-done((bf16[512,2048]{1,0:T(8,128)(2,1)}, bf16[512,2048]{1,0:T(8,128)(2,1)S(1)}, u32[]{:S(2)}, u32[]{:S(2)}) %collective-permute-start.6) | collective-permute-done | bytes 2097184 | tf_op jit(solution)/shard_map/ppermute | solution.py:399
  32.7 3.5 %collective-permute-done.1.y1_ref = bf16[4,128,128]{2,1,0:T(8,128)(2,1)S(1)} collective-permute-done((bf16[4,128,128]{2,1,0:T(8,128)(2,1)S(1)}, bf16[4,128,128]{2,1,0:T(8,128)(2,1)S(1)}, u32[]{:S(2)}, u32[]{:S(2)}) %collective-permute-start.1) | collective-permute-done | bytes 131104 | tf_op jit(solution)/shard_map/ppermute | solution.py:368
  36.2 3.3 %collective-permute-start.2 = (bf16[4,128,128]{2,1,0:T(8,128)(2,1)S(1)}, bf16[4,128,128]{2,1,0:T(8,128)(2,1)S(1)}, u32[]{:S(2)}, u32[]{:S(2)}) collective-permute-start(bf16[4,128,128]{2,1,0:T(8,128)(2,1)S(1)} %add_convert_fusion.2), channel_id=1, source_target_pairs={{0,24},{4,28},{8,16},{12,20},{16,8},{20,12},{24,0},{28,4},{32,56},... | collective-permute-start | bytes 393224 | tf_op jit(solution)/shard_map/ppermute | solution.py:370
  39.5 4.1 %collective-permute-done.2.y2_ref = bf16[4,128,128]{2,1,0:T(8,128)(2,1)S(1)} collective-permute-done((bf16[4,128,128]{2,1,0:T(8,128)(2,1)S(1)}, bf16[4,128,128]{2,1,0:T(8,128)(2,1)S(1)}, u32[]{:S(2)}, u32[]{:S(2)}) %collective-permute-start.2) | collective-permute-done | bytes 131104 | tf_op jit(solution)/shard_map/ppermute | solution.py:370
  46.4 3.9 %collective-permute-done.3.x1_ref = bf16[4,128,128]{2,1,0:T(8,128)(2,1)} collective-permute-done((bf16[4,128,128]{2,1,0:T(8,128)(2,1)}, bf16[4,128,128]{2,1,0:T(8,128)(2,1)}, u32[]{:S(2)}, u32[]{:S(2)}) %collective-permute-start.3) | collective-permute-done | bytes 131104 | tf_op jit(solution)/shard_map/ppermute | solution.py:368
  50.3 1.7 %add_convert_fusion = bf16[4,128,128]{2,1,0:T(8,128)(2,1)} fusion(bf16[4,128,128]{2,1,0:T(8,128)(2,1)} %collective-permute-done.3.x1_ref, bf16[4,128,128]{2,1,0:T(8,128)(2,1)} %add_convert_fusion.1), kind=kLoop, calls=%fused_computation | loop fusion | flops 262144 | bytes 393216 | tf_op jit(solution)/shard_map/convert_element_type | solution.py:369
  51.9 2.8 %collective-permute-start.4 = (bf16[4,128,128]{2,1,0:T(8,128)(2,1)}, bf16[4,128,128]{2,1,0:T(8,128)(2,1)}, u32[]{:S(2)}, u32[]{:S(2)}) collective-permute-start(bf16[4,128,128]{2,1,0:T(8,128)(2,1)} %add_convert_fusion), channel_id=1, source_target_pairs={{0,96},{4,100},{8,104},{12,108},{16,112},{20,116},{24,120},{28,124... | collective-permute-start | bytes 393224 | tf_op jit(solution)/shard_map/ppermute | solution.py:370
  54.7 3.7 %local_part.3.att_in = f32[2048,512]{1,0:T(8,128)} custom-call(bf16[2048,512]{1,0:T(8,128)(2,1)} %get-tuple-element.13.q_ref, bf16[2048,512]{1,0:T(8,128)(2,1)} %get-tuple-element.14.k_ref, bf16[2048,512]{1,0:T(8,128)(2,1)} %get-tuple-element.15.v_ref, bf16[8,4,256,128]{3,2,1,0:T(8,128)(2,1)} %get-tuple-element.16.pre_ref, ...), custom_call_target="tpu_custom_call", output_to_operand_aliasing={{}: (4, {})} | custom-call | flops 536870912 | bytes 3670016 | tf_op jit(solution)/shard_map/local_part/pallas_call | solution.py:176
  58.4 3.8 %local_part.4.att_in = f32[2048,512]{1,0:T(8,128)} custom-call(bf16[2048,512]{1,0:T(8,128)(2,1)} %get-tuple-element.13.q_ref, bf16[2048,512]{1,0:T(8,128)(2,1)} %get-tuple-element.14.k_ref, bf16[2048,512]{1,0:T(8,128)(2,1)} %get-tuple-element.15.v_ref, bf16[8,4,256,128]{3,2,1,0:T(8,128)(2,1)} %get-tuple-element.16.pre_ref, ...), custom_call_target="tpu_custom_call", output_to_operand_aliasing={{}: (4, {})} | custom-call | flops 536870912 | bytes 3670016 | tf_op jit(solution)/shard_map/local_part/pallas_call | solution.py:176
  62.2 3.7 %local_part.5.att_ref = f32[2048,512]{1,0:T(8,128)} custom-call(bf16[2048,512]{1,0:T(8,128)(2,1)} %get-tuple-element.13.q_ref, bf16[2048,512]{1,0:T(8,128)(2,1)} %get-tuple-element.14.k_ref, bf16[2048,512]{1,0:T(8,128)(2,1)} %get-tuple-element.15.v_ref, bf16[8,4,256,128]{3,2,1,0:T(8,128)(2,1)} %get-tuple-element.16.pre_ref, ...), custom_call_target="tpu_custom_call", output_to_operand_aliasing={{}: (4, {})} | custom-call | flops 536870912 | bytes 3670016 | tf_op jit(solution)/shard_map/local_part/pallas_call | solution.py:176
  65.9 3.0 %finish.4 = (bf16[512,512]{1,0:T(8,128)(2,1)}, bf16[4,256,128]{2,1,0:T(8,128)(2,1)}) custom-call(s32[1]{0:T(128)} %bitcast.1.head, s32[1]{0:T(128)} %bitcast.core, s32[1]{0:T(128)} %bitcast.2.y, s32[1]{0:T(128)} %bitcast.3.x, bf16[2048,512]{1,0:T(8,128)(2,1)} %get-tuple-element.13.q_ref, f32[2048,512]{1,0:T(8,128)} %local_part.5.att_ref, ...), custom_call_target="tpu_custom_call" | custom-call | flops 134217728 | bytes 2097152 | tf_op jit(solution)/shard_map/finish/pallas_call | solution.py:244
  69.0 2.7 %finish.6 = bf16[512,512]{1,0:T(8,128)(2,1)} custom-call(s32[1]{0:T(128)} %bitcast.1.head, s32[1]{0:T(128)} %bitcast.core, s32[1]{0:T(128)} %bitcast.2.y, s32[1]{0:T(128)} %bitcast.3.x, bf16[2048,512]{1,0:T(8,128)(2,1)} %get-tuple-element.13.q_ref, f32[2048,512]{1,0:T(8,128)} %local_part.5.att_ref, bf16[4,256,128]{2,1,0:T(8,128)(2,1)} %get-tuple-element.19.pair_ref, ...), custom_call_target="tpu_custom_call" | custom-call | flops 134217728 | bytes 2097152 | tf_op jit(solution)/shard_map/finish/pallas_call | solution.py:244
  72.7 2.7 %finish.7 = bf16[512,512]{1,0:T(8,128)(2,1)} custom-call(s32[1]{0:T(128)} %bitcast.1.head, s32[1]{0:T(128)} %bitcast.core, s32[1]{0:T(128)} %bitcast.2.y, s32[1]{0:T(128)} %bitcast.3.x, bf16[2048,512]{1,0:T(8,128)(2,1)} %get-tuple-element.13.q_ref, f32[2048,512]{1,0:T(8,128)} %local_part.5.att_ref, bf16[4,256,128]{2,1,0:T(8,128)(2,1)} %get-tuple-element.19.pair_ref, ...), custom_call_target="tpu_custom_call" | custom-call | flops 134217728 | bytes 2097152 | tf_op jit(solution)/shard_map/finish/pallas_call | solution.py:244
  75.4 2.3 %collective-permute-start.10 = (bf16[512,512]{1,0:T(8,128)(2,1)}, bf16[512,512]{1,0:T(8,128)(2,1)}, u32[]{:S(2)}, u32[]{:S(2)}) collective-permute-start(bf16[512,512]{1,0:T(8,128)(2,1)} %finish.7), channel_id=1, source_target_pairs={{0,3},{1,0},{2,1},{3,2},{4,5},{5,6},{6,7},{7,4},{8,11},{9,8},{10,9... | collective-permute-start | bytes 1572872 | tf_op jit(solution)/shard_map/ppermute | solution.py:399
  77.7 4.6 %collective-permute-done.11 = bf16[512,512]{1,0:T(8,128)(2,1)} collective-permute-done((bf16[512,512]{1,0:T(8,128)(2,1)}, bf16[512,512]{1,0:T(8,128)(2,1)}, u32[]{:S(2)}, u32[]{:S(2)}) %collective-permute-start.11) | collective-permute-done | bytes 524320 | tf_op jit(solution)/shard_map/ppermute | solution.py:399
  82.3 2.7 %finish.5.n0 = bf16[512,512]{1,0:T(8,128)(2,1)} custom-call(s32[1]{0:T(128)} %bitcast.1.head, s32[1]{0:T(128)} %bitcast.core, s32[1]{0:T(128)} %bitcast.2.y, s32[1]{0:T(128)} %bitcast.3.x, bf16[2048,512]{1,0:T(8,128)(2,1)} %get-tuple-element.13.q_ref, f32[2048,512]{1,0:T(8,128)} %local_part.5.att_ref, bf16[4,256,128]{2,1,0:T(8,128)(2,1)} %get-tuple-element.19.pair_ref, ...), custom_call_target="tpu_custom_call" | custom-call | flops 134217728 | bytes 2097152 | tf_op jit(solution)/shard_map/finish/pallas_call | solution.py:244
  85.0 5.9 %collective-permute-done.5.na = bf16[512,512]{1,0:T(8,128)(2,1)} collective-permute-done((bf16[512,512]{1,0:T(8,128)(2,1)}, bf16[512,512]{1,0:T(8,128)(2,1)}, u32[]{:S(2)}, u32[]{:S(2)}) %collective-permute-start.5) | collective-permute-done | bytes 524320 | tf_op jit(solution)/shard_map/ppermute | solution.py:399
  90.9 1.6 %copy-done.1 = bf16[512,2048]{1,0:T(8,128)(2,1)S(1)} copy-done((bf16[512,2048]{1,0:T(8,128)(2,1)S(1)}, bf16[512,2048]{1,0:T(8,128)(2,1)}, u32[]{:S(2)}) %copy-start.1) | copy-done | bytes 2097176
  92.5 1.6 %copy-done.2 = bf16[512,2048]{1,0:T(8,128)(2,1)S(1)} copy-done((bf16[512,2048]{1,0:T(8,128)(2,1)S(1)}, bf16[512,2048]{1,0:T(8,128)(2,1)}, u32[]{:S(2)}) %copy-start.2) | copy-done | bytes 2097176
  95.2 4.4 %mix_first.1.acc_hbm = f32[512,2048]{1,0:T(8,128)S(1)} custom-call(bf16[512,512]{1,0:T(8,128)(2,1)S(1)} %copy-done.3, bf16[512,512]{1,0:T(8,128)(2,1)} %collective-permute-done.5.na, bf16[512,2048]{1,0:T(8,128)(2,1)S(1)} %copy-done.2, bf16[512,2048]{1,0:T(8,128)(2,1)S(1)} %copy-done.1, bf16[512,2048]{1,0:T(8,128)(2,1)S(1)} %collective-permute-done.7.rest_0_.wb_hbm, ...), custom_call_target="tpu_custom_call" | custom-call | flops 2147483648 | bytes 8388608 | tf_op jit(solution)/shard_map/mix_first/pallas_call | solution.py:316
  99.6 5.9 %mix_last.1 = bf16[512,2048]{1,0:T(8,128)(2,1)} custom-call(s32[1]{0:T(128)} %bitcast.core, f32[512,2048]{1,0:T(8,128)S(1)} %mix_first.1.acc_hbm, bf16[512,512]{1,0:T(8,128)(2,1)} %collective-permute-done.10.nb_hbm, bf16[512,512]{1,0:T(8,128)(2,1)} %collective-permute-done.12.nf_hbm, bf16[512,2048]{1,0:T(8,128)(2,1)S(1)} %collective-permute-done.7.rest_0_.wb_hbm, ...), custom_call_target="tpu_custom_call" | custom-call | flops 2147483648 | bytes 8388608 | tf_op jit(solution)/shard_map/mix_last/pallas_call | solution.py:335
  (33 shorter events, 9.2 us)
Async XLA Ops:
  0.0 28.4 %collective-permute-start.6 = (bf16[512,2048]{1,0:T(8,128)(2,1)}, bf16[512,2048]{1,0:T(8,128)(2,1)S(1)}, u32[]{:S(2)}, u32[]{:S(2)}) collective-permute-start(bf16[512,2048]{1,0:T(8,128)(2,1)} %w0.1), channel_id=1, source_target_pairs={{0,1},{1,2},{2,3},{3,0},{4,7},{5,4},{6,5},{7,6},{8,9},{9,10},{10,1... | collective-permute-start | bytes 6291464 | tf_op jit(solution)/shard_map/ppermute | solution.py:399
  22.9 6.7 %collective-permute-start = (f32[4,128,128]{2,1,0:T(8,128)}, f32[4,128,128]{2,1,0:T(8,128)S(1)}, u32[]{:S(2)}, u32[]{:S(2)}) collective-permute-start(f32[4,128,128]{2,1,0:T(8,128)} %get-tuple-element.18), channel_id=1, source_target_pairs={{0,4},{4,0},{8,12},{12,8},{16,20},{20,16},{24,28},{28,24},{32,36},... | collective-permute-start | bytes 786440 | tf_op jit(solution)/shard_map/ppermute | solution.py:396
  24.6 5.0 %copy-start.7 = (f32[4,128,128]{2,1,0:T(8,128)S(1)}, f32[4,128,128]{2,1,0:T(8,128)}, u32[]{:S(2)}) copy-start(f32[4,128,128]{2,1,0:T(8,128)} %get-tuple-element.18) | copy-start | bytes 786436
  28.4 1.7 %copy-start = (bf16[512,2048]{1,0:T(8,128)(2,1)}, bf16[512,2048]{1,0:T(8,128)(2,1)S(1)}, u32[]{:S(2)}) copy-start(bf16[512,2048]{1,0:T(8,128)(2,1)S(1)} %collective-permute-done.6.wa) | copy-start | bytes 6291460
  29.6 16.8 %collective-permute-start.8 = (bf16[256,2048]{1,0:T(8,128)(2,1)}, bf16[256,2048]{1,0:T(8,128)(2,1)S(1)}, u32[]{:S(2)}, u32[]{:S(2)}) collective-permute-start(bf16[256,2048]{1,0:T(8,128)(2,1)} %constant_dynamic-slice_fusion), channel_id=1, source_target_pairs={{0,1},{1,2},{2,3},{3,0},{4,7},{5,4},{6,5},{7,6},{8,9},{9,10},{10,1... | collective-permute-start | bytes 3145736 | tf_op jit(solution)/shard_map/ppermute | solution.py:399
  29.6 28.8 %copy-start.4 = (f32[4,128,128]{2,1,0:T(8,128)}, f32[4,128,128]{2,1,0:T(8,128)S(1)}, u32[]{:S(2)}) copy-start(f32[4,128,128]{2,1,0:T(8,128)S(1)} %collective-permute-done.core_ref) | copy-start | bytes 786436
  30.1 6.0 %collective-permute-start.1 = (bf16[4,128,128]{2,1,0:T(8,128)(2,1)S(1)}, bf16[4,128,128]{2,1,0:T(8,128)(2,1)S(1)}, u32[]{:S(2)}, u32[]{:S(2)}) collective-permute-start(bf16[4,128,128]{2,1,0:T(8,128)(2,1)S(1)} %add_convert_fusion.3), channel_id=1, source_target_pairs={{0,8},{4,12},{8,0},{12,4},{16,24},{20,28},{24,16},{28,20},{32,40},... | collective-permute-start | bytes 393224 | tf_op jit(solution)/shard_map/ppermute | solution.py:368
  31.7 59.3 %collective-permute-start.7 = (bf16[512,2048]{1,0:T(8,128)(2,1)}, bf16[512,2048]{1,0:T(8,128)(2,1)S(1)}, u32[]{:S(2)}, u32[]{:S(2)}) collective-permute-start(bf16[512,2048]{1,0:T(8,128)(2,1)} %copy-done), channel_id=1, source_target_pairs={{0,4},{4,0},{8,12},{12,8},{16,20},{20,16},{24,28},{28,24},{32,36},... | collective-permute-start | bytes 6291464 | tf_op jit(solution)/shard_map/ppermute | solution.py:396
  36.1 22.3 %copy-start.5 = (bf16[4,128,128]{2,1,0:T(8,128)(2,1)}, bf16[4,128,128]{2,1,0:T(8,128)(2,1)S(1)}, u32[]{:S(2)}) copy-start(bf16[4,128,128]{2,1,0:T(8,128)(2,1)S(1)} %collective-permute-done.1.y1_ref) | copy-start | bytes 393220
  36.2 7.4 %collective-permute-start.2 = (bf16[4,128,128]{2,1,0:T(8,128)(2,1)S(1)}, bf16[4,128,128]{2,1,0:T(8,128)(2,1)S(1)}, u32[]{:S(2)}, u32[]{:S(2)}) collective-permute-start(bf16[4,128,128]{2,1,0:T(8,128)(2,1)S(1)} %add_convert_fusion.2), channel_id=1, source_target_pairs={{0,24},{4,28},{8,16},{12,20},{16,8},{20,12},{24,0},{28,4},{32,56},... | collective-permute-start | bytes 393224 | tf_op jit(solution)/shard_map/ppermute | solution.py:370
  43.6 0.7 copy-start.6
  44.9 5.4 %collective-permute-start.3 = (bf16[4,128,128]{2,1,0:T(8,128)(2,1)}, bf16[4,128,128]{2,1,0:T(8,128)(2,1)}, u32[]{:S(2)}, u32[]{:S(2)}) collective-permute-start(bf16[4,128,128]{2,1,0:T(8,128)(2,1)} %add_convert_fusion.1), channel_id=1, source_target_pairs={{0,32},{4,36},{8,40},{12,44},{16,48},{20,52},{24,56},{28,60},{32,0... | collective-permute-start | bytes 393224 | tf_op jit(solution)/shard_map/ppermute | solution.py:368
  46.4 44.5 %collective-permute-start.9 = (bf16[256,2048]{1,0:T(8,128)(2,1)S(1)}, bf16[256,2048]{1,0:T(8,128)(2,1)}, u32[]{:S(2)}, u32[]{:S(2)}) collective-permute-start(bf16[256,2048]{1,0:T(8,128)(2,1)S(1)} %collective-permute-done.8.rest_1_.mine_hbm), channel_id=1, source_target_pairs={{0,4},{4,0},{8,12},{12,8},{16,20},{20,16},{24,28},{28,24},{32,36},... | collective-permute-start | bytes 3145736 | tf_op jit(solution)/shard_map/ppermute | solution.py:396
  51.9 14.0 %collective-permute-start.4 = (bf16[4,128,128]{2,1,0:T(8,128)(2,1)}, bf16[4,128,128]{2,1,0:T(8,128)(2,1)}, u32[]{:S(2)}, u32[]{:S(2)}) collective-permute-start(bf16[4,128,128]{2,1,0:T(8,128)(2,1)} %add_convert_fusion), channel_id=1, source_target_pairs={{0,96},{4,100},{8,104},{12,108},{16,112},{20,116},{24,120},{28,124... | collective-permute-start | bytes 393224 | tf_op jit(solution)/shard_map/ppermute | solution.py:370
  69.0 13.3 %collective-permute-start.11 = (bf16[512,512]{1,0:T(8,128)(2,1)}, bf16[512,512]{1,0:T(8,128)(2,1)}, u32[]{:S(2)}, u32[]{:S(2)}) collective-permute-start(bf16[512,512]{1,0:T(8,128)(2,1)} %get-tuple-element.20), channel_id=1, source_target_pairs={{0,1},{1,2},{2,3},{3,0},{4,7},{5,4},{6,5},{7,6},{8,9},{9,10},{10,1... | collective-permute-start | bytes 1572872 | tf_op jit(solution)/shard_map/ppermute | solution.py:399
  71.7 19.2 %collective-permute-start.5 = (bf16[512,512]{1,0:T(8,128)(2,1)}, bf16[512,512]{1,0:T(8,128)(2,1)}, u32[]{:S(2)}, u32[]{:S(2)}) collective-permute-start(bf16[512,512]{1,0:T(8,128)(2,1)} %finish.6), channel_id=1, source_target_pairs={{0,1},{1,2},{2,3},{3,0},{4,7},{5,4},{6,5},{7,6},{8,9},{9,10},{10,1... | collective-permute-start | bytes 1572872 | tf_op jit(solution)/shard_map/ppermute | solution.py:399
  75.4 24.2 %collective-permute-start.10 = (bf16[512,512]{1,0:T(8,128)(2,1)}, bf16[512,512]{1,0:T(8,128)(2,1)}, u32[]{:S(2)}, u32[]{:S(2)}) collective-permute-start(bf16[512,512]{1,0:T(8,128)(2,1)} %finish.7), channel_id=1, source_target_pairs={{0,3},{1,0},{2,1},{3,2},{4,5},{5,6},{6,7},{7,4},{8,11},{9,8},{10,9... | collective-permute-start | bytes 1572872 | tf_op jit(solution)/shard_map/ppermute | solution.py:399
  82.3 17.3 %collective-permute-start.12 = (bf16[512,512]{1,0:T(8,128)(2,1)}, bf16[512,512]{1,0:T(8,128)(2,1)}, u32[]{:S(2)}, u32[]{:S(2)}) collective-permute-start(bf16[512,512]{1,0:T(8,128)(2,1)} %collective-permute-done.11), channel_id=1, source_target_pairs={{0,1},{1,2},{2,3},{3,0},{4,7},{5,4},{6,5},{7,6},{8,9},{9,10},{10,1... | collective-permute-start | bytes 1572872 | tf_op jit(solution)/shard_map/ppermute | solution.py:399
  90.9 1.6 %copy-start.1 = (bf16[512,2048]{1,0:T(8,128)(2,1)S(1)}, bf16[512,2048]{1,0:T(8,128)(2,1)}, u32[]{:S(2)}) copy-start(bf16[512,2048]{1,0:T(8,128)(2,1)} %copy-done) | copy-start | bytes 6291460
  92.5 1.6 %copy-start.2 = (bf16[512,2048]{1,0:T(8,128)(2,1)S(1)}, bf16[512,2048]{1,0:T(8,128)(2,1)}, u32[]{:S(2)}) copy-start(bf16[512,2048]{1,0:T(8,128)(2,1)} %w0.1) | copy-start | bytes 6291460
  94.1 1.0 copy-start.3

commit v4 on v3

--- a/solution.py
+++ b/solution.py
@@ -37,9 +37,9 @@
             q, k_ref[rows, cols], (((1,), (1,)), ((), ())), preferred_element_type=F32
         )
         scores = jnp.where(lower, scores, 0.0).astype(BF16)
-        left = jnp.concatenate([scores, q, q], axis=1)
-        right = jnp.concatenate([v_ref[rows, cols], pre[at, h]], axis=0)
-        att_ref[rows, cols] = dot(left, right)
+        att_ref[rows, cols] = dot(scores, v_ref[rows, cols]) + dot(
+            jnp.concatenate([q, q], axis=1), pre[at, h]
+        )
 
 
 def qkv_kernel(
@@ -414,9 +414,9 @@
     received = (other, y1, y2, x1, x2)
 
     gain = norm_gain.reshape(1, -1)
-    nf, pair = finish(place, 0, 2, q, att, received, gain, parts)
-    nf = send(nf, 1)
-    na = send(finish(place, 1, 0, q, att, (pair,), gain, parts), 1)
+    na, pair = finish(place, 1, 0, q, att, received, gain, parts)
+    na = send(na, 1)
+    nf = send(finish(place, 0, 2, q, att, (pair,), gain, parts), 1)
     nb = send(finish(place, -1, 0, q, att, (pair,), gain, parts), -1)
     nf = send(nf, 1)
     n0 = finish(place, 0, 0, q, att, (pair,), gain, parts)

time: 106 us -> 108 us (1.019)
  waiting for transfers between devices: 25.7 us -> 28.9 us
  Pallas kernels: 53.5 us -> 52 us
    ppermute x6, waiting for transfers between devices: 14.3 us -> 17.5 us  [send(): return lax.ppermute(a, ('seq', 'head'), along(direction))]
  transfers between devices with their start and end apart: 13 -> 13, of which waited for: 6 -> 6; matrix products, arithmetic and copies ran while one was open for 3% -> 3% of each run, Pallas kernels for 45% -> 43%
where the time goes in v4:
time: 108 us; the launch traced here: 107 us
  Pallas kernels  52 us (48%)
  waiting for transfers between devices  28.9 us (27%)
  starting transfers between devices  17 us (16%)
  local copies, waits for them, and re-layouts  6.54 us (6%)
  other arithmetic  2.43 us (2%)
    pallas_call x1, Pallas kernels, project(): pl.pallas_call(qkv_kernel, in_specs=[anywhere] * 2, out_specs=[anywhere]...  20.4 us
    ppermute x6, waiting for transfers between devices, send(): return lax.ppermute(a, ('seq', 'head'), along(direction))  17.5 us
    pallas_call x4, Pallas kernels, finish(): pl.pallas_call(start_kernel if first else finish_kernel, grid_spec=pltpu....  11.2 us
    pallas_call x3, Pallas kernels, local_part(): pl.pallas_call(local_kernel, grid=(count // tile,), in_specs=[row, row, r...  10.2 us
    ppermute x2, waiting for transfers between devices, pair_rounds(): other = lax.ppermute(value, 'seq', pair_up(4, stride, total, True))  7.33 us
    ppermute x2, starting transfers between devices, pair_rounds(): far = lax.ppermute(pair, 'seq', pair_up(4, stride, total, False))  5.85 us
    pallas_call x1, Pallas kernels, mix_last(): pl.pallas_call(last_kernel, grid_spec=pltpu.PrefetchScalarGridSpec(num_sc...  5.85 us
    unnamed x16, local copies, waits for them, and re-layouts  5.31 us
  transfers between devices with their start and end apart: 13, of which 6 were waited for; matrix products, arithmetic and copies ran while one was open for 3% of the time, Pallas kernels for 43%

profile of v4, /device:TPU:0, one launch (start us, length us, event | category | flops | bytes accessed | tf_op | source)
XLA Modules:
  0.0 107.1 jit_solution(3182446633616882471)
XLA Ops:
  0.0 2.0 %collective-permute-start.6 = (bf16[512,2048]{1,0:T(8,128)(2,1)}, bf16[512,2048]{1,0:T(8,128)(2,1)S(1)}, u32[]{:S(2)}, u32[]{:S(2)}) collective-permute-start(bf16[512,2048]{1,0:T(8,128)(2,1)} %w0.1), channel_id=1, source_target_pairs={{0,1},{1,2},{2,3},{3,0},{4,7},{5,4},{6,5},{7,6},{8,9},{9,10},{10,1... | collective-permute-start | bytes 6291464 | tf_op jit(solution)/shard_map/ppermute | solution.py:399
  2.0 20.4 %project.1 = (bf16[2048,512]{1,0:T(8,128)(2,1)}, bf16[2048,512]{1,0:T(8,128)(2,1)}, bf16[2048,512]{1,0:T(8,128)(2,1)}, bf16[8,4,256,128]{3,2,1,0:T(8,128)(2,1)},...) custom-call(bf16[2048,2048]{1,0:T(8,128)(2,1)} %x_hbm.1, bf16[3,2048,512]{2,1,0:T(8,128)(2,1)} %w_hbm.1), custom_call_target="tpu_custom_call" | custom-call | flops 12884901888 | bytes 14680064 | tf_op jit(solution)/shard_map/project/pallas_call | solution.py:137
  22.4 1.7 %collective-permute-start = (f32[4,128,128]{2,1,0:T(8,128)}, f32[4,128,128]{2,1,0:T(8,128)S(1)}, u32[]{:S(2)}, u32[]{:S(2)}) collective-permute-start(f32[4,128,128]{2,1,0:T(8,128)} %get-tuple-element.18), channel_id=1, source_target_pairs={{0,4},{4,0},{8,12},{12,8},{16,20},{20,16},{24,28},{28,24},{32,36},... | collective-permute-start | bytes 786440 | tf_op jit(solution)/shard_map/ppermute | solution.py:396
  24.1 4.2 %collective-permute-done.6.wa = bf16[512,2048]{1,0:T(8,128)(2,1)S(1)} collective-permute-done((bf16[512,2048]{1,0:T(8,128)(2,1)}, bf16[512,2048]{1,0:T(8,128)(2,1)S(1)}, u32[]{:S(2)}, u32[]{:S(2)}) %collective-permute-start.6) | collective-permute-done | bytes 2097184 | tf_op jit(solution)/shard_map/ppermute | solution.py:399
  32.7 3.5 %collective-permute-done.1.y1_ref = bf16[4,128,128]{2,1,0:T(8,128)(2,1)S(1)} collective-permute-done((bf16[4,128,128]{2,1,0:T(8,128)(2,1)S(1)}, bf16[4,128,128]{2,1,0:T(8,128)(2,1)S(1)}, u32[]{:S(2)}, u32[]{:S(2)}) %collective-permute-start.1) | collective-permute-done | bytes 131104 | tf_op jit(solution)/shard_map/ppermute | solution.py:368
  36.2 3.1 %collective-permute-start.2 = (bf16[4,128,128]{2,1,0:T(8,128)(2,1)S(1)}, bf16[4,128,128]{2,1,0:T(8,128)(2,1)S(1)}, u32[]{:S(2)}, u32[]{:S(2)}) collective-permute-start(bf16[4,128,128]{2,1,0:T(8,128)(2,1)S(1)} %add_convert_fusion.2), channel_id=1, source_target_pairs={{0,24},{4,28},{8,16},{12,20},{16,8},{20,12},{24,0},{28,4},{32,56},... | collective-permute-start | bytes 393224 | tf_op jit(solution)/shard_map/ppermute | solution.py:370
  39.3 4.1 %collective-permute-done.2.y2_ref = bf16[4,128,128]{2,1,0:T(8,128)(2,1)S(1)} collective-permute-done((bf16[4,128,128]{2,1,0:T(8,128)(2,1)S(1)}, bf16[4,128,128]{2,1,0:T(8,128)(2,1)S(1)}, u32[]{:S(2)}, u32[]{:S(2)}) %collective-permute-start.2) | collective-permute-done | bytes 131104 | tf_op jit(solution)/shard_map/ppermute | solution.py:370
  46.2 3.9 %collective-permute-done.3.x1_ref = bf16[4,128,128]{2,1,0:T(8,128)(2,1)} collective-permute-done((bf16[4,128,128]{2,1,0:T(8,128)(2,1)}, bf16[4,128,128]{2,1,0:T(8,128)(2,1)}, u32[]{:S(2)}, u32[]{:S(2)}) %collective-permute-start.3) | collective-permute-done | bytes 131104 | tf_op jit(solution)/shard_map/ppermute | solution.py:368
  50.1 1.7 %add_convert_fusion = bf16[4,128,128]{2,1,0:T(8,128)(2,1)} fusion(bf16[4,128,128]{2,1,0:T(8,128)(2,1)} %collective-permute-done.3.x1_ref, bf16[4,128,128]{2,1,0:T(8,128)(2,1)} %add_convert_fusion.1), kind=kLoop, calls=%fused_computation | loop fusion | flops 262144 | bytes 393216 | tf_op jit(solution)/shard_map/convert_element_type | solution.py:369
  51.7 2.8 %collective-permute-start.4 = (bf16[4,128,128]{2,1,0:T(8,128)(2,1)}, bf16[4,128,128]{2,1,0:T(8,128)(2,1)}, u32[]{:S(2)}, u32[]{:S(2)}) collective-permute-start(bf16[4,128,128]{2,1,0:T(8,128)(2,1)} %add_convert_fusion), channel_id=1, source_target_pairs={{0,96},{4,100},{8,104},{12,108},{16,112},{20,116},{24,120},{28,124... | collective-permute-start | bytes 393224 | tf_op jit(solution)/shard_map/ppermute | solution.py:370
  54.5 3.4 %local_part.3.att_in = f32[2048,512]{1,0:T(8,128)} custom-call(bf16[2048,512]{1,0:T(8,128)(2,1)} %get-tuple-element.13.q_ref, bf16[2048,512]{1,0:T(8,128)(2,1)} %get-tuple-element.14.k_ref, bf16[2048,512]{1,0:T(8,128)(2,1)} %get-tuple-element.15.v_ref, bf16[8,4,256,128]{3,2,1,0:T(8,128)(2,1)} %get-tuple-element.16.pre_ref, ...), custom_call_target="tpu_custom_call", output_to_operand_aliasing={{}: (4, {})} | custom-call | flops 536870912 | bytes 3670016 | tf_op jit(solution)/shard_map/local_part/pallas_call | solution.py:176
  57.9 3.4 %local_part.4.att_in = f32[2048,512]{1,0:T(8,128)} custom-call(bf16[2048,512]{1,0:T(8,128)(2,1)} %get-tuple-element.13.q_ref, bf16[2048,512]{1,0:T(8,128)(2,1)} %get-tuple-element.14.k_ref, bf16[2048,512]{1,0:T(8,128)(2,1)} %get-tuple-element.15.v_ref, bf16[8,4,256,128]{3,2,1,0:T(8,128)(2,1)} %get-tuple-element.16.pre_ref, ...), custom_call_target="tpu_custom_call", output_to_operand_aliasing={{}: (4, {})} | custom-call | flops 536870912 | bytes 3670016 | tf_op jit(solution)/shard_map/local_part/pallas_call | solution.py:176
  61.3 3.4 %local_part.5.att_ref = f32[2048,512]{1,0:T(8,128)} custom-call(bf16[2048,512]{1,0:T(8,128)(2,1)} %get-tuple-element.13.q_ref, bf16[2048,512]{1,0:T(8,128)(2,1)} %get-tuple-element.14.k_ref, bf16[2048,512]{1,0:T(8,128)(2,1)} %get-tuple-element.15.v_ref, bf16[8,4,256,128]{3,2,1,0:T(8,128)(2,1)} %get-tuple-element.16.pre_ref, ...), custom_call_target="tpu_custom_call", output_to_operand_aliasing={{}: (4, {})} | custom-call | flops 536870912 | bytes 3670016 | tf_op jit(solution)/shard_map/local_part/pallas_call | solution.py:176
  64.7 3.1 %finish.4 = (bf16[512,512]{1,0:T(8,128)(2,1)}, bf16[4,256,128]{2,1,0:T(8,128)(2,1)}) custom-call(s32[1]{0:T(128)} %bitcast.1.head, s32[1]{0:T(128)} %bitcast.core, s32[1]{0:T(128)} %bitcast.2.y, s32[1]{0:T(128)} %bitcast.3.x, bf16[2048,512]{1,0:T(8,128)(2,1)} %get-tuple-element.13.q_ref, f32[2048,512]{1,0:T(8,128)} %local_part.5.att_ref, ...), custom_call_target="tpu_custom_call" | custom-call | flops 134217728 | bytes 2097152 | tf_op jit(solution)/shard_map/finish/pallas_call | solution.py:244
  67.8 2.7 %finish.7 = bf16[512,512]{1,0:T(8,128)(2,1)} custom-call(s32[1]{0:T(128)} %bitcast.1.head, s32[1]{0:T(128)} %bitcast.core, s32[1]{0:T(128)} %bitcast.2.y, s32[1]{0:T(128)} %bitcast.3.x, bf16[2048,512]{1,0:T(8,128)(2,1)} %get-tuple-element.13.q_ref, f32[2048,512]{1,0:T(8,128)} %local_part.5.att_ref, bf16[4,256,128]{2,1,0:T(8,128)(2,1)} %get-tuple-element.19.pair_ref, ...), custom_call_target="tpu_custom_call" | custom-call | flops 134217728 | bytes 2097152 | tf_op jit(solution)/shard_map/finish/pallas_call | solution.py:244
  71.5 2.7 %finish.6 = bf16[512,512]{1,0:T(8,128)(2,1)} custom-call(s32[1]{0:T(128)} %bitcast.1.head, s32[1]{0:T(128)} %bitcast.core, s32[1]{0:T(128)} %bitcast.2.y, s32[1]{0:T(128)} %bitcast.3.x, bf16[2048,512]{1,0:T(8,128)(2,1)} %get-tuple-element.13.q_ref, f32[2048,512]{1,0:T(8,128)} %local_part.5.att_ref, bf16[4,256,128]{2,1,0:T(8,128)(2,1)} %get-tuple-element.19.pair_ref, ...), custom_call_target="tpu_custom_call" | custom-call | flops 134217728 | bytes 2097152 | tf_op jit(solution)/shard_map/finish/pallas_call | solution.py:244
  74.2 2.3 %collective-permute-start.10 = (bf16[512,512]{1,0:T(8,128)(2,1)}, bf16[512,512]{1,0:T(8,128)(2,1)}, u32[]{:S(2)}, u32[]{:S(2)}) collective-permute-start(bf16[512,512]{1,0:T(8,128)(2,1)} %finish.6), channel_id=1, source_target_pairs={{0,3},{1,0},{2,1},{3,2},{4,5},{5,6},{6,7},{7,4},{8,11},{9,8},{10,9... | collective-permute-start | bytes 1572872 | tf_op jit(solution)/shard_map/ppermute | solution.py:399
  76.5 10.1 %collective-permute-done.11 = bf16[512,512]{1,0:T(8,128)(2,1)} collective-permute-done((bf16[512,512]{1,0:T(8,128)(2,1)}, bf16[512,512]{1,0:T(8,128)(2,1)}, u32[]{:S(2)}, u32[]{:S(2)}) %collective-permute-start.11) | collective-permute-done | bytes 524320 | tf_op jit(solution)/shard_map/ppermute | solution.py:399
  86.6 2.7 %finish.5.n0 = bf16[512,512]{1,0:T(8,128)(2,1)} custom-call(s32[1]{0:T(128)} %bitcast.1.head, s32[1]{0:T(128)} %bitcast.core, s32[1]{0:T(128)} %bitcast.2.y, s32[1]{0:T(128)} %bitcast.3.x, bf16[2048,512]{1,0:T(8,128)(2,1)} %get-tuple-element.13.q_ref, f32[2048,512]{1,0:T(8,128)} %local_part.5.att_ref, bf16[4,256,128]{2,1,0:T(8,128)(2,1)} %get-tuple-element.19.pair_ref, ...), custom_call_target="tpu_custom_call" | custom-call | flops 134217728 | bytes 2097152 | tf_op jit(solution)/shard_map/finish/pallas_call | solution.py:244
  89.3 3.2 %collective-permute-done.5.na = bf16[512,512]{1,0:T(8,128)(2,1)} collective-permute-done((bf16[512,512]{1,0:T(8,128)(2,1)}, bf16[512,512]{1,0:T(8,128)(2,1)}, u32[]{:S(2)}, u32[]{:S(2)}) %collective-permute-start.5) | collective-permute-done | bytes 524320 | tf_op jit(solution)/shard_map/ppermute | solution.py:399
  92.5 1.6 %copy-done.1 = bf16[512,2048]{1,0:T(8,128)(2,1)S(1)} copy-done((bf16[512,2048]{1,0:T(8,128)(2,1)S(1)}, bf16[512,2048]{1,0:T(8,128)(2,1)}, u32[]{:S(2)}) %copy-start.1) | copy-done | bytes 2097176
  94.1 1.6 %copy-done.2 = bf16[512,2048]{1,0:T(8,128)(2,1)S(1)} copy-done((bf16[512,2048]{1,0:T(8,128)(2,1)S(1)}, bf16[512,2048]{1,0:T(8,128)(2,1)}, u32[]{:S(2)}) %copy-start.2) | copy-done | bytes 2097176
  96.7 4.4 %mix_first.1.acc_hbm = f32[512,2048]{1,0:T(8,128)S(1)} custom-call(bf16[512,512]{1,0:T(8,128)(2,1)S(1)} %copy-done.3, bf16[512,512]{1,0:T(8,128)(2,1)} %collective-permute-done.5.na, bf16[512,2048]{1,0:T(8,128)(2,1)S(1)} %copy-done.2, bf16[512,2048]{1,0:T(8,128)(2,1)S(1)} %copy-done.1, bf16[512,2048]{1,0:T(8,128)(2,1)S(1)} %collective-permute-done.7.rest_0_.wb_hbm, ...), custom_call_target="tpu_custom_call" | custom-call | flops 2147483648 | bytes 8388608 | tf_op jit(solution)/shard_map/mix_first/pallas_call | solution.py:316
  101.1 5.9 %mix_last.1 = bf16[512,2048]{1,0:T(8,128)(2,1)} custom-call(s32[1]{0:T(128)} %bitcast.core, f32[512,2048]{1,0:T(8,128)S(1)} %mix_first.1.acc_hbm, bf16[512,512]{1,0:T(8,128)(2,1)} %collective-permute-done.10.nb_hbm, bf16[512,512]{1,0:T(8,128)(2,1)} %collective-permute-done.12.nf_hbm, bf16[512,2048]{1,0:T(8,128)(2,1)S(1)} %collective-permute-done.7.rest_0_.wb_hbm, ...), custom_call_target="tpu_custom_call" | custom-call | flops 2147483648 | bytes 8388608 | tf_op jit(solution)/shard_map/mix_last/pallas_call | solution.py:335
  (33 shorter events, 9.2 us)
Async XLA Ops:
  0.0 28.4 %collective-permute-start.6 = (bf16[512,2048]{1,0:T(8,128)(2,1)}, bf16[512,2048]{1,0:T(8,128)(2,1)S(1)}, u32[]{:S(2)}, u32[]{:S(2)}) collective-permute-start(bf16[512,2048]{1,0:T(8,128)(2,1)} %w0.1), channel_id=1, source_target_pairs={{0,1},{1,2},{2,3},{3,0},{4,7},{5,4},{6,5},{7,6},{8,9},{9,10},{10,1... | collective-permute-start | bytes 6291464 | tf_op jit(solution)/shard_map/ppermute | solution.py:399
  22.4 7.2 %collective-permute-start = (f32[4,128,128]{2,1,0:T(8,128)}, f32[4,128,128]{2,1,0:T(8,128)S(1)}, u32[]{:S(2)}, u32[]{:S(2)}) collective-permute-start(f32[4,128,128]{2,1,0:T(8,128)} %get-tuple-element.18), channel_id=1, source_target_pairs={{0,4},{4,0},{8,12},{12,8},{16,20},{20,16},{24,28},{28,24},{32,36},... | collective-permute-start | bytes 786440 | tf_op jit(solution)/shard_map/ppermute | solution.py:396
  24.1 5.5 %copy-start.7 = (f32[4,128,128]{2,1,0:T(8,128)S(1)}, f32[4,128,128]{2,1,0:T(8,128)}, u32[]{:S(2)}) copy-start(f32[4,128,128]{2,1,0:T(8,128)} %get-tuple-element.18) | copy-start | bytes 786436
  28.4 1.7 %copy-start = (bf16[512,2048]{1,0:T(8,128)(2,1)}, bf16[512,2048]{1,0:T(8,128)(2,1)S(1)}, u32[]{:S(2)}) copy-start(bf16[512,2048]{1,0:T(8,128)(2,1)S(1)} %collective-permute-done.6.wa) | copy-start | bytes 6291460
  29.6 16.6 %collective-permute-start.8 = (bf16[256,2048]{1,0:T(8,128)(2,1)}, bf16[256,2048]{1,0:T(8,128)(2,1)S(1)}, u32[]{:S(2)}, u32[]{:S(2)}) collective-permute-start(bf16[256,2048]{1,0:T(8,128)(2,1)} %constant_dynamic-slice_fusion), channel_id=1, source_target_pairs={{0,1},{1,2},{2,3},{3,0},{4,7},{5,4},{6,5},{7,6},{8,9},{9,10},{10,1... | collective-permute-start | bytes 3145736 | tf_op jit(solution)/shard_map/ppermute | solution.py:399
  29.6 28.3 %copy-start.4 = (f32[4,128,128]{2,1,0:T(8,128)}, f32[4,128,128]{2,1,0:T(8,128)S(1)}, u32[]{:S(2)}) copy-start(f32[4,128,128]{2,1,0:T(8,128)S(1)} %collective-permute-done.core_ref) | copy-start | bytes 786436
  30.1 6.0 %collective-permute-start.1 = (bf16[4,128,128]{2,1,0:T(8,128)(2,1)S(1)}, bf16[4,128,128]{2,1,0:T(8,128)(2,1)S(1)}, u32[]{:S(2)}, u32[]{:S(2)}) collective-permute-start(bf16[4,128,128]{2,1,0:T(8,128)(2,1)S(1)} %add_convert_fusion.3), channel_id=1, source_target_pairs={{0,8},{4,12},{8,0},{12,4},{16,24},{20,28},{24,16},{28,20},{32,40},... | collective-permute-start | bytes 393224 | tf_op jit(solution)/shard_map/ppermute | solution.py:368
  31.7 60.8 %collective-permute-start.7 = (bf16[512,2048]{1,0:T(8,128)(2,1)}, bf16[512,2048]{1,0:T(8,128)(2,1)S(1)}, u32[]{:S(2)}, u32[]{:S(2)}) collective-permute-start(bf16[512,2048]{1,0:T(8,128)(2,1)} %copy-done), channel_id=1, source_target_pairs={{0,4},{4,0},{8,12},{12,8},{16,20},{20,16},{24,28},{28,24},{32,36},... | collective-permute-start | bytes 6291464 | tf_op jit(solution)/shard_map/ppermute | solution.py:396
  36.1 21.8 %copy-start.5 = (bf16[4,128,128]{2,1,0:T(8,128)(2,1)}, bf16[4,128,128]{2,1,0:T(8,128)(2,1)S(1)}, u32[]{:S(2)}) copy-start(bf16[4,128,128]{2,1,0:T(8,128)(2,1)S(1)} %collective-permute-done.1.y1_ref) | copy-start | bytes 393220
  36.2 7.2 %collective-permute-start.2 = (bf16[4,128,128]{2,1,0:T(8,128)(2,1)S(1)}, bf16[4,128,128]{2,1,0:T(8,128)(2,1)S(1)}, u32[]{:S(2)}, u32[]{:S(2)}) collective-permute-start(bf16[4,128,128]{2,1,0:T(8,128)(2,1)S(1)} %add_convert_fusion.2), channel_id=1, source_target_pairs={{0,24},{4,28},{8,16},{12,20},{16,8},{20,12},{24,0},{28,4},{32,56},... | collective-permute-start | bytes 393224 | tf_op jit(solution)/shard_map/ppermute | solution.py:370
  43.4 0.7 copy-start.6
  44.7 5.4 %collective-permute-start.3 = (bf16[4,128,128]{2,1,0:T(8,128)(2,1)}, bf16[4,128,128]{2,1,0:T(8,128)(2,1)}, u32[]{:S(2)}, u32[]{:S(2)}) collective-permute-start(bf16[4,128,128]{2,1,0:T(8,128)(2,1)} %add_convert_fusion.1), channel_id=1, source_target_pairs={{0,32},{4,36},{8,40},{12,44},{16,48},{20,52},{24,56},{28,60},{32,0... | collective-permute-start | bytes 393224 | tf_op jit(solution)/shard_map/ppermute | solution.py:368
  46.2 46.3 %collective-permute-start.9 = (bf16[256,2048]{1,0:T(8,128)(2,1)S(1)}, bf16[256,2048]{1,0:T(8,128)(2,1)}, u32[]{:S(2)}, u32[]{:S(2)}) collective-permute-start(bf16[256,2048]{1,0:T(8,128)(2,1)S(1)} %collective-permute-done.8.rest_1_.mine_hbm), channel_id=1, source_target_pairs={{0,4},{4,0},{8,12},{12,8},{16,20},{20,16},{24,28},{28,24},{32,36},... | collective-permute-start | bytes 3145736 | tf_op jit(solution)/shard_map/ppermute | solution.py:396
  51.7 13.0 %collective-permute-start.4 = (bf16[4,128,128]{2,1,0:T(8,128)(2,1)}, bf16[4,128,128]{2,1,0:T(8,128)(2,1)}, u32[]{:S(2)}, u32[]{:S(2)}) collective-permute-start(bf16[4,128,128]{2,1,0:T(8,128)(2,1)} %add_convert_fusion), channel_id=1, source_target_pairs={{0,96},{4,100},{8,104},{12,108},{16,112},{20,116},{24,120},{28,124... | collective-permute-start | bytes 393224 | tf_op jit(solution)/shard_map/ppermute | solution.py:370
  70.5 16.0 %collective-permute-start.11 = (bf16[512,512]{1,0:T(8,128)(2,1)}, bf16[512,512]{1,0:T(8,128)(2,1)}, u32[]{:S(2)}, u32[]{:S(2)}) collective-permute-start(bf16[512,512]{1,0:T(8,128)(2,1)} %finish.7), channel_id=1, source_target_pairs={{0,1},{1,2},{2,3},{3,0},{4,7},{5,4},{6,5},{7,6},{8,9},{9,10},{10,1... | collective-permute-start | bytes 1572872 | tf_op jit(solution)/shard_map/ppermute | solution.py:399
  70.5 21.9 %collective-permute-start.5 = (bf16[512,512]{1,0:T(8,128)(2,1)}, bf16[512,512]{1,0:T(8,128)(2,1)}, u32[]{:S(2)}, u32[]{:S(2)}) collective-permute-start(bf16[512,512]{1,0:T(8,128)(2,1)} %get-tuple-element.20), channel_id=1, source_target_pairs={{0,1},{1,2},{2,3},{3,0},{4,7},{5,4},{6,5},{7,6},{8,9},{9,10},{10,1... | collective-permute-start | bytes 1572872 | tf_op jit(solution)/shard_map/ppermute | solution.py:399
  74.2 26.9 %collective-permute-start.10 = (bf16[512,512]{1,0:T(8,128)(2,1)}, bf16[512,512]{1,0:T(8,128)(2,1)}, u32[]{:S(2)}, u32[]{:S(2)}) collective-permute-start(bf16[512,512]{1,0:T(8,128)(2,1)} %finish.6), channel_id=1, source_target_pairs={{0,3},{1,0},{2,1},{3,2},{4,5},{5,6},{6,7},{7,4},{8,11},{9,8},{10,9... | collective-permute-start | bytes 1572872 | tf_op jit(solution)/shard_map/ppermute | solution.py:399
  86.6 14.6 %collective-permute-start.12 = (bf16[512,512]{1,0:T(8,128)(2,1)}, bf16[512,512]{1,0:T(8,128)(2,1)}, u32[]{:S(2)}, u32[]{:S(2)}) collective-permute-start(bf16[512,512]{1,0:T(8,128)(2,1)} %collective-permute-done.11), channel_id=1, source_target_pairs={{0,1},{1,2},{2,3},{3,0},{4,7},{5,4},{6,5},{7,6},{8,9},{9,10},{10,1... | collective-permute-start | bytes 1572872 | tf_op jit(solution)/shard_map/ppermute | solution.py:399
  92.5 1.6 %copy-start.1 = (bf16[512,2048]{1,0:T(8,128)(2,1)S(1)}, bf16[512,2048]{1,0:T(8,128)(2,1)}, u32[]{:S(2)}) copy-start(bf16[512,2048]{1,0:T(8,128)(2,1)} %copy-done) | copy-start | bytes 6291460
  94.1 1.6 %copy-start.2 = (bf16[512,2048]{1,0:T(8,128)(2,1)S(1)}, bf16[512,2048]{1,0:T(8,128)(2,1)}, u32[]{:S(2)}) copy-start(bf16[512,2048]{1,0:T(8,128)(2,1)} %w0.1) | copy-start | bytes 6291460
  95.7 1.0 copy-start.3

commit v5 on v4

--- a/solution.py
+++ b/solution.py
@@ -121,7 +121,7 @@
         if i < inside:
             put(i, att.at[rows], att_hbm.at[rows], 4)
     for h in range(heads):
-        tot_ref[h] = state[h]
+        tot_ref[h] = state[h].astype(BF16)
     for copy in pending:
         copy.wait()
 
@@ -141,7 +141,7 @@
         out_shape=[jax.ShapeDtypeStruct(wide, BF16)] * 3
         + [
             jax.ShapeDtypeStruct(states, BF16),
-            jax.ShapeDtypeStruct((heads, DH, DH), F32),
+            jax.ShapeDtypeStruct((heads, DH, DH), BF16),
             jax.ShapeDtypeStruct(wide, F32),
         ],
         scratch_shapes=[
@@ -257,9 +257,53 @@
     )(*place, q, att, *received, gain)
 
 
-def first_kernel(n0, na, w0, wa, *rest):
-    acc_ref = rest[-1]
-    acc_ref[...] = dot(n0[...], w0[...]) + dot(na[...], wa[...])
+def first_kernel(
+    n0_hbm, na_hbm, w0_hbm, wa_hbm, wb_hbm, mine_hbm, other_hbm,
+    acc_out, wb_out, mine_out, other_out,
+    n0, na, w0, wa, acc, n_sem, w_sem, out_sem, pass_sem,
+):
+    tiles = w_sem.shape[0]
+    tile = acc.shape[1] // tiles
+    columns = [slice(j * tile, (j + 1) * tile) for j in range(tiles)]
+    rows = [
+        pltpu.make_async_copy(n0_hbm, n0, n_sem.at[0]),
+        pltpu.make_async_copy(na_hbm, na, n_sem.at[1]),
+    ]
+    weights = [
+        [
+            pltpu.make_async_copy(w0_hbm.at[:, cut], w0.at[:, cut], w_sem.at[j, 0]),
+            pltpu.make_async_copy(wa_hbm.at[:, cut], wa.at[:, cut], w_sem.at[j, 1]),
+        ]
+        for j, cut in enumerate(columns)
+    ]
+    for which in range(2):
+        rows[which].start()
+        weights[0][which].start()
+    for copies in weights[1:]:
+        for copy in copies:
+            copy.start()
+    passed = [
+        pltpu.make_async_copy(source, target, pass_sem.at[i])
+        for i, (source, target) in enumerate(
+            ((wb_hbm, wb_out), (mine_hbm, mine_out), (other_hbm, other_out))
+        )
+    ]
+    for copy in passed:
+        copy.start()
+    for j, cut in enumerate(columns):
+        if j == 0:
+            rows[0].wait()
+        weights[j][0].wait()
+        total = dot(n0[...], w0[:, cut])
+        if j == 0:
+            rows[1].wait()
+        weights[j][1].wait()
+        acc[:, cut] = total + dot(na[...], wa[:, cut])
+        copy = pltpu.make_async_copy(acc.at[:, cut], acc_out.at[:, cut], out_sem.at[j])
+        copy.start()
+        passed.append(copy)
+    for copy in passed:
+        copy.wait()
 
 
 def last_kernel(
@@ -310,21 +354,28 @@
         copy.wait()
 
 
-def mix_first(normed, weights, later, tile=512):
+def mix_first(normed, weights, later, tiles=2):
     rows, feats = normed[0].shape
     width = weights[0].shape[1]
+    operands = [*normed, *weights]
     return pl.pallas_call(
         first_kernel,
-        grid=(width // tile,),
-        in_specs=[pl.BlockSpec(a.shape, lambda i: (0, 0)) for a in normed]
-        + [pl.BlockSpec((a.shape[0], tile), lambda i: (0, i)) for a in weights]
-        + [pl.BlockSpec(memory_space=pl.ANY)] * len(later),
-        out_specs=pl.BlockSpec((rows, tile), lambda i: (0, i)),
-        out_shape=jax.ShapeDtypeStruct((rows, width), F32),
+        in_specs=[pl.BlockSpec(memory_space=pltpu.HBM)] * (len(operands) + len(later)),
+        out_specs=[pl.BlockSpec(memory_space=pl.ANY)] * (1 + len(later)),
+        scratch_shapes=[pltpu.VMEM(a.shape, a.dtype) for a in operands]
+        + [
+            pltpu.VMEM((rows, width), F32),
+            pltpu.SemaphoreType.DMA((2,)),
+            pltpu.SemaphoreType.DMA((tiles, 2)),
+            pltpu.SemaphoreType.DMA((tiles,)),
+            pltpu.SemaphoreType.DMA((len(later),)),
+        ],
+        out_shape=[jax.ShapeDtypeStruct((rows, width), F32)]
+        + [jax.ShapeDtypeStruct(a.shape, a.dtype) for a in later],
         cost_estimate=cost(4 * rows * feats * width, 8 * rows * width),
         compiler_params=pltpu.CompilerParams(vmem_limit_bytes=24 << 20),
         name="mix_first",
-    )(*normed, *weights, *later)
+    )(*operands, *later)
 
 
 def mix_last(core, acc, normed, weights, tiles=2):
@@ -409,19 +460,19 @@
     other = swap(tot)
     for piece in range(1, 4):
         att = local_part(q, k, v, pre, att, piece, 4)
-    y1, y2, row = pair_rounds(tot + other, 2, total)
+    y1, y2, row = pair_rounds(tot.astype(F32) + other.astype(F32), 2, total)
     x1, x2, _ = pair_rounds(row, 8, total)
     received = (other, y1, y2, x1, x2)
 
     gain = norm_gain.reshape(1, -1)
-    na, pair = finish(place, 1, 0, q, att, received, gain, parts)
-    na = send(na, 1)
-    nf = send(finish(place, 0, 2, q, att, (pair,), gain, parts), 1)
+    nf, pair = finish(place, 0, 2, q, att, received, gain, parts)
+    nf = send(nf, 1)
+    na = send(finish(place, 1, 0, q, att, (pair,), gain, parts), 1)
     nb = send(finish(place, -1, 0, q, att, (pair,), gain, parts), -1)
     nf = send(nf, 1)
     n0 = finish(place, 0, 0, q, att, (pair,), gain, parts)
     later = [near_other, far, far_other]
-    acc = mix_first([n0, na], [w_out, near], later)
+    acc, *later = mix_first([n0, na], [w_out, near], later)
     return mix_last(core_id, acc, [nb, nf], later)
 
 

time: 108 us -> 103 us (0.954)
  local copies, waits for them, and re-layouts: 6.54 us -> 3.79 us
  waiting for transfers between devices: 28.9 us -> 26.3 us
    unnamed x16 -> x12, local copies, waits for them, and re-layouts: 5.31 us -> 2.65 us
    ppermute x6, waiting for transfers between devices: 17.5 us -> 15.4 us  [send(): return lax.ppermute(a, ('seq', 'head'), along(direction))]
  transfers between devices with their start and end apart: 13 -> 13, of which waited for: 6 -> 7; matrix products, arithmetic and copies ran while one was open for 3% -> 3% of each run, Pallas kernels for 43% -> 45%
where the time goes in v5:
time: 103 us
  Pallas kernels  52.6 us (51%)
  waiting for transfers between devices  26.3 us (26%)
  starting transfers between devices  17.4 us (17%)
  local copies, waits for them, and re-layouts  3.79 us (4%)
  other arithmetic  2.43 us (2%)
    pallas_call x1, Pallas kernels, project(): pl.pallas_call(qkv_kernel, in_specs=[anywhere] * 2, out_specs=[anywhere]...  20.3 us
    ppermute x6, waiting for transfers between devices, send(): return lax.ppermute(a, ('seq', 'head'), along(direction))  15.4 us
    pallas_call x4, Pallas kernels, finish(): pl.pallas_call(start_kernel if first else finish_kernel, grid_spec=pltpu....  11.2 us
    pallas_call x3, Pallas kernels, local_part(): pl.pallas_call(local_kernel, grid=(count // tile,), in_specs=[row, row, r...  10.2 us
    ppermute x2, waiting for transfers between devices, pair_rounds(): other = lax.ppermute(value, 'seq', pair_up(4, stride, total, True))  6.4 us
    pallas_call x1, Pallas kernels, mix_last(): pl.pallas_call(last_kernel, grid_spec=pltpu.PrefetchScalarGridSpec(num_sc...  5.96 us
    ppermute x2, starting transfers between devices, pair_rounds(): far = lax.ppermute(pair, 'seq', pair_up(4, stride, total, False))  5.85 us
    ppermute x6, starting transfers between devices, send(): return lax.ppermute(a, ('seq', 'head'), along(direction))  5.27 us
  transfers between devices with their start and end apart: 13, of which 7 were waited for; matrix products, arithmetic and copies ran while one was open for 3% of the time, Pallas kernels for 45%

profile of v5, /device:TPU:0, one launch (start us, length us, event | category | flops | bytes accessed | tf_op | source)
XLA Modules:
  0.0 102.8 jit_solution(16960718772198886267)
XLA Ops:
  0.0 2.0 %collective-permute-start.6 = (bf16[512,2048]{1,0:T(8,128)(2,1)}, bf16[512,2048]{1,0:T(8,128)(2,1)S(1)}, u32[]{:S(2)}, u32[]{:S(2)}) collective-permute-start(bf16[512,2048]{1,0:T(8,128)(2,1)} %w0_hbm.1), channel_id=1, source_target_pairs={{0,1},{1,2},{2,3},{3,0},{4,7},{5,4},{6,5},{7,6},{8,9},{9,10},{10,1... | collective-permute-start | bytes 6291464 | tf_op jit(solution)/shard_map/ppermute | solution.py:450
  2.0 20.3 %project.1 = (bf16[2048,512]{1,0:T(8,128)(2,1)}, bf16[2048,512]{1,0:T(8,128)(2,1)}, bf16[2048,512]{1,0:T(8,128)(2,1)}, bf16[8,4,256,128]{3,2,1,0:T(8,128)(2,1)},...) custom-call(bf16[2048,2048]{1,0:T(8,128)(2,1)} %x_hbm.1, bf16[3,2048,512]{2,1,0:T(8,128)(2,1)} %w_hbm.1), custom_call_target="tpu_custom_call" | custom-call | flops 12884901888 | bytes 14680064 | tf_op jit(solution)/shard_map/project/pallas_call | solution.py:137
  22.3 1.7 %collective-permute-start = (bf16[4,128,128]{2,1,0:T(8,128)(2,1)}, bf16[4,128,128]{2,1,0:T(8,128)(2,1)S(1)}, u32[]{:S(2)}, u32[]{:S(2)}) collective-permute-start(bf16[4,128,128]{2,1,0:T(8,128)(2,1)} %get-tuple-element.22), channel_id=1, source_target_pairs={{0,4},{4,0},{8,12},{12,8},{16,20},{20,16},{24,28},{28,24},{32,36},... | collective-permute-start | bytes 393224 | tf_op jit(solution)/shard_map/ppermute | solution.py:447
  24.1 4.3 %collective-permute-done.6.wa_hbm = bf16[512,2048]{1,0:T(8,128)(2,1)S(1)} collective-permute-done((bf16[512,2048]{1,0:T(8,128)(2,1)}, bf16[512,2048]{1,0:T(8,128)(2,1)S(1)}, u32[]{:S(2)}, u32[]{:S(2)}) %collective-permute-start.6) | collective-permute-done | bytes 2097184 | tf_op jit(solution)/shard_map/ppermute | solution.py:450
  29.6 1.7 %collective-permute-start.1 = (bf16[4,128,128]{2,1,0:T(8,128)(2,1)S(1)}, bf16[4,128,128]{2,1,0:T(8,128)(2,1)S(1)}, u32[]{:S(2)}, u32[]{:S(2)}) collective-permute-start(bf16[4,128,128]{2,1,0:T(8,128)(2,1)S(1)} %add_convert_fusion.3), channel_id=1, source_target_pairs={{0,8},{4,12},{8,0},{12,4},{16,24},{20,28},{24,16},{28,20},{32,40},... | collective-permute-start | bytes 393224 | tf_op jit(solution)/shard_map/ppermute | solution.py:419
  32.6 2.8 %collective-permute-done.1.y1_ref = bf16[4,128,128]{2,1,0:T(8,128)(2,1)S(1)} collective-permute-done((bf16[4,128,128]{2,1,0:T(8,128)(2,1)S(1)}, bf16[4,128,128]{2,1,0:T(8,128)(2,1)S(1)}, u32[]{:S(2)}, u32[]{:S(2)}) %collective-permute-start.1) | collective-permute-done | bytes 131104 | tf_op jit(solution)/shard_map/ppermute | solution.py:419
  35.4 3.1 %collective-permute-start.2 = (bf16[4,128,128]{2,1,0:T(8,128)(2,1)S(1)}, bf16[4,128,128]{2,1,0:T(8,128)(2,1)S(1)}, u32[]{:S(2)}, u32[]{:S(2)}) collective-permute-start(bf16[4,128,128]{2,1,0:T(8,128)(2,1)S(1)} %add_convert_fusion.2), channel_id=1, source_target_pairs={{0,24},{4,28},{8,16},{12,20},{16,8},{20,12},{24,0},{28,4},{32,56},... | collective-permute-start | bytes 393224 | tf_op jit(solution)/shard_map/ppermute | solution.py:421
  38.5 4.4 %collective-permute-done.2.y2_ref = bf16[4,128,128]{2,1,0:T(8,128)(2,1)S(1)} collective-permute-done((bf16[4,128,128]{2,1,0:T(8,128)(2,1)S(1)}, bf16[4,128,128]{2,1,0:T(8,128)(2,1)S(1)}, u32[]{:S(2)}, u32[]{:S(2)}) %collective-permute-start.2) | collective-permute-done | bytes 131104 | tf_op jit(solution)/shard_map/ppermute | solution.py:421
  45.7 3.6 %collective-permute-done.3.x1_ref = bf16[4,128,128]{2,1,0:T(8,128)(2,1)} collective-permute-done((bf16[4,128,128]{2,1,0:T(8,128)(2,1)}, bf16[4,128,128]{2,1,0:T(8,128)(2,1)}, u32[]{:S(2)}, u32[]{:S(2)}) %collective-permute-start.3) | collective-permute-done | bytes 131104 | tf_op jit(solution)/shard_map/ppermute | solution.py:419
  49.3 1.7 %add_convert_fusion = bf16[4,128,128]{2,1,0:T(8,128)(2,1)} fusion(bf16[4,128,128]{2,1,0:T(8,128)(2,1)} %collective-permute-done.3.x1_ref, bf16[4,128,128]{2,1,0:T(8,128)(2,1)} %add_convert_fusion.1), kind=kLoop, calls=%fused_computation | loop fusion | flops 262144 | bytes 393216 | tf_op jit(solution)/shard_map/convert_element_type | solution.py:420
  51.0 2.8 %collective-permute-start.4 = (bf16[4,128,128]{2,1,0:T(8,128)(2,1)}, bf16[4,128,128]{2,1,0:T(8,128)(2,1)}, u32[]{:S(2)}, u32[]{:S(2)}) collective-permute-start(bf16[4,128,128]{2,1,0:T(8,128)(2,1)} %add_convert_fusion), channel_id=1, source_target_pairs={{0,96},{4,100},{8,104},{12,108},{16,112},{20,116},{24,120},{28,124... | collective-permute-start | bytes 393224 | tf_op jit(solution)/shard_map/ppermute | solution.py:421
  53.8 3.4 %local_part.3.att_in = f32[2048,512]{1,0:T(8,128)} custom-call(bf16[2048,512]{1,0:T(8,128)(2,1)} %get-tuple-element.17.q_ref, bf16[2048,512]{1,0:T(8,128)(2,1)} %get-tuple-element.18.k_ref, bf16[2048,512]{1,0:T(8,128)(2,1)} %get-tuple-element.19.v_ref, bf16[8,4,256,128]{3,2,1,0:T(8,128)(2,1)} %get-tuple-element.20.pre_ref, ...), custom_call_target="tpu_custom_call", output_to_operand_aliasing={{}: (4, {})} | custom-call | flops 536870912 | bytes 3670016 | tf_op jit(solution)/shard_map/local_part/pallas_call | solution.py:176
  57.2 3.4 %local_part.4.att_in = f32[2048,512]{1,0:T(8,128)} custom-call(bf16[2048,512]{1,0:T(8,128)(2,1)} %get-tuple-element.17.q_ref, bf16[2048,512]{1,0:T(8,128)(2,1)} %get-tuple-element.18.k_ref, bf16[2048,512]{1,0:T(8,128)(2,1)} %get-tuple-element.19.v_ref, bf16[8,4,256,128]{3,2,1,0:T(8,128)(2,1)} %get-tuple-element.20.pre_ref, ...), custom_call_target="tpu_custom_call", output_to_operand_aliasing={{}: (4, {})} | custom-call | flops 536870912 | bytes 3670016 | tf_op jit(solution)/shard_map/local_part/pallas_call | solution.py:176
  60.6 3.4 %local_part.5.att_ref = f32[2048,512]{1,0:T(8,128)} custom-call(bf16[2048,512]{1,0:T(8,128)(2,1)} %get-tuple-element.17.q_ref, bf16[2048,512]{1,0:T(8,128)(2,1)} %get-tuple-element.18.k_ref, bf16[2048,512]{1,0:T(8,128)(2,1)} %get-tuple-element.19.v_ref, bf16[8,4,256,128]{3,2,1,0:T(8,128)(2,1)} %get-tuple-element.20.pre_ref, ...), custom_call_target="tpu_custom_call", output_to_operand_aliasing={{}: (4, {})} | custom-call | flops 536870912 | bytes 3670016 | tf_op jit(solution)/shard_map/local_part/pallas_call | solution.py:176
  64.0 3.0 %finish.4 = (bf16[512,512]{1,0:T(8,128)(2,1)}, bf16[4,256,128]{2,1,0:T(8,128)(2,1)}) custom-call(s32[1]{0:T(128)} %bitcast.1.head, s32[1]{0:T(128)} %bitcast.core, s32[1]{0:T(128)} %bitcast.2.y, s32[1]{0:T(128)} %bitcast.3.x, bf16[2048,512]{1,0:T(8,128)(2,1)} %get-tuple-element.17.q_ref, f32[2048,512]{1,0:T(8,128)} %local_part.5.att_ref, ...), custom_call_target="tpu_custom_call" | custom-call | flops 134217728 | bytes 2097152 | tf_op jit(solution)/shard_map/finish/pallas_call | solution.py:244
  67.0 2.7 %finish.6 = bf16[512,512]{1,0:T(8,128)(2,1)} custom-call(s32[1]{0:T(128)} %bitcast.1.head, s32[1]{0:T(128)} %bitcast.core, s32[1]{0:T(128)} %bitcast.2.y, s32[1]{0:T(128)} %bitcast.3.x, bf16[2048,512]{1,0:T(8,128)(2,1)} %get-tuple-element.17.q_ref, f32[2048,512]{1,0:T(8,128)} %local_part.5.att_ref, bf16[4,256,128]{2,1,0:T(8,128)(2,1)} %get-tuple-element.23.pair_ref, ...), custom_call_target="tpu_custom_call" | custom-call | flops 134217728 | bytes 2097152 | tf_op jit(solution)/shard_map/finish/pallas_call | solution.py:244
  70.7 2.7 %finish.7 = bf16[512,512]{1,0:T(8,128)(2,1)} custom-call(s32[1]{0:T(128)} %bitcast.1.head, s32[1]{0:T(128)} %bitcast.core, s32[1]{0:T(128)} %bitcast.2.y, s32[1]{0:T(128)} %bitcast.3.x, bf16[2048,512]{1,0:T(8,128)(2,1)} %get-tuple-element.17.q_ref, f32[2048,512]{1,0:T(8,128)} %local_part.5.att_ref, bf16[4,256,128]{2,1,0:T(8,128)(2,1)} %get-tuple-element.23.pair_ref, ...), custom_call_target="tpu_custom_call" | custom-call | flops 134217728 | bytes 2097152 | tf_op jit(solution)/shard_map/finish/pallas_call | solution.py:244
  73.4 2.3 %collective-permute-start.10 = (bf16[512,512]{1,0:T(8,128)(2,1)}, bf16[512,512]{1,0:T(8,128)(2,1)}, u32[]{:S(2)}, u32[]{:S(2)}) collective-permute-start(bf16[512,512]{1,0:T(8,128)(2,1)} %finish.7), channel_id=1, source_target_pairs={{0,3},{1,0},{2,1},{3,2},{4,5},{5,6},{6,7},{7,4},{8,11},{9,8},{10,9... | collective-permute-start | bytes 1572872 | tf_op jit(solution)/shard_map/ppermute | solution.py:450
  75.7 4.3 %collective-permute-done.11 = bf16[512,512]{1,0:T(8,128)(2,1)} collective-permute-done((bf16[512,512]{1,0:T(8,128)(2,1)}, bf16[512,512]{1,0:T(8,128)(2,1)}, u32[]{:S(2)}, u32[]{:S(2)}) %collective-permute-start.11) | collective-permute-done | bytes 524320 | tf_op jit(solution)/shard_map/ppermute | solution.py:450
  79.9 2.7 %finish.5.n0_hbm = bf16[512,512]{1,0:T(8,128)(2,1)} custom-call(s32[1]{0:T(128)} %bitcast.1.head, s32[1]{0:T(128)} %bitcast.core, s32[1]{0:T(128)} %bitcast.2.y, s32[1]{0:T(128)} %bitcast.3.x, bf16[2048,512]{1,0:T(8,128)(2,1)} %get-tuple-element.17.q_ref, f32[2048,512]{1,0:T(8,128)} %local_part.5.att_ref, bf16[4,256,128]{2,1,0:T(8,128)(2,1)} %get-tuple-element.23.pair_ref, ...), custom_call_target="tpu_custom_call" | custom-call | flops 134217728 | bytes 2097152 | tf_op jit(solution)/shard_map/finish/pallas_call | solution.py:244
  82.6 6.3 %collective-permute-done.5.na_hbm = bf16[512,512]{1,0:T(8,128)(2,1)} collective-permute-done((bf16[512,512]{1,0:T(8,128)(2,1)}, bf16[512,512]{1,0:T(8,128)(2,1)}, u32[]{:S(2)}, u32[]{:S(2)}) %collective-permute-start.5) | collective-permute-done | bytes 524320 | tf_op jit(solution)/shard_map/ppermute | solution.py:450
  90.0 1.6 %copy-done.1 = bf16[512,2048]{1,0:T(8,128)(2,1)S(1)} copy-done((bf16[512,2048]{1,0:T(8,128)(2,1)S(1)}, bf16[512,2048]{1,0:T(8,128)(2,1)}, u32[]{:S(2)}) %copy-start.1) | copy-done | bytes 2097176
  91.6 5.0 %mix_first.1 = (f32[512,2048]{1,0:T(8,128)S(1)}, bf16[512,2048]{1,0:T(8,128)(2,1)S(1)}, bf16[256,2048]{1,0:T(8,128)(2,1)S(1)}, bf16[256,2048]{1,0:T(8,128)(2,1)S(1)}) custom-call(bf16[512,512]{1,0:T(8,128)(2,1)S(1)} %copy-done, bf16[512,512]{1,0:T(8,128)(2,1)} %collective-permute-done.5.na_hbm, bf16[512,2048]{1,0:T(8,128)(2,1)S(1)} %copy-done.1, ...), custom_call_target="tpu_custom_call" | custom-call | flops 2147483648 | bytes 8388608 | tf_op jit(solution)/shard_map/mix_first/pallas_call | solution.py:361
  96.6 6.0 %mix_last.1 = bf16[512,2048]{1,0:T(8,128)(2,1)} custom-call(s32[1]{0:T(128)} %bitcast.core, f32[512,2048]{1,0:T(8,128)S(1)} %get-tuple-element.24.acc_hbm, bf16[512,512]{1,0:T(8,128)(2,1)} %collective-permute-done.10.nb_hbm, bf16[512,512]{1,0:T(8,128)(2,1)} %collective-permute-done.12.nf_hbm, bf16[512,2048]{1,0:T(8,128)(2,1)S(1)} %get-tuple-element.26.wb_hbm, ...), custom_call_target="tpu_custom_call" | custom-call | flops 2147483648 | bytes 8388608 | tf_op jit(solution)/shard_map/mix_last/pallas_call | solution.py:386
  (29 shorter events, 7.4 us)
Async XLA Ops:
  0.0 28.4 %collective-permute-start.6 = (bf16[512,2048]{1,0:T(8,128)(2,1)}, bf16[512,2048]{1,0:T(8,128)(2,1)S(1)}, u32[]{:S(2)}, u32[]{:S(2)}) collective-permute-start(bf16[512,2048]{1,0:T(8,128)(2,1)} %w0_hbm.1), channel_id=1, source_target_pairs={{0,1},{1,2},{2,3},{3,0},{4,7},{5,4},{6,5},{7,6},{8,9},{9,10},{10,1... | collective-permute-start | bytes 6291464 | tf_op jit(solution)/shard_map/ppermute | solution.py:450
  22.3 7.2 %copy-start.5 = (bf16[4,128,128]{2,1,0:T(8,128)(2,1)S(1)}, bf16[4,128,128]{2,1,0:T(8,128)(2,1)}, u32[]{:S(2)}) copy-start(bf16[4,128,128]{2,1,0:T(8,128)(2,1)} %get-tuple-element.22) | copy-start | bytes 393220
  22.3 7.2 %collective-permute-start = (bf16[4,128,128]{2,1,0:T(8,128)(2,1)}, bf16[4,128,128]{2,1,0:T(8,128)(2,1)S(1)}, u32[]{:S(2)}, u32[]{:S(2)}) collective-permute-start(bf16[4,128,128]{2,1,0:T(8,128)(2,1)} %get-tuple-element.22), channel_id=1, source_target_pairs={{0,4},{4,0},{8,12},{12,8},{16,20},{20,16},{24,28},{28,24},{32,36},... | collective-permute-start | bytes 393224 | tf_op jit(solution)/shard_map/ppermute | solution.py:447
  29.5 16.2 %collective-permute-start.8 = (bf16[256,2048]{1,0:T(8,128)(2,1)}, bf16[256,2048]{1,0:T(8,128)(2,1)S(1)}, u32[]{:S(2)}, u32[]{:S(2)}) collective-permute-start(bf16[256,2048]{1,0:T(8,128)(2,1)} %constant_dynamic-slice_fusion), channel_id=1, source_target_pairs={{0,1},{1,2},{2,3},{3,0},{4,7},{5,4},{6,5},{7,6},{8,9},{9,10},{10,1... | collective-permute-start | bytes 3145736 | tf_op jit(solution)/shard_map/ppermute | solution.py:450
  29.5 27.6 %copy-start.2 = (bf16[4,128,128]{2,1,0:T(8,128)(2,1)}, bf16[4,128,128]{2,1,0:T(8,128)(2,1)S(1)}, u32[]{:S(2)}) copy-start(bf16[4,128,128]{2,1,0:T(8,128)(2,1)S(1)} %collective-permute-done.core_ref) | copy-start | bytes 393220
  29.6 5.8 %collective-permute-start.1 = (bf16[4,128,128]{2,1,0:T(8,128)(2,1)S(1)}, bf16[4,128,128]{2,1,0:T(8,128)(2,1)S(1)}, u32[]{:S(2)}, u32[]{:S(2)}) collective-permute-start(bf16[4,128,128]{2,1,0:T(8,128)(2,1)S(1)} %add_convert_fusion.3), channel_id=1, source_target_pairs={{0,8},{4,12},{8,0},{12,4},{16,24},{20,28},{24,16},{28,20},{32,40},... | collective-permute-start | bytes 393224 | tf_op jit(solution)/shard_map/ppermute | solution.py:419
  31.2 57.7 %collective-permute-start.7 = (bf16[512,2048]{1,0:T(8,128)(2,1)S(1)}, bf16[512,2048]{1,0:T(8,128)(2,1)}, u32[]{:S(2)}, u32[]{:S(2)}) collective-permute-start(bf16[512,2048]{1,0:T(8,128)(2,1)S(1)} %collective-permute-done.6.wa_hbm), channel_id=1, source_target_pairs={{0,4},{4,0},{8,12},{12,8},{16,20},{20,16},{24,28},{28,24},{32,36},... | collective-permute-start | bytes 6291464 | tf_op jit(solution)/shard_map/ppermute | solution.py:447
  35.4 21.8 %copy-start.3 = (bf16[4,128,128]{2,1,0:T(8,128)(2,1)}, bf16[4,128,128]{2,1,0:T(8,128)(2,1)S(1)}, u32[]{:S(2)}) copy-start(bf16[4,128,128]{2,1,0:T(8,128)(2,1)S(1)} %collective-permute-done.1.y1_ref) | copy-start | bytes 393220
  35.4 7.5 %collective-permute-start.2 = (bf16[4,128,128]{2,1,0:T(8,128)(2,1)S(1)}, bf16[4,128,128]{2,1,0:T(8,128)(2,1)S(1)}, u32[]{:S(2)}, u32[]{:S(2)}) collective-permute-start(bf16[4,128,128]{2,1,0:T(8,128)(2,1)S(1)} %add_convert_fusion.2), channel_id=1, source_target_pairs={{0,24},{4,28},{8,16},{12,20},{16,8},{20,12},{24,0},{28,4},{32,56},... | collective-permute-start | bytes 393224 | tf_op jit(solution)/shard_map/ppermute | solution.py:421
  43.0 14.2 %copy-start.4 = (bf16[4,128,128]{2,1,0:T(8,128)(2,1)}, bf16[4,128,128]{2,1,0:T(8,128)(2,1)S(1)}, u32[]{:S(2)}) copy-start(bf16[4,128,128]{2,1,0:T(8,128)(2,1)S(1)} %collective-permute-done.2.y2_ref) | copy-start | bytes 393220
  43.6 5.7 %collective-permute-start.3 = (bf16[4,128,128]{2,1,0:T(8,128)(2,1)}, bf16[4,128,128]{2,1,0:T(8,128)(2,1)}, u32[]{:S(2)}, u32[]{:S(2)}) collective-permute-start(bf16[4,128,128]{2,1,0:T(8,128)(2,1)} %add_convert_fusion.1), channel_id=1, source_target_pairs={{0,32},{4,36},{8,40},{12,44},{16,48},{20,52},{24,56},{28,60},{32,0... | collective-permute-start | bytes 393224 | tf_op jit(solution)/shard_map/ppermute | solution.py:419
  45.7 43.2 %collective-permute-start.9 = (bf16[256,2048]{1,0:T(8,128)(2,1)S(1)}, bf16[256,2048]{1,0:T(8,128)(2,1)}, u32[]{:S(2)}, u32[]{:S(2)}) collective-permute-start(bf16[256,2048]{1,0:T(8,128)(2,1)S(1)} %collective-permute-done.8.mine_hbm), channel_id=1, source_target_pairs={{0,4},{4,0},{8,12},{12,8},{16,20},{20,16},{24,28},{28,24},{32,36},... | collective-permute-start | bytes 3145736 | tf_op jit(solution)/shard_map/ppermute | solution.py:447
  51.0 13.0 %collective-permute-start.4 = (bf16[4,128,128]{2,1,0:T(8,128)(2,1)}, bf16[4,128,128]{2,1,0:T(8,128)(2,1)}, u32[]{:S(2)}, u32[]{:S(2)}) collective-permute-start(bf16[4,128,128]{2,1,0:T(8,128)(2,1)} %add_convert_fusion), channel_id=1, source_target_pairs={{0,96},{4,100},{8,104},{12,108},{16,112},{20,116},{24,120},{28,124... | collective-permute-start | bytes 393224 | tf_op jit(solution)/shard_map/ppermute | solution.py:421
  67.0 13.0 %collective-permute-start.11 = (bf16[512,512]{1,0:T(8,128)(2,1)}, bf16[512,512]{1,0:T(8,128)(2,1)}, u32[]{:S(2)}, u32[]{:S(2)}) collective-permute-start(bf16[512,512]{1,0:T(8,128)(2,1)} %get-tuple-element.25), channel_id=1, source_target_pairs={{0,1},{1,2},{2,3},{3,0},{4,7},{5,4},{6,5},{7,6},{8,9},{9,10},{10,1... | collective-permute-start | bytes 1572872 | tf_op jit(solution)/shard_map/ppermute | solution.py:450
  69.7 19.2 %collective-permute-start.5 = (bf16[512,512]{1,0:T(8,128)(2,1)}, bf16[512,512]{1,0:T(8,128)(2,1)}, u32[]{:S(2)}, u32[]{:S(2)}) collective-permute-start(bf16[512,512]{1,0:T(8,128)(2,1)} %finish.6), channel_id=1, source_target_pairs={{0,1},{1,2},{2,3},{3,0},{4,7},{5,4},{6,5},{7,6},{8,9},{9,10},{10,1... | collective-permute-start | bytes 1572872 | tf_op jit(solution)/shard_map/ppermute | solution.py:450
  73.4 23.2 %collective-permute-start.10 = (bf16[512,512]{1,0:T(8,128)(2,1)}, bf16[512,512]{1,0:T(8,128)(2,1)}, u32[]{:S(2)}, u32[]{:S(2)}) collective-permute-start(bf16[512,512]{1,0:T(8,128)(2,1)} %finish.7), channel_id=1, source_target_pairs={{0,3},{1,0},{2,1},{3,2},{4,5},{5,6},{6,7},{7,4},{8,11},{9,8},{10,9... | collective-permute-start | bytes 1572872 | tf_op jit(solution)/shard_map/ppermute | solution.py:450
  79.9 16.7 %collective-permute-start.12 = (bf16[512,512]{1,0:T(8,128)(2,1)}, bf16[512,512]{1,0:T(8,128)(2,1)}, u32[]{:S(2)}, u32[]{:S(2)}) collective-permute-start(bf16[512,512]{1,0:T(8,128)(2,1)} %collective-permute-done.11), channel_id=1, source_target_pairs={{0,1},{1,2},{2,3},{3,0},{4,7},{5,4},{6,5},{7,6},{8,9},{9,10},{10,1... | collective-permute-start | bytes 1572872 | tf_op jit(solution)/shard_map/ppermute | solution.py:450
  88.9 1.0 %copy-start = (bf16[512,512]{1,0:T(8,128)(2,1)S(1)}, bf16[512,512]{1,0:T(8,128)(2,1)}, u32[]{:S(2)}) copy-start(bf16[512,512]{1,0:T(8,128)(2,1)} %finish.5.n0_hbm) | copy-start | bytes 1572868
  90.0 1.6 %copy-start.1 = (bf16[512,2048]{1,0:T(8,128)(2,1)S(1)}, bf16[512,2048]{1,0:T(8,128)(2,1)}, u32[]{:S(2)}) copy-start(bf16[512,2048]{1,0:T(8,128)(2,1)} %w0_hbm.1) | copy-start | bytes 6291460

commit v6 on v4

--- a/solution.py
+++ b/solution.py
@@ -121,7 +121,7 @@
         if i < inside:
             put(i, att.at[rows], att_hbm.at[rows], 4)
     for h in range(heads):
-        tot_ref[h] = state[h]
+        tot_ref[h] = state[h].astype(BF16)
     for copy in pending:
         copy.wait()
 
@@ -141,7 +141,7 @@
         out_shape=[jax.ShapeDtypeStruct(wide, BF16)] * 3
         + [
             jax.ShapeDtypeStruct(states, BF16),
-            jax.ShapeDtypeStruct((heads, DH, DH), F32),
+            jax.ShapeDtypeStruct((heads, DH, DH), BF16),
             jax.ShapeDtypeStruct(wide, F32),
         ],
         scratch_shapes=[
@@ -257,101 +257,77 @@
     )(*place, q, att, *received, gain)
 
 
-def first_kernel(n0, na, w0, wa, *rest):
-    acc_ref = rest[-1]
-    acc_ref[...] = dot(n0[...], w0[...]) + dot(na[...], wa[...])
-
-
-def last_kernel(
-    core, acc_hbm, nb_hbm, nf_hbm, wb_hbm, mine_hbm, other_hbm, out_hbm,
-    acc, nb, nf, wb, mine, other, out, n_sem, w_sem, out_sem,
-):
-    tiles = w_sem.shape[0]
-    tile = out.shape[1] // tiles
-    half = mine.shape[0]
-    rows = [pltpu.make_async_copy(nb_hbm, nb, n_sem.at[0]), pltpu.make_async_copy(nf_hbm, nf, n_sem.at[1])]
-    columns = [slice(j * tile, (j + 1) * tile) for j in range(tiles)]
-    weights = [
-        [
-            pltpu.make_async_copy(source.at[:, cut], target.at[:, cut], w_sem.at[j, which])
-            for which, (source, target) in enumerate(
-                ((wb_hbm, wb), (mine_hbm, mine), (other_hbm, other), (acc_hbm, acc))
-            )
-        ]
-        for j, cut in enumerate(columns)
+def own_kernel(n_ref, w_ref, *rest):
+    later, (acc_ref, *passed, sem) = rest[: len(rest) // 2 - 1], rest[len(rest) // 2 - 1 :]
+    copies = [
+        pltpu.make_async_copy(source, target, sem.at[i])
+        for i, (source, target) in enumerate(zip(later, passed))
     ]
-    for which in range(2):
-        rows[which].start()
-        for copy in weights[0][which :: 2]:
-            copy.start()
-    for copies in weights[1:]:
+
+    @pl.when(pl.program_id(0) == 0)
+    def _():
         for copy in copies:
             copy.start()
-    own = pl.multiple_of(core[0] * half, half)
-    partner = pl.multiple_of((1 - core[0]) * half, half)
-    pending = []
-    for j, cut in enumerate(columns):
-        if j == 0:
-            rows[0].wait()
-        weights[j][0].wait()
-        total = dot(nb[...], wb[:, cut])
-        if j == 0:
-            rows[1].wait()
-        weights[j][1].wait()
-        total += dot(nf[:, pl.ds(own, half)], mine[:, cut])
-        weights[j][2].wait()
-        total += dot(nf[:, pl.ds(partner, half)], other[:, cut])
-        weights[j][3].wait()
-        out[:, cut] = (total + acc[:, cut]).astype(BF16)
-        copy = pltpu.make_async_copy(out.at[:, cut], out_hbm.at[:, cut], out_sem.at[j])
-        copy.start()
-        pending.append(copy)
-    for copy in pending:
-        copy.wait()
-
-
-def mix_first(normed, weights, later, tile=512):
-    rows, feats = normed[0].shape
-    width = weights[0].shape[1]
+
+    acc_ref[...] = dot(n_ref[...], w_ref[...])
+
+    @pl.when(pl.program_id(0) == pl.num_programs(0) - 1)
+    def _():
+        for copy in copies:
+            copy.wait()
+
+
+def mix_own(normed, weight, later, tile=512):
+    rows, feats = normed.shape
+    width = weight.shape[1]
+    anywhere = [pl.BlockSpec(memory_space=pl.ANY)] * len(later)
     return pl.pallas_call(
-        first_kernel,
+        own_kernel,
         grid=(width // tile,),
-        in_specs=[pl.BlockSpec(a.shape, lambda i: (0, 0)) for a in normed]
-        + [pl.BlockSpec((a.shape[0], tile), lambda i: (0, i)) for a in weights]
-        + [pl.BlockSpec(memory_space=pl.ANY)] * len(later),
-        out_specs=pl.BlockSpec((rows, tile), lambda i: (0, i)),
-        out_shape=jax.ShapeDtypeStruct((rows, width), F32),
-        cost_estimate=cost(4 * rows * feats * width, 8 * rows * width),
+        in_specs=[
+            pl.BlockSpec((rows, feats), lambda i: (0, 0)),
+            pl.BlockSpec((feats, tile), lambda i: (0, i)),
+        ]
+        + anywhere,
+        out_specs=[pl.BlockSpec((rows, tile), lambda i: (0, i))] + anywhere,
+        out_shape=[jax.ShapeDtypeStruct((rows, width), F32)]
+        + [jax.ShapeDtypeStruct(a.shape, a.dtype) for a in later],
+        scratch_shapes=[pltpu.SemaphoreType.DMA((len(later),))],
+        cost_estimate=cost(2 * rows * feats * width, 8 * rows * width),
         compiler_params=pltpu.CompilerParams(vmem_limit_bytes=24 << 20),
-        name="mix_first",
-    )(*normed, *weights, *later)
-
-
-def mix_last(core, acc, normed, weights, tiles=2):
+        name="mix_own",
+    )(normed, weight, *later)
+
+
+def last_kernel(core, acc_ref, na, nb, nf, wa, wb, mine_ref, other_ref, out_ref):
+    half = mine_ref.shape[0]
+    mine = pl.multiple_of(core[0] * half, half)
+    other = pl.multiple_of((1 - core[0]) * half, half)
+    acc = dot(na[...], wa[...]) + dot(nb[...], wb[...])
+    acc += dot(nf[:, pl.ds(mine, half)], mine_ref[...])
+    acc += dot(nf[:, pl.ds(other, half)], other_ref[...])
+    out_ref[...] = (acc + acc_ref[...]).astype(BF16)
+
+
+def mix_last(core, acc, normed, weights, tile=512):
     rows, feats = normed[0].shape
     width = acc.shape[1]
-    anywhere = pl.BlockSpec(memory_space=pl.ANY)
-    operands = [acc, *normed, *weights]
+    column = lambda a: pl.BlockSpec((a.shape[0], tile), lambda i, core: (0, i))
     return pl.pallas_call(
         last_kernel,
         grid_spec=pltpu.PrefetchScalarGridSpec(
             num_scalar_prefetch=1,
-            grid=(1,),
-            in_specs=[anywhere] * len(operands),
-            out_specs=anywhere,
-            scratch_shapes=[pltpu.VMEM(a.shape, a.dtype) for a in operands]
-            + [
-                pltpu.VMEM((rows, width), BF16),
-                pltpu.SemaphoreType.DMA((2,)),
-                pltpu.SemaphoreType.DMA((tiles, 4)),
-                pltpu.SemaphoreType.DMA((tiles,)),
-            ],
+            grid=(width // tile,),
+            in_specs=[column(acc)]
+            + [pl.BlockSpec(a.shape, lambda i, core: (0, 0)) for a in normed]
+            + [column(a) for a in weights],
+            out_specs=pl.BlockSpec((rows, tile), lambda i, core: (0, i)),
         ),
         out_shape=jax.ShapeDtypeStruct((rows, width), BF16),
-        cost_estimate=cost(4 * rows * feats * width, 8 * rows * width),
+        cost_estimate=cost(6 * rows * feats * width, 8 * rows * width),
         compiler_params=pltpu.CompilerParams(vmem_limit_bytes=24 << 20),
         name="mix_last",
-    )(core, *operands)
+    )(core, acc, *normed, *weights)
 
 
 def pair_up(size, stride, total, first):
@@ -409,20 +385,19 @@
     other = swap(tot)
     for piece in range(1, 4):
         att = local_part(q, k, v, pre, att, piece, 4)
-    y1, y2, row = pair_rounds(tot + other, 2, total)
+    y1, y2, row = pair_rounds(tot.astype(F32) + other.astype(F32), 2, total)
     x1, x2, _ = pair_rounds(row, 8, total)
     received = (other, y1, y2, x1, x2)
 
     gain = norm_gain.reshape(1, -1)
-    na, pair = finish(place, 1, 0, q, att, received, gain, parts)
-    na = send(na, 1)
-    nf = send(finish(place, 0, 2, q, att, (pair,), gain, parts), 1)
+    nf, pair = finish(place, 0, 2, q, att, received, gain, parts)
+    nf = send(nf, 1)
+    na = send(finish(place, 1, 0, q, att, (pair,), gain, parts), 1)
     nb = send(finish(place, -1, 0, q, att, (pair,), gain, parts), -1)
     nf = send(nf, 1)
     n0 = finish(place, 0, 0, q, att, (pair,), gain, parts)
-    later = [near_other, far, far_other]
-    acc = mix_first([n0, na], [w_out, near], later)
-    return mix_last(core_id, acc, [nb, nf], later)
+    acc, *weights = mix_own(n0, w_out, [near, near_other, far, far_other])
+    return mix_last(core_id, acc, [na, nb, nf], weights)
 
 
 def solution(mesh):

time: 108 us -> 96.9 us (0.90)
  the two profiles are of different devices: /device:TPU:0 before, /device:TPU:1 now
where the time goes in v6:
time: 96.9 us; the launch traced here: 95.7 us
  Pallas kernels  50.9 us (53%)
  starting transfers between devices  23.5 us (24%)
  waiting for transfers between devices  14.1 us (15%)
  local copies, waits for them, and re-layouts  3.77 us (4%)
  other arithmetic  3.36 us (3%)
    pallas_call x1, Pallas kernels, project(): pl.pallas_call(qkv_kernel, in_specs=[anywhere] * 2, out_specs=[anywhere]...  20.3 us
    ppermute x6, starting transfers between devices, send(): return lax.ppermute(a, ('seq', 'head'), along(direction))  12.4 us
    pallas_call x4, Pallas kernels, finish(): pl.pallas_call(start_kernel if first else finish_kernel, grid_spec=pltpu....  11.2 us
    pallas_call x3, Pallas kernels, local_part(): pl.pallas_call(local_kernel, grid=(count // tile,), in_specs=[row, row, r...  10.2 us
    pallas_call x1, Pallas kernels, mix_last(): pl.pallas_call(last_kernel, grid_spec=pltpu.PrefetchScalarGridSpec(num_sc...  6.72 us
    ppermute x6, waiting for transfers between devices, send(): return lax.ppermute(a, ('seq', 'head'), along(direction))  6.36 us
    ppermute x2, starting transfers between devices, pair_rounds(): far = lax.ppermute(pair, 'seq', pair_up(4, stride, total, False))  5.3 us
    ppermute x2, waiting for transfers between devices, pair_rounds(): other = lax.ppermute(value, 'seq', pair_up(4, stride, total, True))  3.58 us
  transfers between devices with their start and end apart: 13, of which 6 were waited for; matrix products, arithmetic and copies ran while one was open for 5% of the time, Pallas kernels for 46%

profile of v6, /device:TPU:1, one launch (start us, length us, event | category | flops | bytes accessed | tf_op | source)
XLA Modules:
  0.0 95.7 jit_solution(12570727067224533831)
XLA Ops:
  0.0 4.6 %collective-permute-start.5 = (bf16[512,2048]{1,0:T(8,128)(2,1)}, bf16[512,2048]{1,0:T(8,128)(2,1)S(1)}, u32[]{:S(2)}, u32[]{:S(2)}) collective-permute-start(bf16[512,2048]{1,0:T(8,128)(2,1)} %w_ref.1), channel_id=1, source_target_pairs={{0,1},{1,2},{2,3},{3,0},{4,7},{5,4},{6,5},{7,6},{8,9},{9,10},{10,1... | collective-permute-start | bytes 6291464 | tf_op jit(solution)/shard_map/ppermute | solution.py:375
  4.6 20.3 %project.1 = (bf16[2048,512]{1,0:T(8,128)(2,1)}, bf16[2048,512]{1,0:T(8,128)(2,1)}, bf16[2048,512]{1,0:T(8,128)(2,1)}, bf16[8,4,256,128]{3,2,1,0:T(8,128)(2,1)},...) custom-call(bf16[2048,2048]{1,0:T(8,128)(2,1)} %x_hbm.1, bf16[3,2048,512]{2,1,0:T(8,128)(2,1)} %w_hbm.1), custom_call_target="tpu_custom_call" | custom-call | flops 12884901888 | bytes 14680064 | tf_op jit(solution)/shard_map/project/pallas_call | solution.py:137
  25.0 1.5 %collective-permute-done.core_ref = bf16[4,128,128]{2,1,0:T(8,128)(2,1)S(1)} collective-permute-done((bf16[4,128,128]{2,1,0:T(8,128)(2,1)}, bf16[4,128,128]{2,1,0:T(8,128)(2,1)S(1)}, u32[]{:S(2)}, u32[]{:S(2)}) %collective-permute-start) | collective-permute-done | bytes 131104 | tf_op jit(solution)/shard_map/ppermute | solution.py:372
  30.0 2.0 %collective-permute-start.7 = (bf16[256,2048]{1,0:T(8,128)(2,1)}, bf16[256,2048]{1,0:T(8,128)(2,1)S(1)}, u32[]{:S(2)}, u32[]{:S(2)}) collective-permute-start(bf16[256,2048]{1,0:T(8,128)(2,1)} %constant_dynamic-slice_fusion), channel_id=1, source_target_pairs={{0,1},{1,2},{2,3},{3,0},{4,7},{5,4},{6,5},{7,6},{8,9},{9,10},{10,1... | collective-permute-start | bytes 3145736 | tf_op jit(solution)/shard_map/ppermute | solution.py:375
  32.5 2.8 %collective-permute-start.2 = (bf16[4,128,128]{2,1,0:T(8,128)(2,1)S(1)}, bf16[4,128,128]{2,1,0:T(8,128)(2,1)S(1)}, u32[]{:S(2)}, u32[]{:S(2)}) collective-permute-start(bf16[4,128,128]{2,1,0:T(8,128)(2,1)S(1)} %add_convert_fusion.2), channel_id=1, source_target_pairs={{0,24},{4,28},{8,16},{12,20},{16,8},{20,12},{24,0},{28,4},{32,56},... | collective-permute-start | bytes 393224 | tf_op jit(solution)/shard_map/ppermute | solution.py:346
  35.3 2.7 %collective-permute-done.2.y2_ref = bf16[4,128,128]{2,1,0:T(8,128)(2,1)S(1)} collective-permute-done((bf16[4,128,128]{2,1,0:T(8,128)(2,1)S(1)}, bf16[4,128,128]{2,1,0:T(8,128)(2,1)S(1)}, u32[]{:S(2)}, u32[]{:S(2)}) %collective-permute-start.2) | collective-permute-done | bytes 131104 | tf_op jit(solution)/shard_map/ppermute | solution.py:346
  39.9 3.1 %collective-permute-done.3.x1_ref = bf16[4,128,128]{2,1,0:T(8,128)(2,1)} collective-permute-done((bf16[4,128,128]{2,1,0:T(8,128)(2,1)}, bf16[4,128,128]{2,1,0:T(8,128)(2,1)}, u32[]{:S(2)}, u32[]{:S(2)}) %collective-permute-start.3) | collective-permute-done | bytes 131104 | tf_op jit(solution)/shard_map/ppermute | solution.py:344
  43.0 1.6 %add_convert_fusion = bf16[4,128,128]{2,1,0:T(8,128)(2,1)} fusion(bf16[4,128,128]{2,1,0:T(8,128)(2,1)} %collective-permute-done.3.x1_ref, bf16[4,128,128]{2,1,0:T(8,128)(2,1)} %add_convert_fusion.1), kind=kLoop, calls=%fused_computation | loop fusion | flops 262144 | bytes 393216 | tf_op jit(solution)/shard_map/convert_element_type | solution.py:345
  44.7 2.5 %collective-permute-start.4 = (bf16[4,128,128]{2,1,0:T(8,128)(2,1)}, bf16[4,128,128]{2,1,0:T(8,128)(2,1)}, u32[]{:S(2)}, u32[]{:S(2)}) collective-permute-start(bf16[4,128,128]{2,1,0:T(8,128)(2,1)} %add_convert_fusion), channel_id=1, source_target_pairs={{0,96},{4,100},{8,104},{12,108},{16,112},{20,116},{24,120},{28,124... | collective-permute-start | bytes 393224 | tf_op jit(solution)/shard_map/ppermute | solution.py:346
  47.1 3.4 %local_part.3.att_in = f32[2048,512]{1,0:T(8,128)} custom-call(bf16[2048,512]{1,0:T(8,128)(2,1)} %get-tuple-element.18.q_ref, bf16[2048,512]{1,0:T(8,128)(2,1)} %get-tuple-element.19.k_ref, bf16[2048,512]{1,0:T(8,128)(2,1)} %get-tuple-element.20.v_ref, bf16[8,4,256,128]{3,2,1,0:T(8,128)(2,1)} %get-tuple-element.21.pre_ref, ...), custom_call_target="tpu_custom_call", output_to_operand_aliasing={{}: (4, {})} | custom-call | flops 536870912 | bytes 3670016 | tf_op jit(solution)/shard_map/local_part/pallas_call | solution.py:176
  50.6 3.1 %collective-permute-start.8 = (bf16[256,2048]{1,0:T(8,128)(2,1)S(1)}, bf16[256,2048]{1,0:T(8,128)(2,1)}, u32[]{:S(2)}, u32[]{:S(2)}) collective-permute-start(bf16[256,2048]{1,0:T(8,128)(2,1)S(1)} %collective-permute-done.7.rest_2_), channel_id=1, source_target_pairs={{0,4},{4,0},{8,12},{12,8},{16,20},{20,16},{24,28},{28,24},{32,36},... | collective-permute-start | bytes 3145736 | tf_op jit(solution)/shard_map/ppermute | solution.py:372
  53.7 3.4 %local_part.4.att_in = f32[2048,512]{1,0:T(8,128)} custom-call(bf16[2048,512]{1,0:T(8,128)(2,1)} %get-tuple-element.18.q_ref, bf16[2048,512]{1,0:T(8,128)(2,1)} %get-tuple-element.19.k_ref, bf16[2048,512]{1,0:T(8,128)(2,1)} %get-tuple-element.20.v_ref, bf16[8,4,256,128]{3,2,1,0:T(8,128)(2,1)} %get-tuple-element.21.pre_ref, ...), custom_call_target="tpu_custom_call", output_to_operand_aliasing={{}: (4, {})} | custom-call | flops 536870912 | bytes 3670016 | tf_op jit(solution)/shard_map/local_part/pallas_call | solution.py:176
  57.1 3.4 %local_part.5.att_ref = f32[2048,512]{1,0:T(8,128)} custom-call(bf16[2048,512]{1,0:T(8,128)(2,1)} %get-tuple-element.18.q_ref, bf16[2048,512]{1,0:T(8,128)(2,1)} %get-tuple-element.19.k_ref, bf16[2048,512]{1,0:T(8,128)(2,1)} %get-tuple-element.20.v_ref, bf16[8,4,256,128]{3,2,1,0:T(8,128)(2,1)} %get-tuple-element.21.pre_ref, ...), custom_call_target="tpu_custom_call", output_to_operand_aliasing={{}: (4, {})} | custom-call | flops 536870912 | bytes 3670016 | tf_op jit(solution)/shard_map/local_part/pallas_call | solution.py:176
  60.5 3.0 %finish.4 = (bf16[512,512]{1,0:T(8,128)(2,1)}, bf16[4,256,128]{2,1,0:T(8,128)(2,1)}) custom-call(s32[1]{0:T(128)} %bitcast.1.head, s32[1]{0:T(128)} %bitcast.core, s32[1]{0:T(128)} %bitcast.2.y, s32[1]{0:T(128)} %bitcast.3.x, bf16[2048,512]{1,0:T(8,128)(2,1)} %get-tuple-element.18.q_ref, f32[2048,512]{1,0:T(8,128)} %local_part.5.att_ref, ...), custom_call_target="tpu_custom_call" | custom-call | flops 134217728 | bytes 2097152 | tf_op jit(solution)/shard_map/finish/pallas_call | solution.py:244
  63.5 1.5 %collective-permute-start.11 = (bf16[512,512]{1,0:T(8,128)(2,1)}, bf16[512,512]{1,0:T(8,128)(2,1)}, u32[]{:S(2)}, u32[]{:S(2)}) collective-permute-start(bf16[512,512]{1,0:T(8,128)(2,1)} %get-tuple-element.26), channel_id=1, source_target_pairs={{0,1},{1,2},{2,3},{3,0},{4,7},{5,4},{6,5},{7,6},{8,9},{9,10},{10,1... | collective-permute-start | bytes 1572872 | tf_op jit(solution)/shard_map/ppermute | solution.py:375
  65.0 2.7 %finish.7 = bf16[512,512]{1,0:T(8,128)(2,1)} custom-call(s32[1]{0:T(128)} %bitcast.1.head, s32[1]{0:T(128)} %bitcast.core, s32[1]{0:T(128)} %bitcast.2.y, s32[1]{0:T(128)} %bitcast.3.x, bf16[2048,512]{1,0:T(8,128)(2,1)} %get-tuple-element.18.q_ref, f32[2048,512]{1,0:T(8,128)} %local_part.5.att_ref, bf16[4,256,128]{2,1,0:T(8,128)(2,1)} %get-tuple-element.24.pair_ref, ...), custom_call_target="tpu_custom_call" | custom-call | flops 134217728 | bytes 2097152 | tf_op jit(solution)/shard_map/finish/pallas_call | solution.py:244
  67.7 2.7 %finish.6 = bf16[512,512]{1,0:T(8,128)(2,1)} custom-call(s32[1]{0:T(128)} %bitcast.1.head, s32[1]{0:T(128)} %bitcast.core, s32[1]{0:T(128)} %bitcast.2.y, s32[1]{0:T(128)} %bitcast.3.x, bf16[2048,512]{1,0:T(8,128)(2,1)} %get-tuple-element.18.q_ref, f32[2048,512]{1,0:T(8,128)} %local_part.5.att_ref, bf16[4,256,128]{2,1,0:T(8,128)(2,1)} %get-tuple-element.24.pair_ref, ...), custom_call_target="tpu_custom_call" | custom-call | flops 134217728 | bytes 2097152 | tf_op jit(solution)/shard_map/finish/pallas_call | solution.py:244
  70.5 2.6 %collective-permute-start.9 = (bf16[512,512]{1,0:T(8,128)(2,1)}, bf16[512,512]{1,0:T(8,128)(2,1)}, u32[]{:S(2)}, u32[]{:S(2)}) collective-permute-start(bf16[512,512]{1,0:T(8,128)(2,1)} %finish.6), channel_id=1, source_target_pairs={{0,1},{1,2},{2,3},{3,0},{4,7},{5,4},{6,5},{7,6},{8,9},{9,10},{10,1... | collective-permute-start | bytes 1572872 | tf_op jit(solution)/shard_map/ppermute | solution.py:375
  74.1 1.7 %collective-permute-start.12 = (bf16[512,512]{1,0:T(8,128)(2,1)}, bf16[512,512]{1,0:T(8,128)(2,1)}, u32[]{:S(2)}, u32[]{:S(2)}) collective-permute-start(bf16[512,512]{1,0:T(8,128)(2,1)} %collective-permute-done.11), channel_id=1, source_target_pairs={{0,1},{1,2},{2,3},{3,0},{4,7},{5,4},{6,5},{7,6},{8,9},{9,10},{10,1... | collective-permute-start | bytes 1572872 | tf_op jit(solution)/shard_map/ppermute | solution.py:375
  75.8 2.7 %finish.5.n_ref = bf16[512,512]{1,0:T(8,128)(2,1)} custom-call(s32[1]{0:T(128)} %bitcast.1.head, s32[1]{0:T(128)} %bitcast.core, s32[1]{0:T(128)} %bitcast.2.y, s32[1]{0:T(128)} %bitcast.3.x, bf16[2048,512]{1,0:T(8,128)(2,1)} %get-tuple-element.18.q_ref, f32[2048,512]{1,0:T(8,128)} %local_part.5.att_ref, bf16[4,256,128]{2,1,0:T(8,128)(2,1)} %get-tuple-element.24.pair_ref, ...), custom_call_target="tpu_custom_call" | custom-call | flops 134217728 | bytes 2097152 | tf_op jit(solution)/shard_map/finish/pallas_call | solution.py:244
  78.5 1.6 %copy-done = bf16[512,2048]{1,0:T(8,128)(2,1)S(1)} copy-done((bf16[512,2048]{1,0:T(8,128)(2,1)S(1)}, bf16[512,2048]{1,0:T(8,128)(2,1)}, u32[]{:S(2)}) %copy-start) | copy-done | bytes 2097176
  81.1 2.5 %mix_own.1 = (f32[512,2048]{1,0:T(8,128)S(1)}, bf16[512,2048]{1,0:T(8,128)(2,1)S(1)}, bf16[512,2048]{1,0:T(8,128)(2,1)S(1)}, bf16[256,2048]{1,0:T(8,128)(2,1)S(1)}, bf16[256,2048]{1,0:T(8,128)(2,1)S(1)}) custom-call(bf16[512,512]{1,0:T(8,128)(2,1)S(1)} %copy-done.1, bf16[512,2048]{1,0:T(8,128)(2,1)S(1)} %copy-done, ...), custom_call_target="tpu_custom_call" | custom-call | flops 1073741824 | bytes 8388608 | tf_op jit(solution)/shard_map/mix_own/pallas_call | solution.py:284
  83.7 5.3 %collective-permute-done.12.nf = bf16[512,512]{1,0:T(8,128)(2,1)} collective-permute-done((bf16[512,512]{1,0:T(8,128)(2,1)}, bf16[512,512]{1,0:T(8,128)(2,1)}, u32[]{:S(2)}, u32[]{:S(2)}) %collective-permute-start.12) | collective-permute-done | bytes 524320 | tf_op jit(solution)/shard_map/ppermute | solution.py:375
  89.0 6.7 %mix_last.1 = bf16[512,2048]{1,0:T(8,128)(2,1)} custom-call(s32[1]{0:T(128)} %bitcast.core, f32[512,2048]{1,0:T(8,128)S(1)} %get-tuple-element.25.acc_ref, bf16[512,512]{1,0:T(8,128)(2,1)} %collective-permute-done.9.na, bf16[512,512]{1,0:T(8,128)(2,1)} %collective-permute-done.10.nb, bf16[512,512]{1,0:T(8,128)(2,1)} %collective-permute-done.12.nf, ...), custom_call_target="tpu_custom_call" | custom-call | flops 3221225472 | bytes 8388608 | tf_op jit(solution)/shard_map/mix_last/pallas_call | solution.py:316
  (27 shorter events, 8.1 us)
Async XLA Ops:
  0.0 28.9 %collective-permute-start.5 = (bf16[512,2048]{1,0:T(8,128)(2,1)}, bf16[512,2048]{1,0:T(8,128)(2,1)S(1)}, u32[]{:S(2)}, u32[]{:S(2)}) collective-permute-start(bf16[512,2048]{1,0:T(8,128)(2,1)} %w_ref.1), channel_id=1, source_target_pairs={{0,1},{1,2},{2,3},{3,0},{4,7},{5,4},{6,5},{7,6},{8,9},{9,10},{10,1... | collective-permute-start | bytes 6291464 | tf_op jit(solution)/shard_map/ppermute | solution.py:375
  24.9 1.6 %collective-permute-start = (bf16[4,128,128]{2,1,0:T(8,128)(2,1)}, bf16[4,128,128]{2,1,0:T(8,128)(2,1)S(1)}, u32[]{:S(2)}, u32[]{:S(2)}) collective-permute-start(bf16[4,128,128]{2,1,0:T(8,128)(2,1)} %get-tuple-element.23), channel_id=1, source_target_pairs={{0,4},{4,0},{8,12},{12,8},{16,20},{20,16},{24,28},{28,24},{32,36},... | collective-permute-start | bytes 393224 | tf_op jit(solution)/shard_map/ppermute | solution.py:372
  26.5 24.1 %copy-start.2 = (bf16[4,128,128]{2,1,0:T(8,128)(2,1)}, bf16[4,128,128]{2,1,0:T(8,128)(2,1)S(1)}, u32[]{:S(2)}) copy-start(bf16[4,128,128]{2,1,0:T(8,128)(2,1)S(1)} %collective-permute-done.core_ref) | copy-start | bytes 393220
  27.5 5.0 %collective-permute-start.1 = (bf16[4,128,128]{2,1,0:T(8,128)(2,1)S(1)}, bf16[4,128,128]{2,1,0:T(8,128)(2,1)S(1)}, u32[]{:S(2)}, u32[]{:S(2)}) collective-permute-start(bf16[4,128,128]{2,1,0:T(8,128)(2,1)S(1)} %add_convert_fusion.3), channel_id=1, source_target_pairs={{0,8},{4,12},{8,0},{12,4},{16,24},{20,28},{24,16},{28,20},{32,40},... | collective-permute-start | bytes 393224 | tf_op jit(solution)/shard_map/ppermute | solution.py:344
  30.0 20.6 %collective-permute-start.7 = (bf16[256,2048]{1,0:T(8,128)(2,1)}, bf16[256,2048]{1,0:T(8,128)(2,1)S(1)}, u32[]{:S(2)}, u32[]{:S(2)}) collective-permute-start(bf16[256,2048]{1,0:T(8,128)(2,1)} %constant_dynamic-slice_fusion), channel_id=1, source_target_pairs={{0,1},{1,2},{2,3},{3,0},{4,7},{5,4},{6,5},{7,6},{8,9},{9,10},{10,1... | collective-permute-start | bytes 3145736 | tf_op jit(solution)/shard_map/ppermute | solution.py:375
  32.0 46.5 %collective-permute-start.6 = (bf16[512,2048]{1,0:T(8,128)(2,1)S(1)}, bf16[512,2048]{1,0:T(8,128)(2,1)}, u32[]{:S(2)}, u32[]{:S(2)}) collective-permute-start(bf16[512,2048]{1,0:T(8,128)(2,1)S(1)} %collective-permute-done.5.rest_0_), channel_id=1, source_target_pairs={{0,4},{4,0},{8,12},{12,8},{16,20},{20,16},{24,28},{28,24},{32,36},... | collective-permute-start | bytes 6291464 | tf_op jit(solution)/shard_map/ppermute | solution.py:372
  32.5 18.1 %copy-start.3 = (bf16[4,128,128]{2,1,0:T(8,128)(2,1)}, bf16[4,128,128]{2,1,0:T(8,128)(2,1)S(1)}, u32[]{:S(2)}) copy-start(bf16[4,128,128]{2,1,0:T(8,128)(2,1)S(1)} %collective-permute-done.1.y1_ref) | copy-start | bytes 393220
  32.5 5.5 %collective-permute-start.2 = (bf16[4,128,128]{2,1,0:T(8,128)(2,1)S(1)}, bf16[4,128,128]{2,1,0:T(8,128)(2,1)S(1)}, u32[]{:S(2)}, u32[]{:S(2)}) collective-permute-start(bf16[4,128,128]{2,1,0:T(8,128)(2,1)S(1)} %add_convert_fusion.2), channel_id=1, source_target_pairs={{0,24},{4,28},{8,16},{12,20},{16,8},{20,12},{24,0},{28,4},{32,56},... | collective-permute-start | bytes 393224 | tf_op jit(solution)/shard_map/ppermute | solution.py:346
  38.0 12.6 %copy-start.4 = (bf16[4,128,128]{2,1,0:T(8,128)(2,1)}, bf16[4,128,128]{2,1,0:T(8,128)(2,1)S(1)}, u32[]{:S(2)}) copy-start(bf16[4,128,128]{2,1,0:T(8,128)(2,1)S(1)} %collective-permute-done.2.y2_ref) | copy-start | bytes 393220
  38.7 4.3 %collective-permute-start.3 = (bf16[4,128,128]{2,1,0:T(8,128)(2,1)}, bf16[4,128,128]{2,1,0:T(8,128)(2,1)}, u32[]{:S(2)}, u32[]{:S(2)}) collective-permute-start(bf16[4,128,128]{2,1,0:T(8,128)(2,1)} %add_convert_fusion.1), channel_id=1, source_target_pairs={{0,32},{4,36},{8,40},{12,44},{16,48},{20,52},{24,56},{28,60},{32,0... | collective-permute-start | bytes 393224 | tf_op jit(solution)/shard_map/ppermute | solution.py:344
  44.7 15.8 %collective-permute-start.4 = (bf16[4,128,128]{2,1,0:T(8,128)(2,1)}, bf16[4,128,128]{2,1,0:T(8,128)(2,1)}, u32[]{:S(2)}, u32[]{:S(2)}) collective-permute-start(bf16[4,128,128]{2,1,0:T(8,128)(2,1)} %add_convert_fusion), channel_id=1, source_target_pairs={{0,96},{4,100},{8,104},{12,108},{16,112},{20,116},{24,120},{28,124... | collective-permute-start | bytes 393224 | tf_op jit(solution)/shard_map/ppermute | solution.py:346
  50.6 27.9 %collective-permute-start.8 = (bf16[256,2048]{1,0:T(8,128)(2,1)S(1)}, bf16[256,2048]{1,0:T(8,128)(2,1)}, u32[]{:S(2)}, u32[]{:S(2)}) collective-permute-start(bf16[256,2048]{1,0:T(8,128)(2,1)S(1)} %collective-permute-done.7.rest_2_), channel_id=1, source_target_pairs={{0,4},{4,0},{8,12},{12,8},{16,20},{20,16},{24,28},{28,24},{32,36},... | collective-permute-start | bytes 3145736 | tf_op jit(solution)/shard_map/ppermute | solution.py:372
  63.5 10.6 %collective-permute-start.11 = (bf16[512,512]{1,0:T(8,128)(2,1)}, bf16[512,512]{1,0:T(8,128)(2,1)}, u32[]{:S(2)}, u32[]{:S(2)}) collective-permute-start(bf16[512,512]{1,0:T(8,128)(2,1)} %get-tuple-element.26), channel_id=1, source_target_pairs={{0,1},{1,2},{2,3},{3,0},{4,7},{5,4},{6,5},{7,6},{8,9},{9,10},{10,1... | collective-permute-start | bytes 1572872 | tf_op jit(solution)/shard_map/ppermute | solution.py:375
  67.7 15.9 %collective-permute-start.10 = (bf16[512,512]{1,0:T(8,128)(2,1)}, bf16[512,512]{1,0:T(8,128)(2,1)}, u32[]{:S(2)}, u32[]{:S(2)}) collective-permute-start(bf16[512,512]{1,0:T(8,128)(2,1)} %finish.7), channel_id=1, source_target_pairs={{0,3},{1,0},{2,1},{3,2},{4,5},{5,6},{6,7},{7,4},{8,11},{9,8},{10,9... | collective-permute-start | bytes 1572872 | tf_op jit(solution)/shard_map/ppermute | solution.py:375
  70.5 13.2 %collective-permute-start.9 = (bf16[512,512]{1,0:T(8,128)(2,1)}, bf16[512,512]{1,0:T(8,128)(2,1)}, u32[]{:S(2)}, u32[]{:S(2)}) collective-permute-start(bf16[512,512]{1,0:T(8,128)(2,1)} %finish.6), channel_id=1, source_target_pairs={{0,1},{1,2},{2,3},{3,0},{4,7},{5,4},{6,5},{7,6},{8,9},{9,10},{10,1... | collective-permute-start | bytes 1572872 | tf_op jit(solution)/shard_map/ppermute | solution.py:375
  74.1 14.8 %collective-permute-start.12 = (bf16[512,512]{1,0:T(8,128)(2,1)}, bf16[512,512]{1,0:T(8,128)(2,1)}, u32[]{:S(2)}, u32[]{:S(2)}) collective-permute-start(bf16[512,512]{1,0:T(8,128)(2,1)} %collective-permute-done.11), channel_id=1, source_target_pairs={{0,1},{1,2},{2,3},{3,0},{4,7},{5,4},{6,5},{7,6},{8,9},{9,10},{10,1... | collective-permute-start | bytes 1572872 | tf_op jit(solution)/shard_map/ppermute | solution.py:375
  78.5 1.6 %copy-start = (bf16[512,2048]{1,0:T(8,128)(2,1)S(1)}, bf16[512,2048]{1,0:T(8,128)(2,1)}, u32[]{:S(2)}) copy-start(bf16[512,2048]{1,0:T(8,128)(2,1)} %w_ref.1) | copy-start | bytes 6291460
  80.1 1.0 %copy-start.1 = (bf16[512,512]{1,0:T(8,128)(2,1)S(1)}, bf16[512,512]{1,0:T(8,128)(2,1)}, u32[]{:S(2)}) copy-start(bf16[512,512]{1,0:T(8,128)(2,1)} %finish.5.n_ref) | copy-start | bytes 1572868

commit v7 on v6

--- a/solution.py
+++ b/solution.py
@@ -299,11 +299,32 @@
     )(normed, weight, *later)
 
 
-def last_kernel(core, acc_ref, na, nb, nf, wa, wb, mine_ref, other_ref, out_ref):
+def middle_kernel(acc_ref, n_ref, w_ref, out_ref):
+    out_ref[...] = acc_ref[...] + dot(n_ref[...], w_ref[...])
+
+
+def mix_middle(acc, normed, weight, tile=512):
+    rows, feats = normed.shape
+    width = acc.shape[1]
+    column = lambda a: pl.BlockSpec((a.shape[0], tile), lambda i: (0, i))
+    return pl.pallas_call(
+        middle_kernel,
+        grid=(width // tile,),
+        in_specs=[column(acc), pl.BlockSpec((rows, feats), lambda i: (0, 0)), column(weight)],
+        out_specs=column(acc),
+        out_shape=jax.ShapeDtypeStruct((rows, width), F32),
+        input_output_aliases={0: 0},
+        cost_estimate=cost(2 * rows * feats * width, 8 * rows * width),
+        compiler_params=pltpu.CompilerParams(vmem_limit_bytes=24 << 20),
+        name="mix_middle",
+    )(acc, normed, weight)
+
+
+def last_kernel(core, acc_ref, nb, nf, wb, mine_ref, other_ref, out_ref):
     half = mine_ref.shape[0]
     mine = pl.multiple_of(core[0] * half, half)
     other = pl.multiple_of((1 - core[0]) * half, half)
-    acc = dot(na[...], wa[...]) + dot(nb[...], wb[...])
+    acc = dot(nb[...], wb[...])
     acc += dot(nf[:, pl.ds(mine, half)], mine_ref[...])
     acc += dot(nf[:, pl.ds(other, half)], other_ref[...])
     out_ref[...] = (acc + acc_ref[...]).astype(BF16)
@@ -324,7 +345,7 @@
             out_specs=pl.BlockSpec((rows, tile), lambda i, core: (0, i)),
         ),
         out_shape=jax.ShapeDtypeStruct((rows, width), BF16),
-        cost_estimate=cost(6 * rows * feats * width, 8 * rows * width),
+        cost_estimate=cost(4 * rows * feats * width, 8 * rows * width),
         compiler_params=pltpu.CompilerParams(vmem_limit_bytes=24 << 20),
         name="mix_last",
     )(core, acc, *normed, *weights)
@@ -396,8 +417,9 @@
     nb = send(finish(place, -1, 0, q, att, (pair,), gain, parts), -1)
     nf = send(nf, 1)
     n0 = finish(place, 0, 0, q, att, (pair,), gain, parts)
-    acc, *weights = mix_own(n0, w_out, [near, near_other, far, far_other])
-    return mix_last(core_id, acc, [na, nb, nf], weights)
+    acc, near, *weights = mix_own(n0, w_out, [near, near_other, far, far_other])
+    acc = mix_middle(acc, na, near)
+    return mix_last(core_id, acc, [nb, nf], weights)
 
 
 def solution(mesh):

time: 96.9 us -> 100 us (1.032)
  the two profiles are of different devices: /device:TPU:1 before, /device:TPU:0 now
where the time goes in v7:
time: 100 us; the launch traced here: 99.9 us
  Pallas kernels  52.9 us (53%)
  waiting for transfers between devices  23.3 us (23%)
  starting transfers between devices  17.4 us (17%)
  local copies, waits for them, and re-layouts  3.78 us (4%)
  other arithmetic  2.43 us (2%)
    pallas_call x1, Pallas kernels, project(): pl.pallas_call(qkv_kernel, in_specs=[anywhere] * 2, out_specs=[anywhere]...  20.3 us
    ppermute x6, waiting for transfers between devices, send(): return lax.ppermute(a, ('seq', 'head'), along(direction))  12.4 us
    pallas_call x4, Pallas kernels, finish(): pl.pallas_call(start_kernel if first else finish_kernel, grid_spec=pltpu....  11.2 us
    pallas_call x3, Pallas kernels, local_part(): pl.pallas_call(local_kernel, grid=(count // tile,), in_specs=[row, row, r...  10.2 us
    ppermute x2, waiting for transfers between devices, pair_rounds(): other = lax.ppermute(value, 'seq', pair_up(4, stride, total, True))  6.4 us
    ppermute x2, starting transfers between devices, pair_rounds(): far = lax.ppermute(pair, 'seq', pair_up(4, stride, total, False))  5.85 us
    pallas_call x1, Pallas kernels, mix_last(): pl.pallas_call(last_kernel, grid_spec=pltpu.PrefetchScalarGridSpec(num_sc...  5.34 us
    ppermute x6, starting transfers between devices, send(): return lax.ppermute(a, ('seq', 'head'), along(direction))  5.28 us
  transfers between devices with their start and end apart: 13, of which 8 were waited for; matrix products, arithmetic and copies ran while one was open for 4% of the time, Pallas kernels for 48%

profile of v7, /device:TPU:0, one launch (start us, length us, event | category | flops | bytes accessed | tf_op | source)
XLA Modules:
  0.0 99.9 jit_solution(12622652907073831778)
XLA Ops:
  0.0 2.0 %collective-permute-start.5 = (bf16[512,2048]{1,0:T(8,128)(2,1)}, bf16[512,2048]{1,0:T(8,128)(2,1)S(1)}, u32[]{:S(2)}, u32[]{:S(2)}) collective-permute-start(bf16[512,2048]{1,0:T(8,128)(2,1)} %w_ref.1), channel_id=1, source_target_pairs={{0,1},{1,2},{2,3},{3,0},{4,7},{5,4},{6,5},{7,6},{8,9},{9,10},{10,1... | collective-permute-start | bytes 6291464 | tf_op jit(solution)/shard_map/ppermute | solution.py:396
  2.0 20.3 %project.1 = (bf16[2048,512]{1,0:T(8,128)(2,1)}, bf16[2048,512]{1,0:T(8,128)(2,1)}, bf16[2048,512]{1,0:T(8,128)(2,1)}, bf16[8,4,256,128]{3,2,1,0:T(8,128)(2,1)},...) custom-call(bf16[2048,2048]{1,0:T(8,128)(2,1)} %x_hbm.1, bf16[3,2048,512]{2,1,0:T(8,128)(2,1)} %w_hbm.1), custom_call_target="tpu_custom_call" | custom-call | flops 12884901888 | bytes 14680064 | tf_op jit(solution)/shard_map/project/pallas_call | solution.py:137
  22.3 1.7 %collective-permute-start = (bf16[4,128,128]{2,1,0:T(8,128)(2,1)}, bf16[4,128,128]{2,1,0:T(8,128)(2,1)S(1)}, u32[]{:S(2)}, u32[]{:S(2)}) collective-permute-start(bf16[4,128,128]{2,1,0:T(8,128)(2,1)} %get-tuple-element.23), channel_id=1, source_target_pairs={{0,4},{4,0},{8,12},{12,8},{16,20},{20,16},{24,28},{28,24},{32,36},... | collective-permute-start | bytes 393224 | tf_op jit(solution)/shard_map/ppermute | solution.py:393
  24.1 4.3 %collective-permute-done.5.rest_0_ = bf16[512,2048]{1,0:T(8,128)(2,1)S(1)} collective-permute-done((bf16[512,2048]{1,0:T(8,128)(2,1)}, bf16[512,2048]{1,0:T(8,128)(2,1)S(1)}, u32[]{:S(2)}, u32[]{:S(2)}) %collective-permute-start.5) | collective-permute-done | bytes 2097184 | tf_op jit(solution)/shard_map/ppermute | solution.py:396
  29.6 1.7 %collective-permute-start.1 = (bf16[4,128,128]{2,1,0:T(8,128)(2,1)S(1)}, bf16[4,128,128]{2,1,0:T(8,128)(2,1)S(1)}, u32[]{:S(2)}, u32[]{:S(2)}) collective-permute-start(bf16[4,128,128]{2,1,0:T(8,128)(2,1)S(1)} %add_convert_fusion.3), channel_id=1, source_target_pairs={{0,8},{4,12},{8,0},{12,4},{16,24},{20,28},{24,16},{28,20},{32,40},... | collective-permute-start | bytes 393224 | tf_op jit(solution)/shard_map/ppermute | solution.py:365
  32.6 2.8 %collective-permute-done.1.y1_ref = bf16[4,128,128]{2,1,0:T(8,128)(2,1)S(1)} collective-permute-done((bf16[4,128,128]{2,1,0:T(8,128)(2,1)S(1)}, bf16[4,128,128]{2,1,0:T(8,128)(2,1)S(1)}, u32[]{:S(2)}, u32[]{:S(2)}) %collective-permute-start.1) | collective-permute-done | bytes 131104 | tf_op jit(solution)/shard_map/ppermute | solution.py:365
  35.4 3.1 %collective-permute-start.2 = (bf16[4,128,128]{2,1,0:T(8,128)(2,1)S(1)}, bf16[4,128,128]{2,1,0:T(8,128)(2,1)S(1)}, u32[]{:S(2)}, u32[]{:S(2)}) collective-permute-start(bf16[4,128,128]{2,1,0:T(8,128)(2,1)S(1)} %add_convert_fusion.2), channel_id=1, source_target_pairs={{0,24},{4,28},{8,16},{12,20},{16,8},{20,12},{24,0},{28,4},{32,56},... | collective-permute-start | bytes 393224 | tf_op jit(solution)/shard_map/ppermute | solution.py:367
  38.5 4.4 %collective-permute-done.2.y2_ref = bf16[4,128,128]{2,1,0:T(8,128)(2,1)S(1)} collective-permute-done((bf16[4,128,128]{2,1,0:T(8,128)(2,1)S(1)}, bf16[4,128,128]{2,1,0:T(8,128)(2,1)S(1)}, u32[]{:S(2)}, u32[]{:S(2)}) %collective-permute-start.2) | collective-permute-done | bytes 131104 | tf_op jit(solution)/shard_map/ppermute | solution.py:367
  45.7 3.6 %collective-permute-done.3.x1_ref = bf16[4,128,128]{2,1,0:T(8,128)(2,1)} collective-permute-done((bf16[4,128,128]{2,1,0:T(8,128)(2,1)}, bf16[4,128,128]{2,1,0:T(8,128)(2,1)}, u32[]{:S(2)}, u32[]{:S(2)}) %collective-permute-start.3) | collective-permute-done | bytes 131104 | tf_op jit(solution)/shard_map/ppermute | solution.py:365
  49.3 1.7 %add_convert_fusion = bf16[4,128,128]{2,1,0:T(8,128)(2,1)} fusion(bf16[4,128,128]{2,1,0:T(8,128)(2,1)} %collective-permute-done.3.x1_ref, bf16[4,128,128]{2,1,0:T(8,128)(2,1)} %add_convert_fusion.1), kind=kLoop, calls=%fused_computation | loop fusion | flops 262144 | bytes 393216 | tf_op jit(solution)/shard_map/convert_element_type | solution.py:366
  51.0 2.8 %collective-permute-start.4 = (bf16[4,128,128]{2,1,0:T(8,128)(2,1)}, bf16[4,128,128]{2,1,0:T(8,128)(2,1)}, u32[]{:S(2)}, u32[]{:S(2)}) collective-permute-start(bf16[4,128,128]{2,1,0:T(8,128)(2,1)} %add_convert_fusion), channel_id=1, source_target_pairs={{0,96},{4,100},{8,104},{12,108},{16,112},{20,116},{24,120},{28,124... | collective-permute-start | bytes 393224 | tf_op jit(solution)/shard_map/ppermute | solution.py:367
  53.8 3.4 %local_part.3.att_in = f32[2048,512]{1,0:T(8,128)} custom-call(bf16[2048,512]{1,0:T(8,128)(2,1)} %get-tuple-element.18.q_ref, bf16[2048,512]{1,0:T(8,128)(2,1)} %get-tuple-element.19.k_ref, bf16[2048,512]{1,0:T(8,128)(2,1)} %get-tuple-element.20.v_ref, bf16[8,4,256,128]{3,2,1,0:T(8,128)(2,1)} %get-tuple-element.21.pre_ref, ...), custom_call_target="tpu_custom_call", output_to_operand_aliasing={{}: (4, {})} | custom-call | flops 536870912 | bytes 3670016 | tf_op jit(solution)/shard_map/local_part/pallas_call | solution.py:176
  57.2 3.4 %local_part.4.att_in = f32[2048,512]{1,0:T(8,128)} custom-call(bf16[2048,512]{1,0:T(8,128)(2,1)} %get-tuple-element.18.q_ref, bf16[2048,512]{1,0:T(8,128)(2,1)} %get-tuple-element.19.k_ref, bf16[2048,512]{1,0:T(8,128)(2,1)} %get-tuple-element.20.v_ref, bf16[8,4,256,128]{3,2,1,0:T(8,128)(2,1)} %get-tuple-element.21.pre_ref, ...), custom_call_target="tpu_custom_call", output_to_operand_aliasing={{}: (4, {})} | custom-call | flops 536870912 | bytes 3670016 | tf_op jit(solution)/shard_map/local_part/pallas_call | solution.py:176
  60.6 3.4 %local_part.5.att_ref = f32[2048,512]{1,0:T(8,128)} custom-call(bf16[2048,512]{1,0:T(8,128)(2,1)} %get-tuple-element.18.q_ref, bf16[2048,512]{1,0:T(8,128)(2,1)} %get-tuple-element.19.k_ref, bf16[2048,512]{1,0:T(8,128)(2,1)} %get-tuple-element.20.v_ref, bf16[8,4,256,128]{3,2,1,0:T(8,128)(2,1)} %get-tuple-element.21.pre_ref, ...), custom_call_target="tpu_custom_call", output_to_operand_aliasing={{}: (4, {})} | custom-call | flops 536870912 | bytes 3670016 | tf_op jit(solution)/shard_map/local_part/pallas_call | solution.py:176
  64.0 3.0 %finish.4 = (bf16[512,512]{1,0:T(8,128)(2,1)}, bf16[4,256,128]{2,1,0:T(8,128)(2,1)}) custom-call(s32[1]{0:T(128)} %bitcast.1.head, s32[1]{0:T(128)} %bitcast.core, s32[1]{0:T(128)} %bitcast.2.y, s32[1]{0:T(128)} %bitcast.3.x, bf16[2048,512]{1,0:T(8,128)(2,1)} %get-tuple-element.18.q_ref, f32[2048,512]{1,0:T(8,128)} %local_part.5.att_ref, ...), custom_call_target="tpu_custom_call" | custom-call | flops 134217728 | bytes 2097152 | tf_op jit(solution)/shard_map/finish/pallas_call | solution.py:244
  67.0 2.8 %finish.6 = bf16[512,512]{1,0:T(8,128)(2,1)} custom-call(s32[1]{0:T(128)} %bitcast.1.head, s32[1]{0:T(128)} %bitcast.core, s32[1]{0:T(128)} %bitcast.2.y, s32[1]{0:T(128)} %bitcast.3.x, bf16[2048,512]{1,0:T(8,128)(2,1)} %get-tuple-element.18.q_ref, f32[2048,512]{1,0:T(8,128)} %local_part.5.att_ref, bf16[4,256,128]{2,1,0:T(8,128)(2,1)} %get-tuple-element.24.pair_ref, ...), custom_call_target="tpu_custom_call" | custom-call | flops 134217728 | bytes 2097152 | tf_op jit(solution)/shard_map/finish/pallas_call | solution.py:244
  70.7 2.7 %finish.7 = bf16[512,512]{1,0:T(8,128)(2,1)} custom-call(s32[1]{0:T(128)} %bitcast.1.head, s32[1]{0:T(128)} %bitcast.core, s32[1]{0:T(128)} %bitcast.2.y, s32[1]{0:T(128)} %bitcast.3.x, bf16[2048,512]{1,0:T(8,128)(2,1)} %get-tuple-element.18.q_ref, f32[2048,512]{1,0:T(8,128)} %local_part.5.att_ref, bf16[4,256,128]{2,1,0:T(8,128)(2,1)} %get-tuple-element.24.pair_ref, ...), custom_call_target="tpu_custom_call" | custom-call | flops 134217728 | bytes 2097152 | tf_op jit(solution)/shard_map/finish/pallas_call | solution.py:244
  73.4 2.3 %collective-permute-start.10 = (bf16[512,512]{1,0:T(8,128)(2,1)}, bf16[512,512]{1,0:T(8,128)(2,1)}, u32[]{:S(2)}, u32[]{:S(2)}) collective-permute-start(bf16[512,512]{1,0:T(8,128)(2,1)} %finish.7), channel_id=1, source_target_pairs={{0,3},{1,0},{2,1},{3,2},{4,5},{5,6},{6,7},{7,4},{8,11},{9,8},{10,9... | collective-permute-start | bytes 1572872 | tf_op jit(solution)/shard_map/ppermute | solution.py:396
  75.7 4.2 %collective-permute-done.11 = bf16[512,512]{1,0:T(8,128)(2,1)} collective-permute-done((bf16[512,512]{1,0:T(8,128)(2,1)}, bf16[512,512]{1,0:T(8,128)(2,1)}, u32[]{:S(2)}, u32[]{:S(2)}) %collective-permute-start.11) | collective-permute-done | bytes 524320 | tf_op jit(solution)/shard_map/ppermute | solution.py:396
  79.9 2.7 %finish.5.n_ref = bf16[512,512]{1,0:T(8,128)(2,1)} custom-call(s32[1]{0:T(128)} %bitcast.1.head, s32[1]{0:T(128)} %bitcast.core, s32[1]{0:T(128)} %bitcast.2.y, s32[1]{0:T(128)} %bitcast.3.x, bf16[2048,512]{1,0:T(8,128)(2,1)} %get-tuple-element.18.q_ref, f32[2048,512]{1,0:T(8,128)} %local_part.5.att_ref, bf16[4,256,128]{2,1,0:T(8,128)(2,1)} %get-tuple-element.24.pair_ref, ...), custom_call_target="tpu_custom_call" | custom-call | flops 134217728 | bytes 2097152 | tf_op jit(solution)/shard_map/finish/pallas_call | solution.py:244
  85.3 2.5 %mix_own.1 = (f32[512,2048]{1,0:T(8,128)S(1)}, bf16[512,2048]{1,0:T(8,128)(2,1)S(1)}, bf16[512,2048]{1,0:T(8,128)(2,1)S(1)}, bf16[256,2048]{1,0:T(8,128)(2,1)S(1)}, bf16[256,2048]{1,0:T(8,128)(2,1)S(1)}) custom-call(bf16[512,512]{1,0:T(8,128)(2,1)S(1)} %copy-done.1, bf16[512,2048]{1,0:T(8,128)(2,1)S(1)} %copy-done, ...), custom_call_target="tpu_custom_call" | custom-call | flops 1073741824 | bytes 8388608 | tf_op jit(solution)/shard_map/mix_own/pallas_call | solution.py:284
  88.9 3.4 %mix_middle.1.acc_ref = f32[512,2048]{1,0:T(8,128)S(1)} custom-call(f32[512,2048]{1,0:T(8,128)S(1)} %get-tuple-element.25.acc_ref, bf16[512,512]{1,0:T(8,128)(2,1)} %collective-permute-done.9.n_ref, bf16[512,2048]{1,0:T(8,128)(2,1)S(1)} %get-tuple-element.26.w_ref), custom_call_target="tpu_custom_call", output_to_operand_aliasing={{}: (0, {})} | custom-call | flops 1073741824 | bytes 8388608 | tf_op jit(solution)/shard_map/mix_middle/pallas_call | solution.py:310
  92.4 2.2 %collective-permute-done.12.nf = bf16[512,512]{1,0:T(8,128)(2,1)} collective-permute-done((bf16[512,512]{1,0:T(8,128)(2,1)}, bf16[512,512]{1,0:T(8,128)(2,1)}, u32[]{:S(2)}, u32[]{:S(2)}) %collective-permute-start.12) | collective-permute-done | bytes 524320 | tf_op jit(solution)/shard_map/ppermute | solution.py:396
  94.5 5.3 %mix_last.1 = bf16[512,2048]{1,0:T(8,128)(2,1)} custom-call(s32[1]{0:T(128)} %bitcast.core, f32[512,2048]{1,0:T(8,128)S(1)} %mix_middle.1.acc_ref, bf16[512,512]{1,0:T(8,128)(2,1)} %collective-permute-done.10.nb, bf16[512,512]{1,0:T(8,128)(2,1)} %collective-permute-done.12.nf, bf16[512,2048]{1,0:T(8,128)(2,1)S(1)} %get-tuple-element.28.wb, ...), custom_call_target="tpu_custom_call" | custom-call | flops 2147483648 | bytes 8388608 | tf_op jit(solution)/shard_map/mix_last/pallas_call | solution.py:337
  (30 shorter events, 10.1 us)
Async XLA Ops:
  0.0 28.4 %collective-permute-start.5 = (bf16[512,2048]{1,0:T(8,128)(2,1)}, bf16[512,2048]{1,0:T(8,128)(2,1)S(1)}, u32[]{:S(2)}, u32[]{:S(2)}) collective-permute-start(bf16[512,2048]{1,0:T(8,128)(2,1)} %w_ref.1), channel_id=1, source_target_pairs={{0,1},{1,2},{2,3},{3,0},{4,7},{5,4},{6,5},{7,6},{8,9},{9,10},{10,1... | collective-permute-start | bytes 6291464 | tf_op jit(solution)/shard_map/ppermute | solution.py:396
  22.3 7.2 %copy-start.5 = (bf16[4,128,128]{2,1,0:T(8,128)(2,1)S(1)}, bf16[4,128,128]{2,1,0:T(8,128)(2,1)}, u32[]{:S(2)}) copy-start(bf16[4,128,128]{2,1,0:T(8,128)(2,1)} %get-tuple-element.23) | copy-start | bytes 393220
  22.3 7.2 %collective-permute-start = (bf16[4,128,128]{2,1,0:T(8,128)(2,1)}, bf16[4,128,128]{2,1,0:T(8,128)(2,1)S(1)}, u32[]{:S(2)}, u32[]{:S(2)}) collective-permute-start(bf16[4,128,128]{2,1,0:T(8,128)(2,1)} %get-tuple-element.23), channel_id=1, source_target_pairs={{0,4},{4,0},{8,12},{12,8},{16,20},{20,16},{24,28},{28,24},{32,36},... | collective-permute-start | bytes 393224 | tf_op jit(solution)/shard_map/ppermute | solution.py:393
  29.5 16.2 %collective-permute-start.7 = (bf16[256,2048]{1,0:T(8,128)(2,1)}, bf16[256,2048]{1,0:T(8,128)(2,1)S(1)}, u32[]{:S(2)}, u32[]{:S(2)}) collective-permute-start(bf16[256,2048]{1,0:T(8,128)(2,1)} %constant_dynamic-slice_fusion), channel_id=1, source_target_pairs={{0,1},{1,2},{2,3},{3,0},{4,7},{5,4},{6,5},{7,6},{8,9},{9,10},{10,1... | collective-permute-start | bytes 3145736 | tf_op jit(solution)/shard_map/ppermute | solution.py:396
  29.5 27.6 %copy-start.2 = (bf16[4,128,128]{2,1,0:T(8,128)(2,1)}, bf16[4,128,128]{2,1,0:T(8,128)(2,1)S(1)}, u32[]{:S(2)}) copy-start(bf16[4,128,128]{2,1,0:T(8,128)(2,1)S(1)} %collective-permute-done.core_ref) | copy-start | bytes 393220
  29.6 5.8 %collective-permute-start.1 = (bf16[4,128,128]{2,1,0:T(8,128)(2,1)S(1)}, bf16[4,128,128]{2,1,0:T(8,128)(2,1)S(1)}, u32[]{:S(2)}, u32[]{:S(2)}) collective-permute-start(bf16[4,128,128]{2,1,0:T(8,128)(2,1)S(1)} %add_convert_fusion.3), channel_id=1, source_target_pairs={{0,8},{4,12},{8,0},{12,4},{16,24},{20,28},{24,16},{28,20},{32,40},... | collective-permute-start | bytes 393224 | tf_op jit(solution)/shard_map/ppermute | solution.py:365
  31.2 51.4 %collective-permute-start.6 = (bf16[512,2048]{1,0:T(8,128)(2,1)S(1)}, bf16[512,2048]{1,0:T(8,128)(2,1)}, u32[]{:S(2)}, u32[]{:S(2)}) collective-permute-start(bf16[512,2048]{1,0:T(8,128)(2,1)S(1)} %collective-permute-done.5.rest_0_), channel_id=1, source_target_pairs={{0,4},{4,0},{8,12},{12,8},{16,20},{20,16},{24,28},{28,24},{32,36},... | collective-permute-start | bytes 6291464 | tf_op jit(solution)/shard_map/ppermute | solution.py:393
  35.4 21.8 %copy-start.3 = (bf16[4,128,128]{2,1,0:T(8,128)(2,1)}, bf16[4,128,128]{2,1,0:T(8,128)(2,1)S(1)}, u32[]{:S(2)}) copy-start(bf16[4,128,128]{2,1,0:T(8,128)(2,1)S(1)} %collective-permute-done.1.y1_ref) | copy-start | bytes 393220
  35.4 7.5 %collective-permute-start.2 = (bf16[4,128,128]{2,1,0:T(8,128)(2,1)S(1)}, bf16[4,128,128]{2,1,0:T(8,128)(2,1)S(1)}, u32[]{:S(2)}, u32[]{:S(2)}) collective-permute-start(bf16[4,128,128]{2,1,0:T(8,128)(2,1)S(1)} %add_convert_fusion.2), channel_id=1, source_target_pairs={{0,24},{4,28},{8,16},{12,20},{16,8},{20,12},{24,0},{28,4},{32,56},... | collective-permute-start | bytes 393224 | tf_op jit(solution)/shard_map/ppermute | solution.py:367
  43.0 14.2 %copy-start.4 = (bf16[4,128,128]{2,1,0:T(8,128)(2,1)}, bf16[4,128,128]{2,1,0:T(8,128)(2,1)S(1)}, u32[]{:S(2)}) copy-start(bf16[4,128,128]{2,1,0:T(8,128)(2,1)S(1)} %collective-permute-done.2.y2_ref) | copy-start | bytes 393220
  43.6 5.7 %collective-permute-start.3 = (bf16[4,128,128]{2,1,0:T(8,128)(2,1)}, bf16[4,128,128]{2,1,0:T(8,128)(2,1)}, u32[]{:S(2)}, u32[]{:S(2)}) collective-permute-start(bf16[4,128,128]{2,1,0:T(8,128)(2,1)} %add_convert_fusion.1), channel_id=1, source_target_pairs={{0,32},{4,36},{8,40},{12,44},{16,48},{20,52},{24,56},{28,60},{32,0... | collective-permute-start | bytes 393224 | tf_op jit(solution)/shard_map/ppermute | solution.py:365
  45.7 36.9 %collective-permute-start.8 = (bf16[256,2048]{1,0:T(8,128)(2,1)S(1)}, bf16[256,2048]{1,0:T(8,128)(2,1)}, u32[]{:S(2)}, u32[]{:S(2)}) collective-permute-start(bf16[256,2048]{1,0:T(8,128)(2,1)S(1)} %collective-permute-done.7.rest_2_), channel_id=1, source_target_pairs={{0,4},{4,0},{8,12},{12,8},{16,20},{20,16},{24,28},{28,24},{32,36},... | collective-permute-start | bytes 3145736 | tf_op jit(solution)/shard_map/ppermute | solution.py:393
  51.0 13.0 %collective-permute-start.4 = (bf16[4,128,128]{2,1,0:T(8,128)(2,1)}, bf16[4,128,128]{2,1,0:T(8,128)(2,1)}, u32[]{:S(2)}, u32[]{:S(2)}) collective-permute-start(bf16[4,128,128]{2,1,0:T(8,128)(2,1)} %add_convert_fusion), channel_id=1, source_target_pairs={{0,96},{4,100},{8,104},{12,108},{16,112},{20,116},{24,120},{28,124... | collective-permute-start | bytes 393224 | tf_op jit(solution)/shard_map/ppermute | solution.py:367
  67.0 13.0 %collective-permute-start.11 = (bf16[512,512]{1,0:T(8,128)(2,1)}, bf16[512,512]{1,0:T(8,128)(2,1)}, u32[]{:S(2)}, u32[]{:S(2)}) collective-permute-start(bf16[512,512]{1,0:T(8,128)(2,1)} %get-tuple-element.27), channel_id=1, source_target_pairs={{0,1},{1,2},{2,3},{3,0},{4,7},{5,4},{6,5},{7,6},{8,9},{9,10},{10,1... | collective-permute-start | bytes 1572872 | tf_op jit(solution)/shard_map/ppermute | solution.py:396
  69.7 19.2 %collective-permute-start.9 = (bf16[512,512]{1,0:T(8,128)(2,1)}, bf16[512,512]{1,0:T(8,128)(2,1)}, u32[]{:S(2)}, u32[]{:S(2)}) collective-permute-start(bf16[512,512]{1,0:T(8,128)(2,1)} %finish.6), channel_id=1, source_target_pairs={{0,1},{1,2},{2,3},{3,0},{4,7},{5,4},{6,5},{7,6},{8,9},{9,10},{10,1... | collective-permute-start | bytes 1572872 | tf_op jit(solution)/shard_map/ppermute | solution.py:396
  73.4 19.0 %collective-permute-start.10 = (bf16[512,512]{1,0:T(8,128)(2,1)}, bf16[512,512]{1,0:T(8,128)(2,1)}, u32[]{:S(2)}, u32[]{:S(2)}) collective-permute-start(bf16[512,512]{1,0:T(8,128)(2,1)} %finish.7), channel_id=1, source_target_pairs={{0,3},{1,0},{2,1},{3,2},{4,5},{5,6},{6,7},{7,4},{8,11},{9,8},{10,9... | collective-permute-start | bytes 1572872 | tf_op jit(solution)/shard_map/ppermute | solution.py:396
  79.9 14.6 %collective-permute-start.12 = (bf16[512,512]{1,0:T(8,128)(2,1)}, bf16[512,512]{1,0:T(8,128)(2,1)}, u32[]{:S(2)}, u32[]{:S(2)}) collective-permute-start(bf16[512,512]{1,0:T(8,128)(2,1)} %collective-permute-done.11), channel_id=1, source_target_pairs={{0,1},{1,2},{2,3},{3,0},{4,7},{5,4},{6,5},{7,6},{8,9},{9,10},{10,1... | collective-permute-start | bytes 1572872 | tf_op jit(solution)/shard_map/ppermute | solution.py:396
  82.7 1.6 %copy-start = (bf16[512,2048]{1,0:T(8,128)(2,1)S(1)}, bf16[512,2048]{1,0:T(8,128)(2,1)}, u32[]{:S(2)}) copy-start(bf16[512,2048]{1,0:T(8,128)(2,1)} %w_ref.1) | copy-start | bytes 6291460
  84.2 1.0 %copy-start.1 = (bf16[512,512]{1,0:T(8,128)(2,1)S(1)}, bf16[512,512]{1,0:T(8,128)(2,1)}, u32[]{:S(2)}) copy-start(bf16[512,512]{1,0:T(8,128)(2,1)} %finish.5.n_ref) | copy-start | bytes 1572868

commit v8 on v7

--- a/solution.py
+++ b/solution.py
@@ -198,30 +198,25 @@
 
 
 def start_kernel(
-    head, core, y, x, q_ref, att_ref, core_ref, y1_ref, y2_ref, x1_ref, x2_ref, gain_ref,
-    n_ref, pair_ref,
+    head, core, q_ref, att_ref, core_ref, mine_ref, partner_ref, gain_ref, n_ref, pair_ref
 ):
-    takes = (
-        (core[0] == 1, core_ref),
-        (lax.rem(y[0], 2) == 1, y1_ref),
-        (y[0] >= 2, y2_ref),
-        (lax.rem(x[0], 2) == 1, x1_ref),
-        (x[0] >= 2, x2_ref),
-    )
-    for h in range(core_ref.shape[0]):
+    heads = core_ref.shape[0]
+    half = heads // 2
+    for h in range(heads):
 
         @pl.when(pl.program_id(0) == 0)
         def _():
-            carried = jnp.zeros((DH, DH), F32)
-            for take, ref in takes:
-                carried = carried + jnp.where(take, ref[h].astype(F32), 0.0)
+            carried = jnp.where(core[0] == 1, core_ref[h].astype(F32), 0.0)
+            carried = carried + jnp.where(
+                core[0] == h // half, mine_ref[h % half], partner_ref[h % half]
+            )
             pair_ref[h] = hi_lo(carried)
 
-    for h in range(core_ref.shape[0]):
+    for h in range(heads):
         norm_rows(q_ref, att_ref, pair_ref[h], gain_ref, n_ref, h)
 
 
-def finish_kernel(head, core, y, x, q_ref, att_ref, pair_ref, gain_ref, n_ref):
+def finish_kernel(head, core, q_ref, att_ref, pair_ref, gain_ref, n_ref):
     for h in range(pair_ref.shape[0]):
         norm_rows(q_ref, att_ref, pair_ref[h], gain_ref, n_ref, h)
 
@@ -232,7 +227,7 @@
     per = count // tile
     heads = feats // DH
 
-    def row(i, head, core, y, x):
+    def row(i, head, core):
         to = head[0] + direction * (1 - 2 * core[0]) + shift + parts
         return (lax.rem(to, parts) * per + i, 0)
 
@@ -244,7 +239,7 @@
     return pl.pallas_call(
         start_kernel if first else finish_kernel,
         grid_spec=pltpu.PrefetchScalarGridSpec(
-            num_scalar_prefetch=4,
+            num_scalar_prefetch=2,
             grid=(per,),
             in_specs=[pl.BlockSpec((tile, feats), row), pl.BlockSpec((tile, feats), row)]
             + [whole(a) for a in received]
@@ -377,7 +372,7 @@
     x = seq // 8
     head = lax.axis_index("head")
     core_id = core.astype(jnp.int32).reshape(1)
-    place = [a.astype(jnp.int32).reshape(1) for a in (head, core, y, x)]
+    place = [a.astype(jnp.int32).reshape(1) for a in (head, core)]
 
     def along(direction):
         pairs = []
@@ -406,9 +401,19 @@
     other = swap(tot)
     for piece in range(1, 4):
         att = local_part(q, k, v, pre, att, piece, 4)
-    y1, y2, row = pair_rounds(tot.astype(F32) + other.astype(F32), 2, total)
+    chip = tot.astype(F32) + other.astype(F32)
+    half = chip.shape[0] // 2
+    chip = lax.dynamic_slice_in_dim(chip, core * half, half, 0)
+    y1, y2, row = pair_rounds(chip, 2, total)
     x1, x2, _ = pair_rounds(row, 8, total)
-    received = (other, y1, y2, x1, x2)
+    takes = (
+        (lax.rem(y, 2) == 1, y1),
+        (y >= 2, y2),
+        (lax.rem(x, 2) == 1, x1),
+        (x >= 2, x2),
+    )
+    mine = sum(jnp.where(take, part.astype(F32), 0.0) for take, part in takes)
+    received = (other, mine, swap(mine))
 
     gain = norm_gain.reshape(1, -1)
     nf, pair = finish(place, 0, 2, q, att, received, gain, parts)

time: 100 us -> 98.8 us (0.988)
  the two profiles are of different devices: /device:TPU:0 before, /device:TPU:1 now
where the time goes in v8:
time: 98.8 us; the launch traced here: 97.7 us
  Pallas kernels  52.7 us (53%)
  starting transfers between devices  26.4 us (27%)
  waiting for transfers between devices  12.5 us (13%)
  local copies, waits for them, and re-layouts  5.02 us (5%)
  other arithmetic  1.01 us (1%)
    pallas_call x1, Pallas kernels, project(): pl.pallas_call(qkv_kernel, in_specs=[anywhere] * 2, out_specs=[anywhere]...  20.3 us
    ppermute x6, starting transfers between devices, send(): return lax.ppermute(a, ('seq', 'head'), along(direction))  14.1 us
    pallas_call x4, Pallas kernels, finish(): pl.pallas_call(start_kernel if first else finish_kernel, grid_spec=pltpu....  10.9 us
    pallas_call x3, Pallas kernels, local_part(): pl.pallas_call(local_kernel, grid=(count // tile,), in_specs=[row, row, r...  10.2 us
    pallas_call x1, Pallas kernels, mix_last(): pl.pallas_call(last_kernel, grid_spec=pltpu.PrefetchScalarGridSpec(num_sc...  5.34 us
    ppermute x6, waiting for transfers between devices, send(): return lax.ppermute(a, ('seq', 'head'), along(direction))  5.31 us
    ppermute x2, starting transfers between devices, pair_rounds(): far = lax.ppermute(pair, 'seq', pair_up(4, stride, total, False))  5.29 us
    ppermute x4, starting transfers between devices, swap(): return lax.ppermute(a, 'seq', partner)  4.38 us
  transfers between devices with their start and end apart: 14, of which 7 were waited for; matrix products, arithmetic and copies ran while one was open for 2% of the time, Pallas kernels for 48%

profile of v8, /device:TPU:1, one launch (start us, length us, event | category | flops | bytes accessed | tf_op | source)
XLA Modules:
  0.0 97.7 jit_solution(9402942221758907302)
XLA Ops:
  0.0 4.6 %collective-permute-start.6 = (bf16[512,2048]{1,0:T(8,128)(2,1)}, bf16[512,2048]{1,0:T(8,128)(2,1)S(1)}, u32[]{:S(2)}, u32[]{:S(2)}) collective-permute-start(bf16[512,2048]{1,0:T(8,128)(2,1)} %w_ref.1), channel_id=1, source_target_pairs={{0,1},{1,2},{2,3},{3,0},{4,7},{5,4},{6,5},{7,6},{8,9},{9,10},{10,1... | collective-permute-start | bytes 6291464 | tf_op jit(solution)/shard_map/ppermute | solution.py:391
  4.6 20.3 %project.1 = (bf16[2048,512]{1,0:T(8,128)(2,1)}, bf16[2048,512]{1,0:T(8,128)(2,1)}, bf16[2048,512]{1,0:T(8,128)(2,1)}, bf16[8,4,256,128]{3,2,1,0:T(8,128)(2,1)},...) custom-call(bf16[2048,2048]{1,0:T(8,128)(2,1)} %x_hbm.1, bf16[3,2048,512]{2,1,0:T(8,128)(2,1)} %w_hbm.1), custom_call_target="tpu_custom_call" | custom-call | flops 12884901888 | bytes 14680064 | tf_op jit(solution)/shard_map/project/pallas_call | solution.py:137
  25.0 2.9 %collective-permute-done.6.rest_0_ = bf16[512,2048]{1,0:T(8,128)(2,1)S(1)} collective-permute-done((bf16[512,2048]{1,0:T(8,128)(2,1)}, bf16[512,2048]{1,0:T(8,128)(2,1)S(1)}, u32[]{:S(2)}, u32[]{:S(2)}) %collective-permute-start.6) | collective-permute-done | bytes 2097184 | tf_op jit(solution)/shard_map/ppermute | solution.py:391
  29.0 3.0 %collective-permute-start.8 = (bf16[256,2048]{1,0:T(8,128)(2,1)}, bf16[256,2048]{1,0:T(8,128)(2,1)S(1)}, u32[]{:S(2)}, u32[]{:S(2)}) collective-permute-start(bf16[256,2048]{1,0:T(8,128)(2,1)} %constant_dynamic-slice_fusion), channel_id=1, source_target_pairs={{0,1},{1,2},{2,3},{3,0},{4,7},{5,4},{6,5},{7,6},{8,9},{9,10},{10,1... | collective-permute-start | bytes 3145736 | tf_op jit(solution)/shard_map/ppermute | solution.py:391
  33.4 2.2 %collective-permute-done.1 = bf16[2,128,128]{2,1,0:T(8,128)(2,1)S(1)} collective-permute-done((bf16[2,128,128]{2,1,0:T(8,128)(2,1)S(1)}, bf16[2,128,128]{2,1,0:T(8,128)(2,1)S(1)}, u32[]{:S(2)}, u32[]{:S(2)}) %collective-permute-start.1) | collective-permute-done | bytes 65568 | tf_op jit(solution)/shard_map/ppermute | solution.py:360
  35.6 2.8 %collective-permute-start.2 = (bf16[2,128,128]{2,1,0:T(8,128)(2,1)S(1)}, bf16[2,128,128]{2,1,0:T(8,128)(2,1)S(1)}, u32[]{:S(2)}, u32[]{:S(2)}) collective-permute-start(bf16[2,128,128]{2,1,0:T(8,128)(2,1)S(1)} %fusion.3), channel_id=1, source_target_pairs={{0,24},{4,28},{8,16},{12,20},{16,8},{20,12},{24,0},{28,4},{32,56},... | collective-permute-start | bytes 196616 | tf_op jit(solution)/shard_map/ppermute | solution.py:362
  38.4 2.5 %collective-permute-done.2 = bf16[2,128,128]{2,1,0:T(8,128)(2,1)S(1)} collective-permute-done((bf16[2,128,128]{2,1,0:T(8,128)(2,1)S(1)}, bf16[2,128,128]{2,1,0:T(8,128)(2,1)S(1)}, u32[]{:S(2)}, u32[]{:S(2)}) %collective-permute-start.2) | collective-permute-done | bytes 65568 | tf_op jit(solution)/shard_map/ppermute | solution.py:362
  42.3 2.2 %collective-permute-done.3 = bf16[2,128,128]{2,1,0:T(8,128)(2,1)S(1)} collective-permute-done((bf16[2,128,128]{2,1,0:T(8,128)(2,1)S(1)}, bf16[2,128,128]{2,1,0:T(8,128)(2,1)S(1)}, u32[]{:S(2)}, u32[]{:S(2)}) %collective-permute-start.3) | collective-permute-done | bytes 65568 | tf_op jit(solution)/shard_map/ppermute | solution.py:360
  45.1 2.5 %collective-permute-start.4 = (bf16[2,128,128]{2,1,0:T(8,128)(2,1)S(1)}, bf16[2,128,128]{2,1,0:T(8,128)(2,1)}, u32[]{:S(2)}, u32[]{:S(2)}) collective-permute-start(bf16[2,128,128]{2,1,0:T(8,128)(2,1)S(1)} %fusion.5), channel_id=1, source_target_pairs={{0,96},{4,100},{8,104},{12,108},{16,112},{20,116},{24,120},{28,124... | collective-permute-start | bytes 196616 | tf_op jit(solution)/shard_map/ppermute | solution.py:362
  47.6 1.7 %collective-permute-start.9 = (bf16[256,2048]{1,0:T(8,128)(2,1)S(1)}, bf16[256,2048]{1,0:T(8,128)(2,1)}, u32[]{:S(2)}, u32[]{:S(2)}) collective-permute-start(bf16[256,2048]{1,0:T(8,128)(2,1)S(1)} %collective-permute-done.8.rest_2_), channel_id=1, source_target_pairs={{0,4},{4,0},{8,12},{12,8},{16,20},{20,16},{24,28},{28,24},{32,36},... | collective-permute-start | bytes 3145736 | tf_op jit(solution)/shard_map/ppermute | solution.py:388
  50.5 2.6 %collective-permute-start.5 = (f32[2,128,128]{2,1,0:T(8,128)S(1)}, f32[2,128,128]{2,1,0:T(8,128)S(1)}, u32[]{:S(2)}, u32[]{:S(2)}) collective-permute-start(f32[2,128,128]{2,1,0:T(8,128)S(1)} %fusion.2.mine_ref), channel_id=1, source_target_pairs={{0,4},{4,0},{8,12},{12,8},{16,20},{20,16},{24,28},{28,24},{32,36},... | collective-permute-start | bytes 393224 | tf_op jit(solution)/shard_map/ppermute | solution.py:388
  53.1 3.4 %local_part.3.att_in = f32[2048,512]{1,0:T(8,128)} custom-call(bf16[2048,512]{1,0:T(8,128)(2,1)} %get-tuple-element.18.q_ref, bf16[2048,512]{1,0:T(8,128)(2,1)} %get-tuple-element.19.k_ref, bf16[2048,512]{1,0:T(8,128)(2,1)} %get-tuple-element.20.v_ref, bf16[8,4,256,128]{3,2,1,0:T(8,128)(2,1)} %get-tuple-element.21.pre_ref, ...), custom_call_target="tpu_custom_call", output_to_operand_aliasing={{}: (4, {})} | custom-call | flops 536870912 | bytes 3670016 | tf_op jit(solution)/shard_map/local_part/pallas_call | solution.py:176
  56.5 3.4 %local_part.4.att_in = f32[2048,512]{1,0:T(8,128)} custom-call(bf16[2048,512]{1,0:T(8,128)(2,1)} %get-tuple-element.18.q_ref, bf16[2048,512]{1,0:T(8,128)(2,1)} %get-tuple-element.19.k_ref, bf16[2048,512]{1,0:T(8,128)(2,1)} %get-tuple-element.20.v_ref, bf16[8,4,256,128]{3,2,1,0:T(8,128)(2,1)} %get-tuple-element.21.pre_ref, ...), custom_call_target="tpu_custom_call", output_to_operand_aliasing={{}: (4, {})} | custom-call | flops 536870912 | bytes 3670016 | tf_op jit(solution)/shard_map/local_part/pallas_call | solution.py:176
  59.9 3.4 %local_part.5.att_ref = f32[2048,512]{1,0:T(8,128)} custom-call(bf16[2048,512]{1,0:T(8,128)(2,1)} %get-tuple-element.18.q_ref, bf16[2048,512]{1,0:T(8,128)(2,1)} %get-tuple-element.19.k_ref, bf16[2048,512]{1,0:T(8,128)(2,1)} %get-tuple-element.20.v_ref, bf16[8,4,256,128]{3,2,1,0:T(8,128)(2,1)} %get-tuple-element.21.pre_ref, ...), custom_call_target="tpu_custom_call", output_to_operand_aliasing={{}: (4, {})} | custom-call | flops 536870912 | bytes 3670016 | tf_op jit(solution)/shard_map/local_part/pallas_call | solution.py:176
  63.9 2.8 %finish.4 = (bf16[512,512]{1,0:T(8,128)(2,1)}, bf16[4,256,128]{2,1,0:T(8,128)(2,1)}) custom-call(s32[1]{0:T(128)} %bitcast.1.head, s32[1]{0:T(128)} %bitcast.core, bf16[2048,512]{1,0:T(8,128)(2,1)} %get-tuple-element.18.q_ref, f32[2048,512]{1,0:T(8,128)} %local_part.5.att_ref, bf16[4,128,128]{2,1,0:T(8,128)(2,1)} %copy-done.3, f32[2,128,128]{2,1,0:T(8,128)} %copy-done.2, ...), custom_call_target="tpu_custom_call" | custom-call | flops 134217728 | bytes 2097152 | tf_op jit(solution)/shard_map/finish/pallas_call | solution.py:239
  66.7 2.3 %collective-permute-start.12 = (bf16[512,512]{1,0:T(8,128)(2,1)}, bf16[512,512]{1,0:T(8,128)(2,1)}, u32[]{:S(2)}, u32[]{:S(2)}) collective-permute-start(bf16[512,512]{1,0:T(8,128)(2,1)} %get-tuple-element.27), channel_id=1, source_target_pairs={{0,1},{1,2},{2,3},{3,0},{4,7},{5,4},{6,5},{7,6},{8,9},{9,10},{10,1... | collective-permute-start | bytes 1572872 | tf_op jit(solution)/shard_map/ppermute | solution.py:391
  69.1 2.7 %finish.6 = bf16[512,512]{1,0:T(8,128)(2,1)} custom-call(s32[1]{0:T(128)} %bitcast.1.head, s32[1]{0:T(128)} %bitcast.core, bf16[2048,512]{1,0:T(8,128)(2,1)} %get-tuple-element.18.q_ref, f32[2048,512]{1,0:T(8,128)} %local_part.5.att_ref, bf16[4,256,128]{2,1,0:T(8,128)(2,1)} %get-tuple-element.24.pair_ref, f32[1,512]{1,0:T(1,128)} %bitcast.4), custom_call_target="tpu_custom_call" | custom-call | flops 134217728 | bytes 2097152 | tf_op jit(solution)/shard_map/finish/pallas_call | solution.py:239
  72.3 2.7 %finish.7 = bf16[512,512]{1,0:T(8,128)(2,1)} custom-call(s32[1]{0:T(128)} %bitcast.1.head, s32[1]{0:T(128)} %bitcast.core, bf16[2048,512]{1,0:T(8,128)(2,1)} %get-tuple-element.18.q_ref, f32[2048,512]{1,0:T(8,128)} %local_part.5.att_ref, bf16[4,256,128]{2,1,0:T(8,128)(2,1)} %get-tuple-element.24.pair_ref, f32[1,512]{1,0:T(1,128)} %bitcast.5), custom_call_target="tpu_custom_call" | custom-call | flops 134217728 | bytes 2097152 | tf_op jit(solution)/shard_map/finish/pallas_call | solution.py:239
  76.0 2.7 %collective-permute-start.13 = (bf16[512,512]{1,0:T(8,128)(2,1)}, bf16[512,512]{1,0:T(8,128)(2,1)}, u32[]{:S(2)}, u32[]{:S(2)}) collective-permute-start(bf16[512,512]{1,0:T(8,128)(2,1)} %collective-permute-done.12), channel_id=1, source_target_pairs={{0,1},{1,2},{2,3},{3,0},{4,7},{5,4},{6,5},{7,6},{8,9},{9,10},{10,1... | collective-permute-start | bytes 1572872 | tf_op jit(solution)/shard_map/ppermute | solution.py:391
  78.6 2.7 %finish.5.n_ref = bf16[512,512]{1,0:T(8,128)(2,1)} custom-call(s32[1]{0:T(128)} %bitcast.1.head, s32[1]{0:T(128)} %bitcast.core, bf16[2048,512]{1,0:T(8,128)(2,1)} %get-tuple-element.18.q_ref, f32[2048,512]{1,0:T(8,128)} %local_part.5.att_ref, bf16[4,256,128]{2,1,0:T(8,128)(2,1)} %get-tuple-element.24.pair_ref, f32[1,512]{1,0:T(1,128)} %bitcast.6), custom_call_target="tpu_custom_call" | custom-call | flops 134217728 | bytes 2097152 | tf_op jit(solution)/shard_map/finish/pallas_call | solution.py:239
  84.0 2.5 %mix_own.1 = (f32[512,2048]{1,0:T(8,128)S(1)}, bf16[512,2048]{1,0:T(8,128)(2,1)S(1)}, bf16[512,2048]{1,0:T(8,128)(2,1)S(1)}, bf16[256,2048]{1,0:T(8,128)(2,1)S(1)}, bf16[256,2048]{1,0:T(8,128)(2,1)S(1)}) custom-call(bf16[512,512]{1,0:T(8,128)(2,1)S(1)} %copy-done.1, bf16[512,2048]{1,0:T(8,128)(2,1)S(1)} %copy-done, ...), custom_call_target="tpu_custom_call" | custom-call | flops 1073741824 | bytes 8388608 | tf_op jit(solution)/shard_map/mix_own/pallas_call | solution.py:279
  86.5 3.5 %mix_middle.1.acc_ref = f32[512,2048]{1,0:T(8,128)S(1)} custom-call(f32[512,2048]{1,0:T(8,128)S(1)} %get-tuple-element.25.acc_ref, bf16[512,512]{1,0:T(8,128)(2,1)} %collective-permute-done.10.n_ref, bf16[512,2048]{1,0:T(8,128)(2,1)S(1)} %get-tuple-element.26.w_ref), custom_call_target="tpu_custom_call", output_to_operand_aliasing={{}: (0, {})} | custom-call | flops 1073741824 | bytes 8388608 | tf_op jit(solution)/shard_map/mix_middle/pallas_call | solution.py:305
  90.5 1.9 %collective-permute-done.13.nf = bf16[512,512]{1,0:T(8,128)(2,1)} collective-permute-done((bf16[512,512]{1,0:T(8,128)(2,1)}, bf16[512,512]{1,0:T(8,128)(2,1)}, u32[]{:S(2)}, u32[]{:S(2)}) %collective-permute-start.13) | collective-permute-done | bytes 524320 | tf_op jit(solution)/shard_map/ppermute | solution.py:391
  92.4 5.3 %mix_last.1 = bf16[512,2048]{1,0:T(8,128)(2,1)} custom-call(s32[1]{0:T(128)} %bitcast.core, f32[512,2048]{1,0:T(8,128)S(1)} %mix_middle.1.acc_ref, bf16[512,512]{1,0:T(8,128)(2,1)} %collective-permute-done.11.nb, bf16[512,512]{1,0:T(8,128)(2,1)} %collective-permute-done.13.nf, bf16[512,2048]{1,0:T(8,128)(2,1)S(1)} %get-tuple-element.28.wb, ...), custom_call_target="tpu_custom_call" | custom-call | flops 2147483648 | bytes 8388608 | tf_op jit(solution)/shard_map/mix_last/pallas_call | solution.py:332
  (35 shorter events, 11.1 us)
Async XLA Ops:
  0.0 27.9 %collective-permute-start.6 = (bf16[512,2048]{1,0:T(8,128)(2,1)}, bf16[512,2048]{1,0:T(8,128)(2,1)S(1)}, u32[]{:S(2)}, u32[]{:S(2)}) collective-permute-start(bf16[512,2048]{1,0:T(8,128)(2,1)} %w_ref.1), channel_id=1, source_target_pairs={{0,1},{1,2},{2,3},{3,0},{4,7},{5,4},{6,5},{7,6},{8,9},{9,10},{10,1... | collective-permute-start | bytes 6291464 | tf_op jit(solution)/shard_map/ppermute | solution.py:391
  24.9 7.2 %copy-start.6 = (bf16[4,128,128]{2,1,0:T(8,128)(2,1)S(1)}, bf16[4,128,128]{2,1,0:T(8,128)(2,1)}, u32[]{:S(2)}) copy-start(bf16[4,128,128]{2,1,0:T(8,128)(2,1)} %get-tuple-element.23) | copy-start | bytes 393220
  24.9 7.2 %collective-permute-start = (bf16[4,128,128]{2,1,0:T(8,128)(2,1)}, bf16[4,128,128]{2,1,0:T(8,128)(2,1)S(1)}, u32[]{:S(2)}, u32[]{:S(2)}) collective-permute-start(bf16[4,128,128]{2,1,0:T(8,128)(2,1)} %get-tuple-element.23), channel_id=1, source_target_pairs={{0,4},{4,0},{8,12},{12,8},{16,20},{20,16},{24,28},{28,24},{32,36},... | collective-permute-start | bytes 393224 | tf_op jit(solution)/shard_map/ppermute | solution.py:388
  29.0 18.6 %collective-permute-start.8 = (bf16[256,2048]{1,0:T(8,128)(2,1)}, bf16[256,2048]{1,0:T(8,128)(2,1)S(1)}, u32[]{:S(2)}, u32[]{:S(2)}) collective-permute-start(bf16[256,2048]{1,0:T(8,128)(2,1)} %constant_dynamic-slice_fusion), channel_id=1, source_target_pairs={{0,1},{1,2},{2,3},{3,0},{4,7},{5,4},{6,5},{7,6},{8,9},{9,10},{10,1... | collective-permute-start | bytes 3145736 | tf_op jit(solution)/shard_map/ppermute | solution.py:391
  32.0 24.4 %copy-start.3 = (bf16[4,128,128]{2,1,0:T(8,128)(2,1)}, bf16[4,128,128]{2,1,0:T(8,128)(2,1)S(1)}, u32[]{:S(2)}) copy-start(bf16[4,128,128]{2,1,0:T(8,128)(2,1)S(1)} %collective-permute-done.core_ref) | copy-start | bytes 393220
  32.1 3.5 %collective-permute-start.1 = (bf16[2,128,128]{2,1,0:T(8,128)(2,1)S(1)}, bf16[2,128,128]{2,1,0:T(8,128)(2,1)S(1)}, u32[]{:S(2)}, u32[]{:S(2)}) collective-permute-start(bf16[2,128,128]{2,1,0:T(8,128)(2,1)S(1)} %add_convert_fusion), channel_id=1, source_target_pairs={{0,8},{4,12},{8,0},{12,4},{16,24},{20,28},{24,16},{28,20},{32,40},... | collective-permute-start | bytes 196616 | tf_op jit(solution)/shard_map/ppermute | solution.py:360
  33.4 47.9 %collective-permute-start.7 = (bf16[512,2048]{1,0:T(8,128)(2,1)S(1)}, bf16[512,2048]{1,0:T(8,128)(2,1)}, u32[]{:S(2)}, u32[]{:S(2)}) collective-permute-start(bf16[512,2048]{1,0:T(8,128)(2,1)S(1)} %collective-permute-done.6.rest_0_), channel_id=1, source_target_pairs={{0,4},{4,0},{8,12},{12,8},{16,20},{20,16},{24,28},{28,24},{32,36},... | collective-permute-start | bytes 6291464 | tf_op jit(solution)/shard_map/ppermute | solution.py:388
  35.6 5.3 %collective-permute-start.2 = (bf16[2,128,128]{2,1,0:T(8,128)(2,1)S(1)}, bf16[2,128,128]{2,1,0:T(8,128)(2,1)S(1)}, u32[]{:S(2)}, u32[]{:S(2)}) collective-permute-start(bf16[2,128,128]{2,1,0:T(8,128)(2,1)S(1)} %fusion.3), channel_id=1, source_target_pairs={{0,24},{4,28},{8,16},{12,20},{16,8},{20,12},{24,0},{28,4},{32,56},... | collective-permute-start | bytes 196616 | tf_op jit(solution)/shard_map/ppermute | solution.py:362
  41.0 3.5 %collective-permute-start.3 = (bf16[2,128,128]{2,1,0:T(8,128)(2,1)S(1)}, bf16[2,128,128]{2,1,0:T(8,128)(2,1)S(1)}, u32[]{:S(2)}, u32[]{:S(2)}) collective-permute-start(bf16[2,128,128]{2,1,0:T(8,128)(2,1)S(1)} %fusion.4), channel_id=1, source_target_pairs={{0,32},{4,36},{8,40},{12,44},{16,48},{20,52},{24,56},{28,60},{32,0... | collective-permute-start | bytes 196616 | tf_op jit(solution)/shard_map/ppermute | solution.py:360
  44.5 0.6 copy-start.4
  45.1 4.4 %collective-permute-start.4 = (bf16[2,128,128]{2,1,0:T(8,128)(2,1)S(1)}, bf16[2,128,128]{2,1,0:T(8,128)(2,1)}, u32[]{:S(2)}, u32[]{:S(2)}) collective-permute-start(bf16[2,128,128]{2,1,0:T(8,128)(2,1)S(1)} %fusion.5), channel_id=1, source_target_pairs={{0,96},{4,100},{8,104},{12,108},{16,112},{20,116},{24,120},{28,124... | collective-permute-start | bytes 196616 | tf_op jit(solution)/shard_map/ppermute | solution.py:362
  47.6 33.8 %collective-permute-start.9 = (bf16[256,2048]{1,0:T(8,128)(2,1)S(1)}, bf16[256,2048]{1,0:T(8,128)(2,1)}, u32[]{:S(2)}, u32[]{:S(2)}) collective-permute-start(bf16[256,2048]{1,0:T(8,128)(2,1)S(1)} %collective-permute-done.8.rest_2_), channel_id=1, source_target_pairs={{0,4},{4,0},{8,12},{12,8},{16,20},{20,16},{24,28},{28,24},{32,36},... | collective-permute-start | bytes 3145736 | tf_op jit(solution)/shard_map/ppermute | solution.py:388
  50.4 6.0 %copy-start.2 = (f32[2,128,128]{2,1,0:T(8,128)}, f32[2,128,128]{2,1,0:T(8,128)S(1)}, u32[]{:S(2)}) copy-start(f32[2,128,128]{2,1,0:T(8,128)S(1)} %fusion.2.mine_ref) | copy-start | bytes 393220
  50.5 12.8 %collective-permute-start.5 = (f32[2,128,128]{2,1,0:T(8,128)S(1)}, f32[2,128,128]{2,1,0:T(8,128)S(1)}, u32[]{:S(2)}, u32[]{:S(2)}) collective-permute-start(f32[2,128,128]{2,1,0:T(8,128)S(1)} %fusion.2.mine_ref), channel_id=1, source_target_pairs={{0,4},{4,0},{8,12},{12,8},{16,20},{20,16},{24,28},{28,24},{32,36},... | collective-permute-start | bytes 393224 | tf_op jit(solution)/shard_map/ppermute | solution.py:388
  63.3 0.7 copy-start.5
  66.7 9.2 %collective-permute-start.12 = (bf16[512,512]{1,0:T(8,128)(2,1)}, bf16[512,512]{1,0:T(8,128)(2,1)}, u32[]{:S(2)}, u32[]{:S(2)}) collective-permute-start(bf16[512,512]{1,0:T(8,128)(2,1)} %get-tuple-element.27), channel_id=1, source_target_pairs={{0,1},{1,2},{2,3},{3,0},{4,7},{5,4},{6,5},{7,6},{8,9},{9,10},{10,1... | collective-permute-start | bytes 1572872 | tf_op jit(solution)/shard_map/ppermute | solution.py:391
  71.8 14.7 %collective-permute-start.10 = (bf16[512,512]{1,0:T(8,128)(2,1)}, bf16[512,512]{1,0:T(8,128)(2,1)}, u32[]{:S(2)}, u32[]{:S(2)}) collective-permute-start(bf16[512,512]{1,0:T(8,128)(2,1)} %finish.6), channel_id=1, source_target_pairs={{0,1},{1,2},{2,3},{3,0},{4,7},{5,4},{6,5},{7,6},{8,9},{9,10},{10,1... | collective-permute-start | bytes 1572872 | tf_op jit(solution)/shard_map/ppermute | solution.py:391
  75.0 15.5 %collective-permute-start.11 = (bf16[512,512]{1,0:T(8,128)(2,1)}, bf16[512,512]{1,0:T(8,128)(2,1)}, u32[]{:S(2)}, u32[]{:S(2)}) collective-permute-start(bf16[512,512]{1,0:T(8,128)(2,1)} %finish.7), channel_id=1, source_target_pairs={{0,3},{1,0},{2,1},{3,2},{4,5},{5,6},{6,7},{7,4},{8,11},{9,8},{10,9... | collective-permute-start | bytes 1572872 | tf_op jit(solution)/shard_map/ppermute | solution.py:391
  76.0 16.4 %collective-permute-start.13 = (bf16[512,512]{1,0:T(8,128)(2,1)}, bf16[512,512]{1,0:T(8,128)(2,1)}, u32[]{:S(2)}, u32[]{:S(2)}) collective-permute-start(bf16[512,512]{1,0:T(8,128)(2,1)} %collective-permute-done.12), channel_id=1, source_target_pairs={{0,1},{1,2},{2,3},{3,0},{4,7},{5,4},{6,5},{7,6},{8,9},{9,10},{10,1... | collective-permute-start | bytes 1572872 | tf_op jit(solution)/shard_map/ppermute | solution.py:391
  81.3 1.6 %copy-start = (bf16[512,2048]{1,0:T(8,128)(2,1)S(1)}, bf16[512,2048]{1,0:T(8,128)(2,1)}, u32[]{:S(2)}) copy-start(bf16[512,2048]{1,0:T(8,128)(2,1)} %w_ref.1) | copy-start | bytes 6291460
  82.9 1.0 %copy-start.1 = (bf16[512,512]{1,0:T(8,128)(2,1)S(1)}, bf16[512,512]{1,0:T(8,128)(2,1)}, u32[]{:S(2)}) copy-start(bf16[512,512]{1,0:T(8,128)(2,1)} %finish.5.n_ref) | copy-start | bytes 1572868

commit v9 on v8

--- a/solution.py
+++ b/solution.py
@@ -43,41 +43,45 @@
 
 
 def qkv_kernel(
-    x_hbm, w_hbm, q_hbm, k_hbm, v_hbm, pre_hbm, tot_ref, att_hbm,
-    x, w, q, k, v, pre, att, x_sem, w_sem, out_sem,
+    x_hbm, w_hbm, qkv_hbm, pre_hbm, tot_ref, att_hbm,
+    x, w, qkv, pre, att, x_sem, w_sem, out_sem,
 ):
-    steps = x_sem.shape[0] // 2
+    steps = x_sem.shape[0] - 1
     tile = x.shape[0] // steps
-    width = x.shape[1]
-    half = width // 2
+    half = x.shape[1] // 2
     heads = tot_ref.shape[0]
     blocks = tile // BLK
     inside = att.shape[0] // tile
-
-    def tokens(i, part):
-        at = (pl.ds(i * tile, tile), pl.ds(part * half, half))
-        return pltpu.make_async_copy(x_hbm.at[at], x.at[at], x_sem.at[2 * i + part])
-
-    def weight(which, part):
-        at = pl.ds(part * half, half)
-        return pltpu.make_async_copy(
-            w_hbm.at[which, at], w.at[which, at], w_sem.at[2 * which + part]
+    q, k, v = (qkv.at[which] for which in range(3))
+
+    firsts = []
+    for part in range(2):
+        cut = pl.ds(part * half, half)
+        at = (pl.ds(0, tile), cut)
+        firsts.append(
+            (
+                pltpu.make_async_copy(x_hbm.at[at], x.at[at], x_sem.at[part]),
+                pltpu.make_async_copy(w_hbm.at[1, cut], w.at[1, cut], w_sem.at[part]),
+            )
         )
-
-    for part in range(2):
-        tokens(0, part).start()
-        weight(1, part).start()
-    for which in (2, 0):
-        for part in range(2):
-            weight(which, part).start()
+    weights = {
+        which: pltpu.make_async_copy(w_hbm.at[which], w.at[which], w_sem.at[2 + at])
+        for at, which in enumerate((2, 0))
+    }
+    tokens = []
     for i in range(1, steps):
-        for part in range(2):
-            tokens(i, part).start()
+        at = pl.ds(i * tile, tile)
+        tokens.append(pltpu.make_async_copy(x_hbm.at[at], x.at[at], x_sem.at[1 + i]))
+    for copies in firsts:
+        for copy in copies:
+            copy.start()
+    for copy in (*weights.values(), *tokens):
+        copy.start()
 
     pending = []
 
-    def put(i, source, target, which):
-        copy = pltpu.make_async_copy(source, target, out_sem.at[i, which])
+    def put(source, target):
+        copy = pltpu.make_async_copy(source, target, out_sem.at[len(pending)])
         copy.start()
         pending.append(copy)
 
@@ -86,21 +90,19 @@
         rows = pl.ds(i * tile, tile)
         if i == 0:
             total = None
-            for part in range(2):
-                tokens(0, part).wait()
-                weight(1, part).wait()
+            for part, copies in enumerate(firsts):
+                for copy in copies:
+                    copy.wait()
                 cut = pl.ds(part * half, half)
                 product = dot(x[rows, cut], w[1, cut])
                 total = product if total is None else total + product
             k[rows] = total.astype(BF16)
         else:
-            for part in range(2):
-                tokens(i, part).wait()
+            tokens[i - 1].wait()
             k[rows] = dot(x[rows], w[1]).astype(BF16)
         for which, out in ((2, v), (0, q)):
             if i == 0:
-                for part in range(2):
-                    weight(which, part).wait()
+                weights[which].wait()
             out[rows] = dot(x[rows], w[which]).astype(BF16)
         for b in range(i * blocks, (i + 1) * blocks):
             block = slice(b * BLK, (b + 1) * BLK)
@@ -113,13 +115,12 @@
                 )
             if i < inside:
                 local_block(att, block, q, k, v, pre, b)
-        put(i, q.at[rows], q_hbm.at[rows], 0)
-        put(i, k.at[rows], k_hbm.at[rows], 1)
-        put(i, v.at[rows], v_hbm.at[rows], 2)
+        put(qkv.at[:, rows], qkv_hbm.at[:, rows])
         at = pl.ds(i * blocks, blocks)
-        put(i, pre.at[at], pre_hbm.at[at], 3)
-        if i < inside:
-            put(i, att.at[rows], att_hbm.at[rows], 4)
+        put(pre.at[at], pre_hbm.at[at])
+        if i == inside - 1:
+            at = pl.ds(0, inside * tile)
+            put(att, att_hbm.at[at])
     for h in range(heads):
         tot_ref[h] = state[h].astype(BF16)
     for copy in pending:
@@ -137,9 +138,9 @@
     return pl.pallas_call(
         qkv_kernel,
         in_specs=[anywhere] * 2,
-        out_specs=[anywhere] * 4 + [pl.BlockSpec(memory_space=pltpu.VMEM), anywhere],
-        out_shape=[jax.ShapeDtypeStruct(wide, BF16)] * 3
-        + [
+        out_specs=[anywhere] * 2 + [pl.BlockSpec(memory_space=pltpu.VMEM), anywhere],
+        out_shape=[
+            jax.ShapeDtypeStruct((3, *wide), BF16),
             jax.ShapeDtypeStruct(states, BF16),
             jax.ShapeDtypeStruct((heads, DH, DH), BF16),
             jax.ShapeDtypeStruct(wide, F32),
@@ -147,14 +148,12 @@
         scratch_shapes=[
             pltpu.VMEM((tokens, width), BF16),
             pltpu.VMEM((3, width, feats), BF16),
-            pltpu.VMEM(wide, BF16),
-            pltpu.VMEM(wide, BF16),
-            pltpu.VMEM(wide, BF16),
+            pltpu.VMEM((3, *wide), BF16),
             pltpu.VMEM(states, BF16),
             pltpu.VMEM((inside * tile, feats), F32),
-            pltpu.SemaphoreType.DMA((2 * steps,)),
-            pltpu.SemaphoreType.DMA((6,)),
-            pltpu.SemaphoreType.DMA((steps, 5)),
+            pltpu.SemaphoreType.DMA((steps + 1,)),
+            pltpu.SemaphoreType.DMA((4,)),
+            pltpu.SemaphoreType.DMA((2 * steps + 1,)),
         ],
         cost_estimate=cost(6 * tokens * width * feats, 2 * tokens * width + 6 * width * feats),
         name="project",
@@ -166,18 +165,19 @@
         local_block(att_ref, slice(b * BLK, (b + 1) * BLK), q_ref, k_ref, v_ref, pre_ref, b)
 
 
-def local_part(q, k, v, pre, att, piece, pieces, tile=256):
-    tokens, feats = q.shape
+def local_part(qkv, pre, att, piece, pieces, tile=256):
+    _, tokens, feats = qkv.shape
     heads = feats // DH
     blocks = tile // BLK
     count = tokens // pieces
     start = piece * count // tile
     row = pl.BlockSpec((tile, feats), lambda i: (i + start, 0))
+    part = lambda which: pl.BlockSpec((None, tile, feats), lambda i: (which, i + start, 0))
     return pl.pallas_call(
         local_kernel,
         grid=(count // tile,),
         in_specs=[
-            row, row, row,
+            part(0), part(1), part(2),
             pl.BlockSpec((blocks, heads, 2 * DH, DH), lambda i: (i + start, 0, 0, 0)),
             pl.BlockSpec(memory_space=pl.ANY),
         ],
@@ -186,7 +186,7 @@
         input_output_aliases={4: 0},
         cost_estimate=cost(8 * count * feats * BLK, 14 * count * feats),
         name="local_part",
-    )(q, k, v, pre, att)
+    )(qkv, qkv, qkv, pre, att)
 
 
 def norm_rows(q_ref, att_ref, pair, gain_ref, n_ref, h):
@@ -221,8 +221,8 @@
         norm_rows(q_ref, att_ref, pair_ref[h], gain_ref, n_ref, h)
 
 
-def finish(place, direction, shift, q, att, received, gain, parts, tile=256):
-    tokens, feats = q.shape
+def finish(place, direction, shift, qkv, att, received, gain, parts, tile=256):
+    _, tokens, feats = qkv.shape
     count = tokens // parts
     per = count // tile
     heads = feats // DH
@@ -241,7 +241,10 @@
         grid_spec=pltpu.PrefetchScalarGridSpec(
             num_scalar_prefetch=2,
             grid=(per,),
-            in_specs=[pl.BlockSpec((tile, feats), row), pl.BlockSpec((tile, feats), row)]
+            in_specs=[
+                pl.BlockSpec((None, tile, feats), lambda *at: (0, *row(*at))),
+                pl.BlockSpec((tile, feats), row),
+            ]
             + [whole(a) for a in received]
             + [whole(gain)],
             out_specs=[rows, whole(pair)] if first else rows,
@@ -249,7 +252,7 @@
         out_shape=[normed, pair] if first else normed,
         cost_estimate=cost(2 * count * feats * DH * 2, count * feats * 8),
         name="finish",
-    )(*place, q, att, *received, gain)
+    )(*place, qkv, att, *received, gain)
 
 
 def own_kernel(n_ref, w_ref, *rest):
@@ -315,12 +318,11 @@
     )(acc, normed, weight)
 
 
-def last_kernel(core, acc_ref, nb, nf, wb, mine_ref, other_ref, out_ref):
+def last_kernel(core, acc_ref, nf, mine_ref, other_ref, out_ref):
     half = mine_ref.shape[0]
     mine = pl.multiple_of(core[0] * half, half)
     other = pl.multiple_of((1 - core[0]) * half, half)
-    acc = dot(nb[...], wb[...])
-    acc += dot(nf[:, pl.ds(mine, half)], mine_ref[...])
+    acc = dot(nf[:, pl.ds(mine, half)], mine_ref[...])
     acc += dot(nf[:, pl.ds(other, half)], other_ref[...])
     out_ref[...] = (acc + acc_ref[...]).astype(BF16)
 
@@ -340,7 +342,7 @@
             out_specs=pl.BlockSpec((rows, tile), lambda i, core: (0, i)),
         ),
         out_shape=jax.ShapeDtypeStruct((rows, width), BF16),
-        cost_estimate=cost(4 * rows * feats * width, 8 * rows * width),
+        cost_estimate=cost(2 * rows * feats * width, 8 * rows * width),
         compiler_params=pltpu.CompilerParams(vmem_limit_bytes=24 << 20),
         name="mix_last",
     )(core, acc, *normed, *weights)
@@ -397,10 +399,10 @@
     near_other = swap(near)
     far_other = swap(far)
 
-    q, k, v, pre, tot, att = project(inputs, w_qkv, 1)
+    qkv, pre, tot, att = project(inputs, w_qkv, 1)
     other = swap(tot)
     for piece in range(1, 4):
-        att = local_part(q, k, v, pre, att, piece, 4)
+        att = local_part(qkv, pre, att, piece, 4)
     chip = tot.astype(F32) + other.astype(F32)
     half = chip.shape[0] // 2
     chip = lax.dynamic_slice_in_dim(chip, core * half, half, 0)
@@ -416,15 +418,16 @@
     received = (other, mine, swap(mine))
 
     gain = norm_gain.reshape(1, -1)
-    nf, pair = finish(place, 0, 2, q, att, received, gain, parts)
+    nf, pair = finish(place, 0, 2, qkv, att, received, gain, parts)
     nf = send(nf, 1)
-    na = send(finish(place, 1, 0, q, att, (pair,), gain, parts), 1)
-    nb = send(finish(place, -1, 0, q, att, (pair,), gain, parts), -1)
+    na = send(finish(place, 1, 0, qkv, att, (pair,), gain, parts), 1)
+    nb = send(finish(place, -1, 0, qkv, att, (pair,), gain, parts), -1)
     nf = send(nf, 1)
-    n0 = finish(place, 0, 0, q, att, (pair,), gain, parts)
-    acc, near, *weights = mix_own(n0, w_out, [near, near_other, far, far_other])
+    n0 = finish(place, 0, 0, qkv, att, (pair,), gain, parts)
+    acc, near, near_other, *weights = mix_own(n0, w_out, [near, near_other, far, far_other])
     acc = mix_middle(acc, na, near)
-    return mix_last(core_id, acc, [nb, nf], weights)
+    acc = mix_middle(acc, nb, near_other)
+    return mix_last(core_id, acc, [nf], weights)
 
 
 def solution(mesh):

time: 98.8 us -> 100 us (1.012)
  waiting for transfers between devices: 12.5 us -> 10.3 us
  Pallas kernels: 52.7 us -> 54.7 us
    pallas_call x1 -> x2, Pallas kernels: 3.46 us -> 6.9 us  [mix_middle(): pl.pallas_call(middle_kernel, grid=(width // tile,), in_specs=[column(acc...]
    ppermute x4, starting transfers between devices: 4.38 us -> 6.26 us  [swap(): return lax.ppermute(a, 'seq', partner)]
    ppermute x6, waiting for transfers between devices: 5.31 us -> 4.06 us  [send(): return lax.ppermute(a, ('seq', 'head'), along(direction))]
    pallas_call x1, Pallas kernels: 5.34 us -> 4.22 us  [mix_last(): pl.pallas_call(last_kernel, grid_spec=pltpu.PrefetchScalarGridSpec(num_sc...]
    unnamed x14 -> x12, local copies, waits for them, and re-layouts: 3.88 us -> 3.91 us
  transfers between devices with their start and end apart: 14 -> 14, of which waited for: 7 -> 6; matrix products, arithmetic and copies ran while one was open for 2% -> 3% of each run, Pallas kernels for 48% -> 51%
where the time goes in v9:
time: 100 us; the launch traced here: 99.4 us
  Pallas kernels  54.7 us (55%)
  starting transfers between devices  27.3 us (27%)
  waiting for transfers between devices  10.3 us (10%)
  local copies, waits for them, and re-layouts  5.05 us (5%)
  other arithmetic  1.9 us (2%)
    pallas_call x1, Pallas kernels, project(): pl.pallas_call(qkv_kernel, in_specs=[anywhere] * 2, out_specs=[anywhere]...  19.8 us
    ppermute x6, starting transfers between devices, send(): return lax.ppermute(a, ('seq', 'head'), along(direction))  13.1 us
    pallas_call x4, Pallas kernels, finish(): pl.pallas_call(start_kernel if first else finish_kernel, grid_spec=pltpu....  10.9 us
    pallas_call x3, Pallas kernels, local_part(): pl.pallas_call(local_kernel, grid=(count // tile,), in_specs=[part(0), pa...  10.3 us
    pallas_call x2, Pallas kernels, mix_middle(): pl.pallas_call(middle_kernel, grid=(width // tile,), in_specs=[column(acc...  6.9 us
    ppermute x4, starting transfers between devices, swap(): return lax.ppermute(a, 'seq', partner)  6.26 us
    ppermute x2, starting transfers between devices, pair_rounds(): far = lax.ppermute(pair, 'seq', pair_up(4, stride, total, False))  5.29 us
    ppermute x2, waiting for transfers between devices, pair_rounds(): other = lax.ppermute(value, 'seq', pair_up(4, stride, total, True))  4.31 us
  transfers between devices with their start and end apart: 14, of which 6 were waited for; matrix products, arithmetic and copies ran while one was open for 3% of the time, Pallas kernels for 51%

profile of v9, /device:TPU:1, one launch (start us, length us, event | category | flops | bytes accessed | tf_op | source)
XLA Modules:
  0.0 99.4 jit_solution(6316109744858021052)
XLA Ops:
  0.0 4.6 %collective-permute-start.6 = (bf16[512,2048]{1,0:T(8,128)(2,1)}, bf16[512,2048]{1,0:T(8,128)(2,1)S(1)}, u32[]{:S(2)}, u32[]{:S(2)}) collective-permute-start(bf16[512,2048]{1,0:T(8,128)(2,1)} %w_ref.1), channel_id=1, source_target_pairs={{0,1},{1,2},{2,3},{3,0},{4,7},{5,4},{6,5},{7,6},{8,9},{9,10},{10,1... | collective-permute-start | bytes 6291464 | tf_op jit(solution)/shard_map/ppermute | solution.py:393
  4.6 19.8 %project.1 = (bf16[3,2048,512]{2,1,0:T(8,128)(2,1)}, bf16[8,4,256,128]{3,2,1,0:T(8,128)(2,1)}, bf16[4,128,128]{2,1,0:T(8,128)(2,1)}, f32[2048,512]{1,0:T(8,128)}) custom-call(bf16[2048,2048]{1,0:T(8,128)(2,1)} %x_hbm.1, bf16[3,2048,512]{2,1,0:T(8,128)(2,1)} %w_hbm.1), custom_call_target="tpu_custom_call" | custom-call | flops 12884901888 | bytes 14680064 | tf_op jit(solution)/shard_map/project/pallas_call | solution.py:138
  24.5 3.3 %collective-permute-done.6.rest_0_ = bf16[512,2048]{1,0:T(8,128)(2,1)S(1)} collective-permute-done((bf16[512,2048]{1,0:T(8,128)(2,1)}, bf16[512,2048]{1,0:T(8,128)(2,1)S(1)}, u32[]{:S(2)}, u32[]{:S(2)}) %collective-permute-start.6) | collective-permute-done | bytes 2097184 | tf_op jit(solution)/shard_map/ppermute | solution.py:393
  29.0 3.0 %collective-permute-start.8 = (bf16[256,2048]{1,0:T(8,128)(2,1)}, bf16[256,2048]{1,0:T(8,128)(2,1)S(1)}, u32[]{:S(2)}, u32[]{:S(2)}) collective-permute-start(bf16[256,2048]{1,0:T(8,128)(2,1)} %constant_dynamic-slice_fusion), channel_id=1, source_target_pairs={{0,1},{1,2},{2,3},{3,0},{4,7},{5,4},{6,5},{7,6},{8,9},{9,10},{10,1... | collective-permute-start | bytes 3145736 | tf_op jit(solution)/shard_map/ppermute | solution.py:393
  34.3 2.1 %collective-permute-done.1 = bf16[2,128,128]{2,1,0:T(8,128)(2,1)S(1)} collective-permute-done((bf16[2,128,128]{2,1,0:T(8,128)(2,1)S(1)}, bf16[2,128,128]{2,1,0:T(8,128)(2,1)S(1)}, u32[]{:S(2)}, u32[]{:S(2)}) %collective-permute-start.1) | collective-permute-done | bytes 65568 | tf_op jit(solution)/shard_map/ppermute | solution.py:362
  36.5 2.8 %collective-permute-start.2 = (bf16[2,128,128]{2,1,0:T(8,128)(2,1)S(1)}, bf16[2,128,128]{2,1,0:T(8,128)(2,1)S(1)}, u32[]{:S(2)}, u32[]{:S(2)}) collective-permute-start(bf16[2,128,128]{2,1,0:T(8,128)(2,1)S(1)} %fusion.3), channel_id=1, source_target_pairs={{0,24},{4,28},{8,16},{12,20},{16,8},{20,12},{24,0},{28,4},{32,56},... | collective-permute-start | bytes 196616 | tf_op jit(solution)/shard_map/ppermute | solution.py:364
  39.3 2.0 %collective-permute-done.2 = bf16[2,128,128]{2,1,0:T(8,128)(2,1)S(1)} collective-permute-done((bf16[2,128,128]{2,1,0:T(8,128)(2,1)S(1)}, bf16[2,128,128]{2,1,0:T(8,128)(2,1)S(1)}, u32[]{:S(2)}, u32[]{:S(2)}) %collective-permute-start.2) | collective-permute-done | bytes 65568 | tf_op jit(solution)/shard_map/ppermute | solution.py:364
  42.6 2.2 %collective-permute-done.3 = bf16[2,128,128]{2,1,0:T(8,128)(2,1)S(1)} collective-permute-done((bf16[2,128,128]{2,1,0:T(8,128)(2,1)S(1)}, bf16[2,128,128]{2,1,0:T(8,128)(2,1)S(1)}, u32[]{:S(2)}, u32[]{:S(2)}) %collective-permute-start.3) | collective-permute-done | bytes 65568 | tf_op jit(solution)/shard_map/ppermute | solution.py:362
  45.4 2.5 %collective-permute-start.4 = (bf16[2,128,128]{2,1,0:T(8,128)(2,1)S(1)}, bf16[2,128,128]{2,1,0:T(8,128)(2,1)}, u32[]{:S(2)}, u32[]{:S(2)}) collective-permute-start(bf16[2,128,128]{2,1,0:T(8,128)(2,1)S(1)} %fusion.5), channel_id=1, source_target_pairs={{0,96},{4,100},{8,104},{12,108},{16,112},{20,116},{24,120},{28,124... | collective-permute-start | bytes 196616 | tf_op jit(solution)/shard_map/ppermute | solution.py:364
  47.9 3.3 %collective-permute-start.9 = (bf16[256,2048]{1,0:T(8,128)(2,1)S(1)}, bf16[256,2048]{1,0:T(8,128)(2,1)}, u32[]{:S(2)}, u32[]{:S(2)}) collective-permute-start(bf16[256,2048]{1,0:T(8,128)(2,1)S(1)} %collective-permute-done.8.rest_2_), channel_id=1, source_target_pairs={{0,4},{4,0},{8,12},{12,8},{16,20},{20,16},{24,28},{28,24},{32,36},... | collective-permute-start | bytes 3145736 | tf_op jit(solution)/shard_map/ppermute | solution.py:390
  52.1 2.9 %collective-permute-start.5 = (f32[2,128,128]{2,1,0:T(8,128)S(1)}, f32[2,128,128]{2,1,0:T(8,128)S(1)}, u32[]{:S(2)}, u32[]{:S(2)}) collective-permute-start(f32[2,128,128]{2,1,0:T(8,128)S(1)} %fusion.2.mine_ref), channel_id=1, source_target_pairs={{0,4},{4,0},{8,12},{12,8},{16,20},{20,16},{24,28},{28,24},{32,36},... | collective-permute-start | bytes 393224 | tf_op jit(solution)/shard_map/ppermute | solution.py:390
  55.0 3.4 %local_part.3.att_in = f32[2048,512]{1,0:T(8,128)} custom-call(bf16[3,2048,512]{2,1,0:T(8,128)(2,1)} %get-tuple-element.16.q_ref.k_ref.v_ref, bf16[3,2048,512]{2,1,0:T(8,128)(2,1)} %get-tuple-element.16.q_ref.k_ref.v_ref, bf16[3,2048,512]{2,1,0:T(8,128)(2,1)} %get-tuple-element.16.q_ref.k_ref.v_ref, ...), custom_call_target="tpu_custom_call", output_to_operand_aliasing={{}: (4, {})} | custom-call | flops 536870912 | bytes 3670016 | tf_op jit(solution)/shard_map/local_part/pallas_call | solution.py:176
  58.4 3.4 %local_part.4.att_in = f32[2048,512]{1,0:T(8,128)} custom-call(bf16[3,2048,512]{2,1,0:T(8,128)(2,1)} %get-tuple-element.16.q_ref.k_ref.v_ref, bf16[3,2048,512]{2,1,0:T(8,128)(2,1)} %get-tuple-element.16.q_ref.k_ref.v_ref, bf16[3,2048,512]{2,1,0:T(8,128)(2,1)} %get-tuple-element.16.q_ref.k_ref.v_ref, ...), custom_call_target="tpu_custom_call", output_to_operand_aliasing={{}: (4, {})} | custom-call | flops 536870912 | bytes 3670016 | tf_op jit(solution)/shard_map/local_part/pallas_call | solution.py:176
  61.8 3.4 %local_part.5.att_ref = f32[2048,512]{1,0:T(8,128)} custom-call(bf16[3,2048,512]{2,1,0:T(8,128)(2,1)} %get-tuple-element.16.q_ref.k_ref.v_ref, bf16[3,2048,512]{2,1,0:T(8,128)(2,1)} %get-tuple-element.16.q_ref.k_ref.v_ref, bf16[3,2048,512]{2,1,0:T(8,128)(2,1)} %get-tuple-element.16.q_ref.k_ref.v_ref, ...), custom_call_target="tpu_custom_call", output_to_operand_aliasing={{}: (4, {})} | custom-call | flops 536870912 | bytes 3670016 | tf_op jit(solution)/shard_map/local_part/pallas_call | solution.py:176
  65.9 2.8 %finish.4 = (bf16[512,512]{1,0:T(8,128)(2,1)}, bf16[4,256,128]{2,1,0:T(8,128)(2,1)}) custom-call(s32[1]{0:T(128)} %bitcast.1.head, s32[1]{0:T(128)} %bitcast.core, bf16[3,2048,512]{2,1,0:T(8,128)(2,1)} %get-tuple-element.16.q_ref.k_ref.v_ref, f32[2048,512]{1,0:T(8,128)} %local_part.5.att_ref, bf16[4,128,128]{2,1,0:T(8,128)(2,1)} %copy-done.3, ...), custom_call_target="tpu_custom_call" | custom-call | flops 134217728 | bytes 2097152 | tf_op jit(solution)/shard_map/finish/pallas_call | solution.py:239
  70.3 2.7 %finish.6 = bf16[512,512]{1,0:T(8,128)(2,1)} custom-call(s32[1]{0:T(128)} %bitcast.1.head, s32[1]{0:T(128)} %bitcast.core, bf16[3,2048,512]{2,1,0:T(8,128)(2,1)} %get-tuple-element.16.q_ref.k_ref.v_ref, f32[2048,512]{1,0:T(8,128)} %local_part.5.att_ref, bf16[4,256,128]{2,1,0:T(8,128)(2,1)} %get-tuple-element.20.pair_ref, f32[1,512]{1,0:T(1,128)} %bitcast.4), custom_call_target="tpu_custom_call" | custom-call | flops 134217728 | bytes 2097152 | tf_op jit(solution)/shard_map/finish/pallas_call | solution.py:239
  73.6 2.7 %finish.7 = bf16[512,512]{1,0:T(8,128)(2,1)} custom-call(s32[1]{0:T(128)} %bitcast.1.head, s32[1]{0:T(128)} %bitcast.core, bf16[3,2048,512]{2,1,0:T(8,128)(2,1)} %get-tuple-element.16.q_ref.k_ref.v_ref, f32[2048,512]{1,0:T(8,128)} %local_part.5.att_ref, bf16[4,256,128]{2,1,0:T(8,128)(2,1)} %get-tuple-element.20.pair_ref, f32[1,512]{1,0:T(1,128)} %bitcast.5), custom_call_target="tpu_custom_call" | custom-call | flops 134217728 | bytes 2097152 | tf_op jit(solution)/shard_map/finish/pallas_call | solution.py:239
  77.4 2.5 %collective-permute-start.13 = (bf16[512,512]{1,0:T(8,128)(2,1)}, bf16[512,512]{1,0:T(8,128)(2,1)}, u32[]{:S(2)}, u32[]{:S(2)}) collective-permute-start(bf16[512,512]{1,0:T(8,128)(2,1)} %collective-permute-done.12), channel_id=1, source_target_pairs={{0,1},{1,2},{2,3},{3,0},{4,7},{5,4},{6,5},{7,6},{8,9},{9,10},{10,1... | collective-permute-start | bytes 1572872 | tf_op jit(solution)/shard_map/ppermute | solution.py:393
  79.9 2.7 %finish.5.n_ref = bf16[512,512]{1,0:T(8,128)(2,1)} custom-call(s32[1]{0:T(128)} %bitcast.1.head, s32[1]{0:T(128)} %bitcast.core, bf16[3,2048,512]{2,1,0:T(8,128)(2,1)} %get-tuple-element.16.q_ref.k_ref.v_ref, f32[2048,512]{1,0:T(8,128)} %local_part.5.att_ref, bf16[4,256,128]{2,1,0:T(8,128)(2,1)} %get-tuple-element.20.pair_ref, f32[1,512]{1,0:T(1,128)} %bitcast.6), custom_call_target="tpu_custom_call" | custom-call | flops 134217728 | bytes 2097152 | tf_op jit(solution)/shard_map/finish/pallas_call | solution.py:239
  82.6 1.6 %copy-done = bf16[512,2048]{1,0:T(8,128)(2,1)S(1)} copy-done((bf16[512,2048]{1,0:T(8,128)(2,1)S(1)}, bf16[512,2048]{1,0:T(8,128)(2,1)}, u32[]{:S(2)}) %copy-start) | copy-done | bytes 2097176
  85.2 2.5 %mix_own.1 = (f32[512,2048]{1,0:T(8,128)S(1)}, bf16[512,2048]{1,0:T(8,128)(2,1)S(1)}, bf16[512,2048]{1,0:T(8,128)(2,1)S(1)}, bf16[256,2048]{1,0:T(8,128)(2,1)S(1)}, bf16[256,2048]{1,0:T(8,128)(2,1)S(1)}) custom-call(bf16[512,512]{1,0:T(8,128)(2,1)S(1)} %copy-done.1, bf16[512,2048]{1,0:T(8,128)(2,1)S(1)} %copy-done, ...), custom_call_target="tpu_custom_call" | custom-call | flops 1073741824 | bytes 8388608 | tf_op jit(solution)/shard_map/mix_own/pallas_call | solution.py:282
  87.8 3.5 %mix_middle.2.acc_ref = f32[512,2048]{1,0:T(8,128)S(1)} custom-call(f32[512,2048]{1,0:T(8,128)S(1)} %get-tuple-element.21.acc_ref, bf16[512,512]{1,0:T(8,128)(2,1)} %collective-permute-done.10.n_ref, bf16[512,2048]{1,0:T(8,128)(2,1)S(1)} %get-tuple-element.22.w_ref), custom_call_target="tpu_custom_call", output_to_operand_aliasing={{}: (0, {})} | custom-call | flops 1073741824 | bytes 8388608 | tf_op jit(solution)/shard_map/mix_middle/pallas_call | solution.py:308
  91.7 3.4 %mix_middle.3.acc_ref = f32[512,2048]{1,0:T(8,128)S(1)} custom-call(f32[512,2048]{1,0:T(8,128)S(1)} %mix_middle.2.acc_ref, bf16[512,512]{1,0:T(8,128)(2,1)} %collective-permute-done.11.n_ref, bf16[512,2048]{1,0:T(8,128)(2,1)S(1)} %get-tuple-element.23.w_ref), custom_call_target="tpu_custom_call", output_to_operand_aliasing={{}: (0, {})} | custom-call | flops 1073741824 | bytes 8388608 | tf_op jit(solution)/shard_map/mix_middle/pallas_call | solution.py:308
  95.2 4.2 %mix_last.1 = bf16[512,2048]{1,0:T(8,128)(2,1)} custom-call(s32[1]{0:T(128)} %bitcast.core, f32[512,2048]{1,0:T(8,128)S(1)} %mix_middle.3.acc_ref, bf16[512,512]{1,0:T(8,128)(2,1)} %collective-permute-done.13.nf, bf16[256,2048]{1,0:T(8,128)(2,1)S(1)} %get-tuple-element.25.mine_ref, bf16[256,2048]{1,0:T(8,128)(2,1)S(1)} %get-tuple-element.26.other_ref), custom_call_target="tpu_custom_call" | custom-call | flops 1073741824 | bytes 8388608 | tf_op jit(solution)/shard_map/mix_last/pallas_call | solution.py:334
  (34 shorter events, 11.9 us)
Async XLA Ops:
  0.0 27.9 %collective-permute-start.6 = (bf16[512,2048]{1,0:T(8,128)(2,1)}, bf16[512,2048]{1,0:T(8,128)(2,1)S(1)}, u32[]{:S(2)}, u32[]{:S(2)}) collective-permute-start(bf16[512,2048]{1,0:T(8,128)(2,1)} %w_ref.1), channel_id=1, source_target_pairs={{0,1},{1,2},{2,3},{3,0},{4,7},{5,4},{6,5},{7,6},{8,9},{9,10},{10,1... | collective-permute-start | bytes 6291464 | tf_op jit(solution)/shard_map/ppermute | solution.py:393
  24.4 7.6 %collective-permute-start = (bf16[4,128,128]{2,1,0:T(8,128)(2,1)}, bf16[4,128,128]{2,1,0:T(8,128)(2,1)S(1)}, u32[]{:S(2)}, u32[]{:S(2)}) collective-permute-start(bf16[4,128,128]{2,1,0:T(8,128)(2,1)} %get-tuple-element.19), channel_id=1, source_target_pairs={{0,4},{4,0},{8,12},{12,8},{16,20},{20,16},{24,28},{28,24},{32,36},... | collective-permute-start | bytes 393224 | tf_op jit(solution)/shard_map/ppermute | solution.py:390
  29.0 18.9 %collective-permute-start.8 = (bf16[256,2048]{1,0:T(8,128)(2,1)}, bf16[256,2048]{1,0:T(8,128)(2,1)S(1)}, u32[]{:S(2)}, u32[]{:S(2)}) collective-permute-start(bf16[256,2048]{1,0:T(8,128)(2,1)} %constant_dynamic-slice_fusion), channel_id=1, source_target_pairs={{0,1},{1,2},{2,3},{3,0},{4,7},{5,4},{6,5},{7,6},{8,9},{9,10},{10,1... | collective-permute-start | bytes 3145736 | tf_op jit(solution)/shard_map/ppermute | solution.py:393
  32.0 50.6 %collective-permute-start.7 = (bf16[512,2048]{1,0:T(8,128)(2,1)S(1)}, bf16[512,2048]{1,0:T(8,128)(2,1)}, u32[]{:S(2)}, u32[]{:S(2)}) collective-permute-start(bf16[512,2048]{1,0:T(8,128)(2,1)S(1)} %collective-permute-done.6.rest_0_), channel_id=1, source_target_pairs={{0,4},{4,0},{8,12},{12,8},{16,20},{20,16},{24,28},{28,24},{32,36},... | collective-permute-start | bytes 6291464 | tf_op jit(solution)/shard_map/ppermute | solution.py:390
  32.0 26.4 %copy-start.3 = (bf16[4,128,128]{2,1,0:T(8,128)(2,1)}, bf16[4,128,128]{2,1,0:T(8,128)(2,1)S(1)}, u32[]{:S(2)}) copy-start(bf16[4,128,128]{2,1,0:T(8,128)(2,1)S(1)} %collective-permute-done.core_ref) | copy-start | bytes 393220
  33.0 3.5 %collective-permute-start.1 = (bf16[2,128,128]{2,1,0:T(8,128)(2,1)S(1)}, bf16[2,128,128]{2,1,0:T(8,128)(2,1)S(1)}, u32[]{:S(2)}, u32[]{:S(2)}) collective-permute-start(bf16[2,128,128]{2,1,0:T(8,128)(2,1)S(1)} %add_convert_fusion), channel_id=1, source_target_pairs={{0,8},{4,12},{8,0},{12,4},{16,24},{20,28},{24,16},{28,20},{32,40},... | collective-permute-start | bytes 196616 | tf_op jit(solution)/shard_map/ppermute | solution.py:362
  36.5 4.8 %collective-permute-start.2 = (bf16[2,128,128]{2,1,0:T(8,128)(2,1)S(1)}, bf16[2,128,128]{2,1,0:T(8,128)(2,1)S(1)}, u32[]{:S(2)}, u32[]{:S(2)}) collective-permute-start(bf16[2,128,128]{2,1,0:T(8,128)(2,1)S(1)} %fusion.3), channel_id=1, source_target_pairs={{0,24},{4,28},{8,16},{12,20},{16,8},{20,12},{24,0},{28,4},{32,56},... | collective-permute-start | bytes 196616 | tf_op jit(solution)/shard_map/ppermute | solution.py:364
  41.3 3.5 %collective-permute-start.3 = (bf16[2,128,128]{2,1,0:T(8,128)(2,1)S(1)}, bf16[2,128,128]{2,1,0:T(8,128)(2,1)S(1)}, u32[]{:S(2)}, u32[]{:S(2)}) collective-permute-start(bf16[2,128,128]{2,1,0:T(8,128)(2,1)S(1)} %fusion.4), channel_id=1, source_target_pairs={{0,32},{4,36},{8,40},{12,44},{16,48},{20,52},{24,56},{28,60},{32,0... | collective-permute-start | bytes 196616 | tf_op jit(solution)/shard_map/ppermute | solution.py:362
  44.8 0.6 copy-start.4
  45.4 5.8 %collective-permute-start.4 = (bf16[2,128,128]{2,1,0:T(8,128)(2,1)S(1)}, bf16[2,128,128]{2,1,0:T(8,128)(2,1)}, u32[]{:S(2)}, u32[]{:S(2)}) collective-permute-start(bf16[2,128,128]{2,1,0:T(8,128)(2,1)S(1)} %fusion.5), channel_id=1, source_target_pairs={{0,96},{4,100},{8,104},{12,108},{16,112},{20,116},{24,120},{28,124... | collective-permute-start | bytes 196616 | tf_op jit(solution)/shard_map/ppermute | solution.py:364
  47.9 34.7 %collective-permute-start.9 = (bf16[256,2048]{1,0:T(8,128)(2,1)S(1)}, bf16[256,2048]{1,0:T(8,128)(2,1)}, u32[]{:S(2)}, u32[]{:S(2)}) collective-permute-start(bf16[256,2048]{1,0:T(8,128)(2,1)S(1)} %collective-permute-done.8.rest_2_), channel_id=1, source_target_pairs={{0,4},{4,0},{8,12},{12,8},{16,20},{20,16},{24,28},{28,24},{32,36},... | collective-permute-start | bytes 3145736 | tf_op jit(solution)/shard_map/ppermute | solution.py:390
  52.1 6.3 %copy-start.2 = (f32[2,128,128]{2,1,0:T(8,128)}, f32[2,128,128]{2,1,0:T(8,128)S(1)}, u32[]{:S(2)}) copy-start(f32[2,128,128]{2,1,0:T(8,128)S(1)} %fusion.2.mine_ref) | copy-start | bytes 393220
  52.1 13.2 %collective-permute-start.5 = (f32[2,128,128]{2,1,0:T(8,128)S(1)}, f32[2,128,128]{2,1,0:T(8,128)S(1)}, u32[]{:S(2)}, u32[]{:S(2)}) collective-permute-start(f32[2,128,128]{2,1,0:T(8,128)S(1)} %fusion.2.mine_ref), channel_id=1, source_target_pairs={{0,4},{4,0},{8,12},{12,8},{16,20},{20,16},{24,28},{28,24},{32,36},... | collective-permute-start | bytes 393224 | tf_op jit(solution)/shard_map/ppermute | solution.py:390
  65.3 0.7 copy-start.5
  68.8 8.6 %collective-permute-start.12 = (bf16[512,512]{1,0:T(8,128)(2,1)}, bf16[512,512]{1,0:T(8,128)(2,1)}, u32[]{:S(2)}, u32[]{:S(2)}) collective-permute-start(bf16[512,512]{1,0:T(8,128)(2,1)} %get-tuple-element.24), channel_id=1, source_target_pairs={{0,1},{1,2},{2,3},{3,0},{4,7},{5,4},{6,5},{7,6},{8,9},{9,10},{10,1... | collective-permute-start | bytes 1572872 | tf_op jit(solution)/shard_map/ppermute | solution.py:393
  73.0 14.7 %collective-permute-start.10 = (bf16[512,512]{1,0:T(8,128)(2,1)}, bf16[512,512]{1,0:T(8,128)(2,1)}, u32[]{:S(2)}, u32[]{:S(2)}) collective-permute-start(bf16[512,512]{1,0:T(8,128)(2,1)} %finish.6), channel_id=1, source_target_pairs={{0,1},{1,2},{2,3},{3,0},{4,7},{5,4},{6,5},{7,6},{8,9},{9,10},{10,1... | collective-permute-start | bytes 1572872 | tf_op jit(solution)/shard_map/ppermute | solution.py:393
  76.3 15.5 %collective-permute-start.11 = (bf16[512,512]{1,0:T(8,128)(2,1)}, bf16[512,512]{1,0:T(8,128)(2,1)}, u32[]{:S(2)}, u32[]{:S(2)}) collective-permute-start(bf16[512,512]{1,0:T(8,128)(2,1)} %finish.7), channel_id=1, source_target_pairs={{0,3},{1,0},{2,1},{3,2},{4,5},{5,6},{6,7},{7,4},{8,11},{9,8},{10,9... | collective-permute-start | bytes 1572872 | tf_op jit(solution)/shard_map/ppermute | solution.py:393
  77.4 17.8 %collective-permute-start.13 = (bf16[512,512]{1,0:T(8,128)(2,1)}, bf16[512,512]{1,0:T(8,128)(2,1)}, u32[]{:S(2)}, u32[]{:S(2)}) collective-permute-start(bf16[512,512]{1,0:T(8,128)(2,1)} %collective-permute-done.12), channel_id=1, source_target_pairs={{0,1},{1,2},{2,3},{3,0},{4,7},{5,4},{6,5},{7,6},{8,9},{9,10},{10,1... | collective-permute-start | bytes 1572872 | tf_op jit(solution)/shard_map/ppermute | solution.py:393
  82.6 1.6 %copy-start = (bf16[512,2048]{1,0:T(8,128)(2,1)S(1)}, bf16[512,2048]{1,0:T(8,128)(2,1)}, u32[]{:S(2)}) copy-start(bf16[512,2048]{1,0:T(8,128)(2,1)} %w_ref.1) | copy-start | bytes 6291460
  84.2 1.0 %copy-start.1 = (bf16[512,512]{1,0:T(8,128)(2,1)S(1)}, bf16[512,512]{1,0:T(8,128)(2,1)}, u32[]{:S(2)}) copy-start(bf16[512,512]{1,0:T(8,128)(2,1)} %finish.5.n_ref) | copy-start | bytes 1572868

commit v10 on v9

--- a/solution.py
+++ b/solution.py
@@ -46,17 +46,18 @@
     x_hbm, w_hbm, qkv_hbm, pre_hbm, tot_ref, att_hbm,
     x, w, qkv, pre, att, x_sem, w_sem, out_sem,
 ):
-    steps = x_sem.shape[0] - 1
+    cuts = w_sem.shape[0] - 2
+    steps = x_sem.shape[0] - cuts + 1
     tile = x.shape[0] // steps
-    half = x.shape[1] // 2
+    depth = x.shape[1] // cuts
     heads = tot_ref.shape[0]
     blocks = tile // BLK
     inside = att.shape[0] // tile
     q, k, v = (qkv.at[which] for which in range(3))
 
     firsts = []
-    for part in range(2):
-        cut = pl.ds(part * half, half)
+    for part in range(cuts):
+        cut = pl.ds(part * depth, depth)
         at = (pl.ds(0, tile), cut)
         firsts.append(
             (
@@ -65,13 +66,13 @@
             )
         )
     weights = {
-        which: pltpu.make_async_copy(w_hbm.at[which], w.at[which], w_sem.at[2 + at])
+        which: pltpu.make_async_copy(w_hbm.at[which], w.at[which], w_sem.at[cuts + at])
         for at, which in enumerate((2, 0))
     }
     tokens = []
     for i in range(1, steps):
         at = pl.ds(i * tile, tile)
-        tokens.append(pltpu.make_async_copy(x_hbm.at[at], x.at[at], x_sem.at[1 + i]))
+        tokens.append(pltpu.make_async_copy(x_hbm.at[at], x.at[at], x_sem.at[cuts - 1 + i]))
     for copies in firsts:
         for copy in copies:
             copy.start()
@@ -93,7 +94,7 @@
             for part, copies in enumerate(firsts):
                 for copy in copies:
                     copy.wait()
-                cut = pl.ds(part * half, half)
+                cut = pl.ds(part * depth, depth)
                 product = dot(x[rows, cut], w[1, cut])
                 total = product if total is None else total + product
             k[rows] = total.astype(BF16)
@@ -127,7 +128,7 @@
         copy.wait()
 
 
-def project(x, w_qkv, inside, tile=512):
+def project(x, w_qkv, inside, tile=512, cuts=2):
     tokens, width = x.shape
     feats = w_qkv.shape[2]
     heads = feats // DH
@@ -151,8 +152,8 @@
             pltpu.VMEM((3, *wide), BF16),
             pltpu.VMEM(states, BF16),
             pltpu.VMEM((inside * tile, feats), F32),
-            pltpu.SemaphoreType.DMA((steps + 1,)),
-            pltpu.SemaphoreType.DMA((4,)),
+            pltpu.SemaphoreType.DMA((steps - 1 + cuts,)),
+            pltpu.SemaphoreType.DMA((2 + cuts,)),
             pltpu.SemaphoreType.DMA((2 * steps + 1,)),
         ],
         cost_estimate=cost(6 * tokens * width * feats, 2 * tokens * width + 6 * width * feats),
@@ -301,7 +302,7 @@
     out_ref[...] = acc_ref[...] + dot(n_ref[...], w_ref[...])
 
 
-def mix_middle(acc, normed, weight, tile=512):
+def mix_middle(acc, normed, weight, tile=1024):
     rows, feats = normed.shape
     width = acc.shape[1]
     column = lambda a: pl.BlockSpec((a.shape[0], tile), lambda i: (0, i))
@@ -327,7 +328,7 @@
     out_ref[...] = (acc + acc_ref[...]).astype(BF16)
 
 
-def mix_last(core, acc, normed, weights, tile=512):
+def mix_last(core, acc, normed, weights, tile=2048):
     rows, feats = normed[0].shape
     width = acc.shape[1]
     column = lambda a: pl.BlockSpec((a.shape[0], tile), lambda i, core: (0, i))

time: 100 us -> 99.2 us (level)
  Pallas kernels: 54.7 us -> 53.2 us
  transfers between devices with their start and end apart: 14 -> 14, of which waited for: 6 -> 6; matrix products, arithmetic and copies ran while one was open for 3% -> 3% of each run, Pallas kernels for 51% -> 50%
where the time goes in v10:
time: 99.2 us; the launch traced here: 98.4 us
  Pallas kernels  53.2 us (54%)
  starting transfers between devices  27.3 us (28%)
  waiting for transfers between devices  10.8 us (11%)
  local copies, waits for them, and re-layouts  5.05 us (5%)
  other arithmetic  1.9 us (2%)
    pallas_call x1, Pallas kernels, project(): pl.pallas_call(qkv_kernel, in_specs=[anywhere] * 2, out_specs=[anywhere]...  19.8 us
    ppermute x6, starting transfers between devices, send(): return lax.ppermute(a, ('seq', 'head'), along(direction))  13.1 us
    pallas_call x4, Pallas kernels, finish(): pl.pallas_call(start_kernel if first else finish_kernel, grid_spec=pltpu....  10.9 us
    pallas_call x3, Pallas kernels, local_part(): pl.pallas_call(local_kernel, grid=(count // tile,), in_specs=[part(0), pa...  10.3 us
    ppermute x4, starting transfers between devices, swap(): return lax.ppermute(a, 'seq', partner)  6.26 us
    pallas_call x2, Pallas kernels, mix_middle(): pl.pallas_call(middle_kernel, grid=(width // tile,), in_specs=[column(acc...  5.97 us
    ppermute x2, starting transfers between devices, pair_rounds(): far = lax.ppermute(pair, 'seq', pair_up(4, stride, total, False))  5.29 us
    ppermute x6, waiting for transfers between devices, send(): return lax.ppermute(a, ('seq', 'head'), along(direction))  4.52 us
  transfers between devices with their start and end apart: 14, of which 6 were waited for; matrix products, arithmetic and copies ran while one was open for 3% of the time, Pallas kernels for 50%

profile of v10, /device:TPU:1, one launch (start us, length us, event | category | flops | bytes accessed | tf_op | source)
XLA Modules:
  0.0 98.4 jit_solution(13756323686556296706)
XLA Ops:
  0.0 4.6 %collective-permute-start.6 = (bf16[512,2048]{1,0:T(8,128)(2,1)}, bf16[512,2048]{1,0:T(8,128)(2,1)S(1)}, u32[]{:S(2)}, u32[]{:S(2)}) collective-permute-start(bf16[512,2048]{1,0:T(8,128)(2,1)} %w_ref.1), channel_id=1, source_target_pairs={{0,1},{1,2},{2,3},{3,0},{4,7},{5,4},{6,5},{7,6},{8,9},{9,10},{10,1... | collective-permute-start | bytes 6291464 | tf_op jit(solution)/shard_map/ppermute | solution.py:394
  4.6 19.8 %project.1 = (bf16[3,2048,512]{2,1,0:T(8,128)(2,1)}, bf16[8,4,256,128]{3,2,1,0:T(8,128)(2,1)}, bf16[4,128,128]{2,1,0:T(8,128)(2,1)}, f32[2048,512]{1,0:T(8,128)}) custom-call(bf16[2048,2048]{1,0:T(8,128)(2,1)} %x_hbm.1, bf16[3,2048,512]{2,1,0:T(8,128)(2,1)} %w_hbm.1), custom_call_target="tpu_custom_call" | custom-call | flops 12884901888 | bytes 14680064 | tf_op jit(solution)/shard_map/project/pallas_call | solution.py:139
  24.5 3.3 %collective-permute-done.6.rest_0_ = bf16[512,2048]{1,0:T(8,128)(2,1)S(1)} collective-permute-done((bf16[512,2048]{1,0:T(8,128)(2,1)}, bf16[512,2048]{1,0:T(8,128)(2,1)S(1)}, u32[]{:S(2)}, u32[]{:S(2)}) %collective-permute-start.6) | collective-permute-done | bytes 2097184 | tf_op jit(solution)/shard_map/ppermute | solution.py:394
  29.0 3.0 %collective-permute-start.8 = (bf16[256,2048]{1,0:T(8,128)(2,1)}, bf16[256,2048]{1,0:T(8,128)(2,1)S(1)}, u32[]{:S(2)}, u32[]{:S(2)}) collective-permute-start(bf16[256,2048]{1,0:T(8,128)(2,1)} %constant_dynamic-slice_fusion), channel_id=1, source_target_pairs={{0,1},{1,2},{2,3},{3,0},{4,7},{5,4},{6,5},{7,6},{8,9},{9,10},{10,1... | collective-permute-start | bytes 3145736 | tf_op jit(solution)/shard_map/ppermute | solution.py:394
  34.3 2.1 %collective-permute-done.1 = bf16[2,128,128]{2,1,0:T(8,128)(2,1)S(1)} collective-permute-done((bf16[2,128,128]{2,1,0:T(8,128)(2,1)S(1)}, bf16[2,128,128]{2,1,0:T(8,128)(2,1)S(1)}, u32[]{:S(2)}, u32[]{:S(2)}) %collective-permute-start.1) | collective-permute-done | bytes 65568 | tf_op jit(solution)/shard_map/ppermute | solution.py:363
  36.5 2.8 %collective-permute-start.2 = (bf16[2,128,128]{2,1,0:T(8,128)(2,1)S(1)}, bf16[2,128,128]{2,1,0:T(8,128)(2,1)S(1)}, u32[]{:S(2)}, u32[]{:S(2)}) collective-permute-start(bf16[2,128,128]{2,1,0:T(8,128)(2,1)S(1)} %fusion.3), channel_id=1, source_target_pairs={{0,24},{4,28},{8,16},{12,20},{16,8},{20,12},{24,0},{28,4},{32,56},... | collective-permute-start | bytes 196616 | tf_op jit(solution)/shard_map/ppermute | solution.py:365
  39.3 2.0 %collective-permute-done.2 = bf16[2,128,128]{2,1,0:T(8,128)(2,1)S(1)} collective-permute-done((bf16[2,128,128]{2,1,0:T(8,128)(2,1)S(1)}, bf16[2,128,128]{2,1,0:T(8,128)(2,1)S(1)}, u32[]{:S(2)}, u32[]{:S(2)}) %collective-permute-start.2) | collective-permute-done | bytes 65568 | tf_op jit(solution)/shard_map/ppermute | solution.py:365
  42.6 2.2 %collective-permute-done.3 = bf16[2,128,128]{2,1,0:T(8,128)(2,1)S(1)} collective-permute-done((bf16[2,128,128]{2,1,0:T(8,128)(2,1)S(1)}, bf16[2,128,128]{2,1,0:T(8,128)(2,1)S(1)}, u32[]{:S(2)}, u32[]{:S(2)}) %collective-permute-start.3) | collective-permute-done | bytes 65568 | tf_op jit(solution)/shard_map/ppermute | solution.py:363
  45.4 2.5 %collective-permute-start.4 = (bf16[2,128,128]{2,1,0:T(8,128)(2,1)S(1)}, bf16[2,128,128]{2,1,0:T(8,128)(2,1)}, u32[]{:S(2)}, u32[]{:S(2)}) collective-permute-start(bf16[2,128,128]{2,1,0:T(8,128)(2,1)S(1)} %fusion.5), channel_id=1, source_target_pairs={{0,96},{4,100},{8,104},{12,108},{16,112},{20,116},{24,120},{28,124... | collective-permute-start | bytes 196616 | tf_op jit(solution)/shard_map/ppermute | solution.py:365
  47.9 3.3 %collective-permute-start.9 = (bf16[256,2048]{1,0:T(8,128)(2,1)S(1)}, bf16[256,2048]{1,0:T(8,128)(2,1)}, u32[]{:S(2)}, u32[]{:S(2)}) collective-permute-start(bf16[256,2048]{1,0:T(8,128)(2,1)S(1)} %collective-permute-done.8.rest_2_), channel_id=1, source_target_pairs={{0,4},{4,0},{8,12},{12,8},{16,20},{20,16},{24,28},{28,24},{32,36},... | collective-permute-start | bytes 3145736 | tf_op jit(solution)/shard_map/ppermute | solution.py:391
  52.1 2.9 %collective-permute-start.5 = (f32[2,128,128]{2,1,0:T(8,128)S(1)}, f32[2,128,128]{2,1,0:T(8,128)S(1)}, u32[]{:S(2)}, u32[]{:S(2)}) collective-permute-start(f32[2,128,128]{2,1,0:T(8,128)S(1)} %fusion.2.mine_ref), channel_id=1, source_target_pairs={{0,4},{4,0},{8,12},{12,8},{16,20},{20,16},{24,28},{28,24},{32,36},... | collective-permute-start | bytes 393224 | tf_op jit(solution)/shard_map/ppermute | solution.py:391
  55.0 3.4 %local_part.3.att_in = f32[2048,512]{1,0:T(8,128)} custom-call(bf16[3,2048,512]{2,1,0:T(8,128)(2,1)} %get-tuple-element.16.q_ref.k_ref.v_ref, bf16[3,2048,512]{2,1,0:T(8,128)(2,1)} %get-tuple-element.16.q_ref.k_ref.v_ref, bf16[3,2048,512]{2,1,0:T(8,128)(2,1)} %get-tuple-element.16.q_ref.k_ref.v_ref, ...), custom_call_target="tpu_custom_call", output_to_operand_aliasing={{}: (4, {})} | custom-call | flops 536870912 | bytes 3670016 | tf_op jit(solution)/shard_map/local_part/pallas_call | solution.py:177
  58.4 3.4 %local_part.4.att_in = f32[2048,512]{1,0:T(8,128)} custom-call(bf16[3,2048,512]{2,1,0:T(8,128)(2,1)} %get-tuple-element.16.q_ref.k_ref.v_ref, bf16[3,2048,512]{2,1,0:T(8,128)(2,1)} %get-tuple-element.16.q_ref.k_ref.v_ref, bf16[3,2048,512]{2,1,0:T(8,128)(2,1)} %get-tuple-element.16.q_ref.k_ref.v_ref, ...), custom_call_target="tpu_custom_call", output_to_operand_aliasing={{}: (4, {})} | custom-call | flops 536870912 | bytes 3670016 | tf_op jit(solution)/shard_map/local_part/pallas_call | solution.py:177
  61.8 3.4 %local_part.5.att_ref = f32[2048,512]{1,0:T(8,128)} custom-call(bf16[3,2048,512]{2,1,0:T(8,128)(2,1)} %get-tuple-element.16.q_ref.k_ref.v_ref, bf16[3,2048,512]{2,1,0:T(8,128)(2,1)} %get-tuple-element.16.q_ref.k_ref.v_ref, bf16[3,2048,512]{2,1,0:T(8,128)(2,1)} %get-tuple-element.16.q_ref.k_ref.v_ref, ...), custom_call_target="tpu_custom_call", output_to_operand_aliasing={{}: (4, {})} | custom-call | flops 536870912 | bytes 3670016 | tf_op jit(solution)/shard_map/local_part/pallas_call | solution.py:177
  65.9 2.8 %finish.4 = (bf16[512,512]{1,0:T(8,128)(2,1)}, bf16[4,256,128]{2,1,0:T(8,128)(2,1)}) custom-call(s32[1]{0:T(128)} %bitcast.1.head, s32[1]{0:T(128)} %bitcast.core, bf16[3,2048,512]{2,1,0:T(8,128)(2,1)} %get-tuple-element.16.q_ref.k_ref.v_ref, f32[2048,512]{1,0:T(8,128)} %local_part.5.att_ref, bf16[4,128,128]{2,1,0:T(8,128)(2,1)} %copy-done.3, ...), custom_call_target="tpu_custom_call" | custom-call | flops 134217728 | bytes 2097152 | tf_op jit(solution)/shard_map/finish/pallas_call | solution.py:240
  70.3 2.7 %finish.6 = bf16[512,512]{1,0:T(8,128)(2,1)} custom-call(s32[1]{0:T(128)} %bitcast.1.head, s32[1]{0:T(128)} %bitcast.core, bf16[3,2048,512]{2,1,0:T(8,128)(2,1)} %get-tuple-element.16.q_ref.k_ref.v_ref, f32[2048,512]{1,0:T(8,128)} %local_part.5.att_ref, bf16[4,256,128]{2,1,0:T(8,128)(2,1)} %get-tuple-element.20.pair_ref, f32[1,512]{1,0:T(1,128)} %bitcast.4), custom_call_target="tpu_custom_call" | custom-call | flops 134217728 | bytes 2097152 | tf_op jit(solution)/shard_map/finish/pallas_call | solution.py:240
  73.6 2.7 %finish.7 = bf16[512,512]{1,0:T(8,128)(2,1)} custom-call(s32[1]{0:T(128)} %bitcast.1.head, s32[1]{0:T(128)} %bitcast.core, bf16[3,2048,512]{2,1,0:T(8,128)(2,1)} %get-tuple-element.16.q_ref.k_ref.v_ref, f32[2048,512]{1,0:T(8,128)} %local_part.5.att_ref, bf16[4,256,128]{2,1,0:T(8,128)(2,1)} %get-tuple-element.20.pair_ref, f32[1,512]{1,0:T(1,128)} %bitcast.5), custom_call_target="tpu_custom_call" | custom-call | flops 134217728 | bytes 2097152 | tf_op jit(solution)/shard_map/finish/pallas_call | solution.py:240
  77.4 2.5 %collective-permute-start.13 = (bf16[512,512]{1,0:T(8,128)(2,1)}, bf16[512,512]{1,0:T(8,128)(2,1)}, u32[]{:S(2)}, u32[]{:S(2)}) collective-permute-start(bf16[512,512]{1,0:T(8,128)(2,1)} %collective-permute-done.12), channel_id=1, source_target_pairs={{0,1},{1,2},{2,3},{3,0},{4,7},{5,4},{6,5},{7,6},{8,9},{9,10},{10,1... | collective-permute-start | bytes 1572872 | tf_op jit(solution)/shard_map/ppermute | solution.py:394
  79.9 2.7 %finish.5.n_ref = bf16[512,512]{1,0:T(8,128)(2,1)} custom-call(s32[1]{0:T(128)} %bitcast.1.head, s32[1]{0:T(128)} %bitcast.core, bf16[3,2048,512]{2,1,0:T(8,128)(2,1)} %get-tuple-element.16.q_ref.k_ref.v_ref, f32[2048,512]{1,0:T(8,128)} %local_part.5.att_ref, bf16[4,256,128]{2,1,0:T(8,128)(2,1)} %get-tuple-element.20.pair_ref, f32[1,512]{1,0:T(1,128)} %bitcast.6), custom_call_target="tpu_custom_call" | custom-call | flops 134217728 | bytes 2097152 | tf_op jit(solution)/shard_map/finish/pallas_call | solution.py:240
  82.6 1.6 %copy-done = bf16[512,2048]{1,0:T(8,128)(2,1)S(1)} copy-done((bf16[512,2048]{1,0:T(8,128)(2,1)S(1)}, bf16[512,2048]{1,0:T(8,128)(2,1)}, u32[]{:S(2)}) %copy-start) | copy-done | bytes 2097176
  85.2 2.5 %mix_own.1 = (f32[512,2048]{1,0:T(8,128)S(1)}, bf16[512,2048]{1,0:T(8,128)(2,1)S(1)}, bf16[512,2048]{1,0:T(8,128)(2,1)S(1)}, bf16[256,2048]{1,0:T(8,128)(2,1)S(1)}, bf16[256,2048]{1,0:T(8,128)(2,1)S(1)}) custom-call(bf16[512,512]{1,0:T(8,128)(2,1)S(1)} %copy-done.1, bf16[512,2048]{1,0:T(8,128)(2,1)S(1)} %copy-done, ...), custom_call_target="tpu_custom_call" | custom-call | flops 1073741824 | bytes 8388608 | tf_op jit(solution)/shard_map/mix_own/pallas_call | solution.py:283
  87.8 3.0 %mix_middle.2.acc_ref = f32[512,2048]{1,0:T(8,128)S(1)} custom-call(f32[512,2048]{1,0:T(8,128)S(1)} %get-tuple-element.21.acc_ref, bf16[512,512]{1,0:T(8,128)(2,1)} %collective-permute-done.10.n_ref, bf16[512,2048]{1,0:T(8,128)(2,1)S(1)} %get-tuple-element.22.w_ref), custom_call_target="tpu_custom_call", output_to_operand_aliasing={{}: (0, {})} | custom-call | flops 1073741824 | bytes 8388608 | tf_op jit(solution)/shard_map/mix_middle/pallas_call | solution.py:309
  91.7 3.0 %mix_middle.3.acc_ref = f32[512,2048]{1,0:T(8,128)S(1)} custom-call(f32[512,2048]{1,0:T(8,128)S(1)} %mix_middle.2.acc_ref, bf16[512,512]{1,0:T(8,128)(2,1)} %collective-permute-done.11.n_ref, bf16[512,2048]{1,0:T(8,128)(2,1)S(1)} %get-tuple-element.23.w_ref), custom_call_target="tpu_custom_call", output_to_operand_aliasing={{}: (0, {})} | custom-call | flops 1073741824 | bytes 8388608 | tf_op jit(solution)/shard_map/mix_middle/pallas_call | solution.py:309
  94.7 3.7 %mix_last.1 = bf16[512,2048]{1,0:T(8,128)(2,1)} custom-call(s32[1]{0:T(128)} %bitcast.core, f32[512,2048]{1,0:T(8,128)S(1)} %mix_middle.3.acc_ref, bf16[512,512]{1,0:T(8,128)(2,1)} %collective-permute-done.13.nf, bf16[256,2048]{1,0:T(8,128)(2,1)S(1)} %get-tuple-element.25.mine_ref, bf16[256,2048]{1,0:T(8,128)(2,1)S(1)} %get-tuple-element.26.other_ref), custom_call_target="tpu_custom_call" | custom-call | flops 1073741824 | bytes 8388608 | tf_op jit(solution)/shard_map/mix_last/pallas_call | solution.py:335
  (34 shorter events, 12.3 us)
Async XLA Ops:
  0.0 27.9 %collective-permute-start.6 = (bf16[512,2048]{1,0:T(8,128)(2,1)}, bf16[512,2048]{1,0:T(8,128)(2,1)S(1)}, u32[]{:S(2)}, u32[]{:S(2)}) collective-permute-start(bf16[512,2048]{1,0:T(8,128)(2,1)} %w_ref.1), channel_id=1, source_target_pairs={{0,1},{1,2},{2,3},{3,0},{4,7},{5,4},{6,5},{7,6},{8,9},{9,10},{10,1... | collective-permute-start | bytes 6291464 | tf_op jit(solution)/shard_map/ppermute | solution.py:394
  24.4 7.6 %collective-permute-start = (bf16[4,128,128]{2,1,0:T(8,128)(2,1)}, bf16[4,128,128]{2,1,0:T(8,128)(2,1)S(1)}, u32[]{:S(2)}, u32[]{:S(2)}) collective-permute-start(bf16[4,128,128]{2,1,0:T(8,128)(2,1)} %get-tuple-element.19), channel_id=1, source_target_pairs={{0,4},{4,0},{8,12},{12,8},{16,20},{20,16},{24,28},{28,24},{32,36},... | collective-permute-start | bytes 393224 | tf_op jit(solution)/shard_map/ppermute | solution.py:391
  29.0 18.9 %collective-permute-start.8 = (bf16[256,2048]{1,0:T(8,128)(2,1)}, bf16[256,2048]{1,0:T(8,128)(2,1)S(1)}, u32[]{:S(2)}, u32[]{:S(2)}) collective-permute-start(bf16[256,2048]{1,0:T(8,128)(2,1)} %constant_dynamic-slice_fusion), channel_id=1, source_target_pairs={{0,1},{1,2},{2,3},{3,0},{4,7},{5,4},{6,5},{7,6},{8,9},{9,10},{10,1... | collective-permute-start | bytes 3145736 | tf_op jit(solution)/shard_map/ppermute | solution.py:394
  32.0 50.6 %collective-permute-start.7 = (bf16[512,2048]{1,0:T(8,128)(2,1)S(1)}, bf16[512,2048]{1,0:T(8,128)(2,1)}, u32[]{:S(2)}, u32[]{:S(2)}) collective-permute-start(bf16[512,2048]{1,0:T(8,128)(2,1)S(1)} %collective-permute-done.6.rest_0_), channel_id=1, source_target_pairs={{0,4},{4,0},{8,12},{12,8},{16,20},{20,16},{24,28},{28,24},{32,36},... | collective-permute-start | bytes 6291464 | tf_op jit(solution)/shard_map/ppermute | solution.py:391
  32.0 26.4 %copy-start.3 = (bf16[4,128,128]{2,1,0:T(8,128)(2,1)}, bf16[4,128,128]{2,1,0:T(8,128)(2,1)S(1)}, u32[]{:S(2)}) copy-start(bf16[4,128,128]{2,1,0:T(8,128)(2,1)S(1)} %collective-permute-done.core_ref) | copy-start | bytes 393220
  33.0 3.5 %collective-permute-start.1 = (bf16[2,128,128]{2,1,0:T(8,128)(2,1)S(1)}, bf16[2,128,128]{2,1,0:T(8,128)(2,1)S(1)}, u32[]{:S(2)}, u32[]{:S(2)}) collective-permute-start(bf16[2,128,128]{2,1,0:T(8,128)(2,1)S(1)} %add_convert_fusion), channel_id=1, source_target_pairs={{0,8},{4,12},{8,0},{12,4},{16,24},{20,28},{24,16},{28,20},{32,40},... | collective-permute-start | bytes 196616 | tf_op jit(solution)/shard_map/ppermute | solution.py:363
  36.5 4.8 %collective-permute-start.2 = (bf16[2,128,128]{2,1,0:T(8,128)(2,1)S(1)}, bf16[2,128,128]{2,1,0:T(8,128)(2,1)S(1)}, u32[]{:S(2)}, u32[]{:S(2)}) collective-permute-start(bf16[2,128,128]{2,1,0:T(8,128)(2,1)S(1)} %fusion.3), channel_id=1, source_target_pairs={{0,24},{4,28},{8,16},{12,20},{16,8},{20,12},{24,0},{28,4},{32,56},... | collective-permute-start | bytes 196616 | tf_op jit(solution)/shard_map/ppermute | solution.py:365
  41.3 3.5 %collective-permute-start.3 = (bf16[2,128,128]{2,1,0:T(8,128)(2,1)S(1)}, bf16[2,128,128]{2,1,0:T(8,128)(2,1)S(1)}, u32[]{:S(2)}, u32[]{:S(2)}) collective-permute-start(bf16[2,128,128]{2,1,0:T(8,128)(2,1)S(1)} %fusion.4), channel_id=1, source_target_pairs={{0,32},{4,36},{8,40},{12,44},{16,48},{20,52},{24,56},{28,60},{32,0... | collective-permute-start | bytes 196616 | tf_op jit(solution)/shard_map/ppermute | solution.py:363
  44.8 0.6 copy-start.4
  45.4 5.8 %collective-permute-start.4 = (bf16[2,128,128]{2,1,0:T(8,128)(2,1)S(1)}, bf16[2,128,128]{2,1,0:T(8,128)(2,1)}, u32[]{:S(2)}, u32[]{:S(2)}) collective-permute-start(bf16[2,128,128]{2,1,0:T(8,128)(2,1)S(1)} %fusion.5), channel_id=1, source_target_pairs={{0,96},{4,100},{8,104},{12,108},{16,112},{20,116},{24,120},{28,124... | collective-permute-start | bytes 196616 | tf_op jit(solution)/shard_map/ppermute | solution.py:365
  47.9 34.7 %collective-permute-start.9 = (bf16[256,2048]{1,0:T(8,128)(2,1)S(1)}, bf16[256,2048]{1,0:T(8,128)(2,1)}, u32[]{:S(2)}, u32[]{:S(2)}) collective-permute-start(bf16[256,2048]{1,0:T(8,128)(2,1)S(1)} %collective-permute-done.8.rest_2_), channel_id=1, source_target_pairs={{0,4},{4,0},{8,12},{12,8},{16,20},{20,16},{24,28},{28,24},{32,36},... | collective-permute-start | bytes 3145736 | tf_op jit(solution)/shard_map/ppermute | solution.py:391
  52.1 6.3 %copy-start.2 = (f32[2,128,128]{2,1,0:T(8,128)}, f32[2,128,128]{2,1,0:T(8,128)S(1)}, u32[]{:S(2)}) copy-start(f32[2,128,128]{2,1,0:T(8,128)S(1)} %fusion.2.mine_ref) | copy-start | bytes 393220
  52.1 13.2 %collective-permute-start.5 = (f32[2,128,128]{2,1,0:T(8,128)S(1)}, f32[2,128,128]{2,1,0:T(8,128)S(1)}, u32[]{:S(2)}, u32[]{:S(2)}) collective-permute-start(f32[2,128,128]{2,1,0:T(8,128)S(1)} %fusion.2.mine_ref), channel_id=1, source_target_pairs={{0,4},{4,0},{8,12},{12,8},{16,20},{20,16},{24,28},{28,24},{32,36},... | collective-permute-start | bytes 393224 | tf_op jit(solution)/shard_map/ppermute | solution.py:391
  65.3 0.7 copy-start.5
  68.8 8.6 %collective-permute-start.12 = (bf16[512,512]{1,0:T(8,128)(2,1)}, bf16[512,512]{1,0:T(8,128)(2,1)}, u32[]{:S(2)}, u32[]{:S(2)}) collective-permute-start(bf16[512,512]{1,0:T(8,128)(2,1)} %get-tuple-element.24), channel_id=1, source_target_pairs={{0,1},{1,2},{2,3},{3,0},{4,7},{5,4},{6,5},{7,6},{8,9},{9,10},{10,1... | collective-permute-start | bytes 1572872 | tf_op jit(solution)/shard_map/ppermute | solution.py:394
  73.0 14.7 %collective-permute-start.10 = (bf16[512,512]{1,0:T(8,128)(2,1)}, bf16[512,512]{1,0:T(8,128)(2,1)}, u32[]{:S(2)}, u32[]{:S(2)}) collective-permute-start(bf16[512,512]{1,0:T(8,128)(2,1)} %finish.6), channel_id=1, source_target_pairs={{0,1},{1,2},{2,3},{3,0},{4,7},{5,4},{6,5},{7,6},{8,9},{9,10},{10,1... | collective-permute-start | bytes 1572872 | tf_op jit(solution)/shard_map/ppermute | solution.py:394
  76.3 15.5 %collective-permute-start.11 = (bf16[512,512]{1,0:T(8,128)(2,1)}, bf16[512,512]{1,0:T(8,128)(2,1)}, u32[]{:S(2)}, u32[]{:S(2)}) collective-permute-start(bf16[512,512]{1,0:T(8,128)(2,1)} %finish.7), channel_id=1, source_target_pairs={{0,3},{1,0},{2,1},{3,2},{4,5},{5,6},{6,7},{7,4},{8,11},{9,8},{10,9... | collective-permute-start | bytes 1572872 | tf_op jit(solution)/shard_map/ppermute | solution.py:394
  77.4 17.3 %collective-permute-start.13 = (bf16[512,512]{1,0:T(8,128)(2,1)}, bf16[512,512]{1,0:T(8,128)(2,1)}, u32[]{:S(2)}, u32[]{:S(2)}) collective-permute-start(bf16[512,512]{1,0:T(8,128)(2,1)} %collective-permute-done.12), channel_id=1, source_target_pairs={{0,1},{1,2},{2,3},{3,0},{4,7},{5,4},{6,5},{7,6},{8,9},{9,10},{10,1... | collective-permute-start | bytes 1572872 | tf_op jit(solution)/shard_map/ppermute | solution.py:394
  82.6 1.6 %copy-start = (bf16[512,2048]{1,0:T(8,128)(2,1)S(1)}, bf16[512,2048]{1,0:T(8,128)(2,1)}, u32[]{:S(2)}) copy-start(bf16[512,2048]{1,0:T(8,128)(2,1)} %w_ref.1) | copy-start | bytes 6291460
  84.2 1.0 %copy-start.1 = (bf16[512,512]{1,0:T(8,128)(2,1)S(1)}, bf16[512,512]{1,0:T(8,128)(2,1)}, u32[]{:S(2)}) copy-start(bf16[512,512]{1,0:T(8,128)(2,1)} %finish.5.n_ref) | copy-start | bytes 1572868
